TPU v7x, 32 devices: a whole 2x2x4 slice. The times are simulated.
32 devices in a mesh: sec: 4 (over y, x), term: 8 (over z, core).
Axes of the slice: x: 2, y: 2, z: 4, core: 2. Of those that a mesh axis runs over, the one named last changes fastest.
Arguments:
- theta: bfloat16 [4, 896, 896], P('sec', 'term'), may hold values from -6 to 6
- left_env: bfloat16 [16, 4, 896, 896], P('term', 'sec'), may hold values from -2 to 2
- right_env: bfloat16 [16, 4, 896, 896], P('term', 'sec'), may hold values from -2 to 2
- term_shift: int32 [16], P('term'), may hold values from -1 to 1
- term_on: int32 [16, 4], P('term', 'sec'), may hold values 0 or 1
- block_rows: int32 [4], P('sec'), may hold values from 224 to 896
- block_cols: int32 [4], P('sec'), may hold values from 224 to 896
Outputs:
- basis_last: float32 [4, 896, 896], P('sec', 'term')
- alphas: float32 [2], replicated
- betas: float32 [2], replicated
All inputs are finite; a program needn't handle non-finite values. No bound on the sum of `term_on` on one device may be relied on, other than what follows from the above.
Results may differ from a plain program's by a relative error of at most 0.0037.
Values may be sent and summed in bfloat16 or wider, within the bound.
No kernel may reach another device: no remote copies, remote signals or barrier semaphores. Data moves between devices by JAX's collectives and lax.ppermute only.
A program may use at most 64 MiB of HBM per device.

v0:
```python
import jax
import jax.numpy as jnp
from jax import lax
from jax.sharding import PartitionSpec as P

ITERS = 2


EPS = 1e-06


def extended(block, sides, width):
    for axis, dim in sides:
        count = lax.axis_size(axis)
        forward = [(i, i + 1) for i in range(count - 1)]
        backward = [(target, source) for source, target in forward]
        low = lax.ppermute(
            lax.slice_in_dim(block, block.shape[dim] - width, None, axis=dim), axis, forward
        )
        high = lax.ppermute(lax.slice_in_dim(block, 0, width, axis=dim), axis, backward)
        block = jnp.concatenate([low, block, high], axis=dim)
    return block


def on_device(theta, left_env, right_env, term_shift, term_on, block_rows, block_cols):
    sectors = theta.shape[0]
    row_count = theta.shape[1]
    width = theta.shape[2]
    terms_here = left_env.shape[0]
    full_count = row_count * lax.axis_size("term")
    row_offset = lax.axis_index("term") * row_count
    col_line = jnp.arange(width, dtype=jnp.int32)
    col_mask = (col_line[None, :] < block_cols[:, None]).astype(jnp.float32)
    local_rows = row_offset + jnp.arange(row_count, dtype=jnp.int32)
    row_mask = (local_rows[None, :] < block_rows[:, None]).astype(jnp.float32)
    mask = row_mask[:, :, None] * col_mask[:, None, :]
    on_float = term_on.astype(jnp.float32)
    start = mask * theta.astype(jnp.float32)
    norm_start = lax.psum(jnp.sum(start * start), ("sec", "term"))
    vector = start / jnp.sqrt(norm_start + EPS)
    previous = jnp.zeros_like(vector)
    beta_prev = jnp.float32(0.0)
    alpha_list = []
    beta_list = []
    for step in range(ITERS):
        vector_bf = vector.astype(jnp.bfloat16)
        full_rows = lax.all_gather(vector_bf, "term", axis=1, tiled=True)
        padded = extended(full_rows, (("sec", 0),), 1)
        source_list = [
            lax.dynamic_slice_in_dim(padded, 1 + term_shift[term_index], sectors, 0)
            for term_index in range(terms_here)
        ]
        total = jnp.zeros((full_count, sectors, width), jnp.float32)
        for partial_term_index in range(terms_here):
            left_rows = left_env[partial_term_index]
            product = jnp.einsum(
                "sik,skj->sij",
                left_rows,
                source_list[partial_term_index],
                preferred_element_type=jnp.float32,
            ).astype(jnp.bfloat16)
            result = jnp.einsum(
                "sij,sjk->isk",
                product,
                right_env[partial_term_index],
                preferred_element_type=jnp.float32,
            )
            total = total + on_float[partial_term_index][None, :, None] * result
        row_index = jnp.arange(full_count, dtype=jnp.int32)
        rows_inside = (row_index[:, None] < block_rows[None, :]).astype(jnp.float32)
        total = total * rows_inside[:, :, None] * col_mask[None, :, :]
        summed = lax.psum(total.reshape(full_count, sectors * width), "term")
        scattered = lax.dynamic_slice_in_dim(summed, row_offset, row_count, 0)
        image = scattered.reshape(row_count, sectors, width).transpose(1, 0, 2)
        alpha = lax.psum(jnp.sum(vector * image), ("sec", "term"))
        residual = image - alpha * vector - beta_prev * previous
        beta_square = lax.psum(jnp.sum(residual * residual), ("sec", "term"))
        beta = jnp.sqrt(beta_square + EPS)
        previous = vector
        vector = residual / beta
        beta_prev = beta
        alpha_list.append(alpha)
        beta_list.append(beta)
    return (vector, jnp.stack(alpha_list), jnp.stack(beta_list))


def solution(mesh):
    return jax.shard_map(
        on_device,
        mesh=mesh,
        in_specs=(
            P("sec", "term", None),
            P("term", "sec", None, None),
            P("term", "sec", None, None),
            P("term"),
            P("term", "sec"),
            P("sec"),
            P("sec"),
        ),
        out_specs=(P("sec", "term", None), P(), P()),
        check_vma=False,
    )
```

profile of v0, /device:TPU:0, one launch (start us, length us, event | category | flops | bytes accessed | tf_op | source)
XLA Modules:
  0.0 632.7 jit_solution(16715820950023222964)
XLA Ops:
  7.2 0.0 all-gather.3.cloned.1.call-start
  8.5 1.7 multiply_reduce_fusion.2
  10.2 42.2 %psum.49 = f32[]{:T(128)} all-reduce(f32[]{:T(128)} %multiply_reduce_fusion.2), channel_id=1, replica_groups=mesh['sec'=4,'term'=8] {'sec','term'}, use_global_device_ids=true, to_apply=%region_1.0 | all-reduce | flops 1 | bytes 8 | tf_op jit(solution)/shard_map/psum | solution.py:39
  53.1 1.7 fusion.61
  54.9 0.0 all-gather.3.cloned.1.call-update
  54.9 0.0 all-reduce.3.cloned.1.call-start
  55.0 25.3 %all-gather.3.cloned.1.call-done = bf16[1,896,896]{2,1,0:T(8,128)(2,1)} async-done(((bf16[1,112,896]{2,1,0:T(8,128)(2,1)}), bf16[1,896,896]{2,1,0:T(8,128)(2,1)}) %all-gather.3.cloned.1.call-update) | async-done | bytes 1605648 | tf_op jit(solution)/shard_map/all_gather | solution.py:47
  80.3 4.7 collective-permute-start
  85.0 1.3 collective-permute-start.1
  86.2 1.3 fusion.63
  90.2 0.7 convert_element_type.60
  90.8 0.6 fusion.64
  91.4 27.4 %collective-permute-done = bf16[1,896,896]{2,1,0:T(8,128)(2,1)} collective-permute-done((bf16[1,896,896]{2,1,0:T(8,128)(2,1)}, bf16[1,896,896]{2,1,0:T(8,128)(2,1)}, u32[]{:S(2)}, u32[]{:S(2)}) %collective-permute-start) | collective-permute-done | bytes 1605664 | tf_op jit(solution)/shard_map/ppermute | solution.py:17
  118.8 2.7 constant_dynamic-update-slice_fusion.2
  121.6 1.3 constant_dynamic-update-slice_fusion.1
  122.9 32.2 %collective-permute-done.1 = bf16[1,896,896]{2,1,0:T(8,128)(2,1)S(1)} collective-permute-done((bf16[1,896,896]{2,1,0:T(8,128)(2,1)}, bf16[1,896,896]{2,1,0:T(8,128)(2,1)S(1)}, u32[]{:S(2)}, u32[]{:S(2)}) %collective-permute-start.1) | collective-permute-done | bytes 1605664 | tf_op jit(solution)/shard_map/ppermute | solution.py:20
  155.1 1.3 constant_dynamic-update-slice_fusion
  156.4 8.2 %fusion.13 = f32[896,896]{1,0:T(8,128)} fusion(bf16[2,1,896,896]{3,2,1,0:T(8,128)(2,1)} %param.9, bf16[3,896,896]{2,1,0:T(8,128)(2,1)} %constant_dynamic-update-slice_fusion, s32[]{:T(128)S(6)} %select_n.12, bf16[2,1,896,896]{3,2,1,0:T(8,128)(2,1)} %param.8), kind=kOutput, calls=%fused_computation.19 | convolution fusion | flops 2878095360 | bytes 8028164 | tf_op jit(solution)/shard_map/sij,sjk->isk/dot_general | solution.py:62
  164.6 10.1 %fusion.3 = f32[896,896]{1,0:T(8,128)} fusion(f32[896,896]{1,0:T(8,128)} %fusion.13, f32[896]{0:T(1024)S(1)} %fusion.50, f32[896]{0:T(1024)S(1)} %fusion.51, f32[]{:T(128)} %bitcast.8, f32[]{:T(128)} %bitcast, bf16[2,1,896,896]{3,2,1,0:T(8,128)(2,1)S(1)} %copy-done.3, bf16[3,896,896]{2,1,0:T(8,128)(2,1)} %constant_dynamic-update-slice_fusion, ...), kind=kOutput, calls=%fused_computation.5 | convolution fusion | flops 2882109440 | bytes 11248644 | tf_op jit(solution)/shard_map/sij,sjk->isk/dot_general | solution.py:62
  174.7 0.0 all-reduce.3.cloned.1.call-update
  174.7 0.0 all-gather.5.cloned.1.call-start
  174.8 76.8 %all-reduce.3.cloned.1.call-done = f32[896,896]{1,0:T(8,128)} async-done(((f32[896,896]{1,0:T(8,128)}), f32[896,896]{1,0:T(8,128)}) %all-reduce.3.cloned.1.call-update) | async-done | bytes 3211280 | tf_op jit(solution)/shard_map/psum | solution.py:72
  251.5 1.8 fusion.48
  253.3 40.4 %psum.51 = f32[]{:T(128)} all-reduce(f32[]{:T(128)} %fusion.48), channel_id=1, replica_groups=mesh['sec'=4,'term'=8] {'sec','term'}, use_global_device_ids=true, to_apply=%region_4.0 | all-reduce | flops 1 | bytes 8 | tf_op jit(solution)/shard_map/psum | solution.py:75
  293.7 2.4 multiply_reduce_fusion.1
  296.1 39.6 %psum.52 = f32[]{:T(128)} all-reduce(f32[]{:T(128)} %multiply_reduce_fusion.1), channel_id=1, replica_groups=mesh['sec'=4,'term'=8] {'sec','term'}, use_global_device_ids=true, to_apply=%region_6.0 | all-reduce | flops 1 | bytes 8 | tf_op jit(solution)/shard_map/psum | solution.py:77
  336.4 2.5 fusion.60
  338.8 0.0 all-gather.5.cloned.1.call-update
  338.9 0.2 all-reduce.5.cloned.1.call-start
  339.1 26.1 %all-gather.5.cloned.1.call-done = bf16[1,896,896]{2,1,0:T(8,128)(2,1)} async-done(((bf16[1,112,896]{2,1,0:T(8,128)(2,1)}), bf16[1,896,896]{2,1,0:T(8,128)(2,1)}) %all-gather.5.cloned.1.call-update) | async-done | bytes 1605648 | tf_op jit(solution)/shard_map/all_gather | solution.py:47
  365.2 3.6 collective-permute-start.2
  368.8 1.3 collective-permute-start.3
  370.1 33.6 %collective-permute-done.2 = bf16[1,896,896]{2,1,0:T(8,128)(2,1)S(1)} collective-permute-done((bf16[1,896,896]{2,1,0:T(8,128)(2,1)}, bf16[1,896,896]{2,1,0:T(8,128)(2,1)S(1)}, u32[]{:S(2)}, u32[]{:S(2)}) %collective-permute-start.2) | collective-permute-done | bytes 1605664 | tf_op jit(solution)/shard_map/ppermute | solution.py:17
  403.7 1.3 constant_dynamic-update-slice_fusion.5
  405.0 1.3 constant_dynamic-update-slice_fusion.4
  406.3 33.6 %collective-permute-done.3 = bf16[1,896,896]{2,1,0:T(8,128)(2,1)S(1)} collective-permute-done((bf16[1,896,896]{2,1,0:T(8,128)(2,1)}, bf16[1,896,896]{2,1,0:T(8,128)(2,1)S(1)}, u32[]{:S(2)}, u32[]{:S(2)}) %collective-permute-start.3) | collective-permute-done | bytes 1605664 | tf_op jit(solution)/shard_map/ppermute | solution.py:20
  439.9 1.3 constant_dynamic-update-slice_fusion.3
  441.2 8.1 %fusion.11 = f32[896,896]{1,0:T(8,128)} fusion(bf16[2,1,896,896]{3,2,1,0:T(8,128)(2,1)} %param.9, bf16[3,896,896]{2,1,0:T(8,128)(2,1)} %constant_dynamic-update-slice_fusion.3, s32[]{:T(128)S(6)} %select_n.12, bf16[2,1,896,896]{3,2,1,0:T(8,128)(2,1)} %param.8), kind=kOutput, calls=%fused_computation.17 | convolution fusion | flops 2878095360 | bytes 8028164 | tf_op jit(solution)/shard_map/sij,sjk->isk/dot_general | solution.py:62
  449.3 10.6 %fusion.1 = f32[896,896]{1,0:T(8,128)} fusion(f32[896,896]{1,0:T(8,128)} %fusion.11, f32[896]{0:T(1024)S(1)} %fusion.50, f32[896]{0:T(1024)S(1)} %fusion.51, f32[]{:T(128)} %bitcast.8, f32[]{:T(128)} %bitcast, bf16[2,1,896,896]{3,2,1,0:T(8,128)(2,1)} %param.9, bf16[3,896,896]{2,1,0:T(8,128)(2,1)} %constant_dynamic-update-slice_fusion.3, s32[]{:T(128)S(6)} %select_n.13, ...), kind=kOutput, calls=%fused_computation.2 | convolution fusion | flops 2882109440 | bytes 11247620 | tf_op jit(solution)/shard_map/sij,sjk->isk/dot_general | solution.py:62
  459.9 0.0 all-reduce.5.cloned.1.call-update
  459.9 76.8 %all-reduce.5.cloned.1.call-done = f32[896,896]{1,0:T(8,128)} async-done(((f32[896,896]{1,0:T(8,128)}), f32[896,896]{1,0:T(8,128)}) %all-reduce.5.cloned.1.call-update) | async-done | bytes 3211280 | tf_op jit(solution)/shard_map/psum | solution.py:72
  536.7 2.5 fusion.46
  539.2 40.4 %psum.54 = f32[]{:T(128)} all-reduce(f32[]{:T(128)} %fusion.46), channel_id=1, replica_groups=mesh['sec'=4,'term'=8] {'sec','term'}, use_global_device_ids=true, to_apply=%region_9.0 | all-reduce | flops 1 | bytes 8 | tf_op jit(solution)/shard_map/psum | solution.py:75
  579.6 3.2 multiply_reduce_fusion
  582.8 39.5 %psum.55 = f32[]{:T(128)} all-reduce(f32[]{:T(128)} %get-tuple-element.3), channel_id=1, replica_groups=mesh['sec'=4,'term'=8] {'sec','term'}, use_global_device_ids=true, to_apply=%region_11.0 | all-reduce | flops 1 | bytes 8 | tf_op jit(solution)/shard_map/psum | solution.py:77
  623.0 0.8 broadcast_divide_fusion
  623.8 0.6 pad_maximum_fusion.1
  624.4 1.7 pad_maximum_fusion
  (11 shorter events, 0.0 us)
Async XLA Ops:
  7.2 73.1 %all-gather.3.cloned.1.call-start = ((), (), s32[]{:S(2)}) async-start(), calls=%async_computation | async-start | bytes 1806336 | tf_op jit(solution)/shard_map/all_gather | solution.py:47
  54.9 196.6 %all-reduce.3.cloned.1.call-start = ((), (), s32[]{:S(2)}) async-start(), calls=%async_computation.1 | async-start | bytes 6422528 | tf_op jit(solution)/shard_map/psum | solution.py:72
  80.3 41.3 %copy-start.1 = (bf16[1,896,896]{2,1,0:T(8,128)(2,1)S(1)}, bf16[1,896,896]{2,1,0:T(8,128)(2,1)}, u32[]{:S(2)}) copy-start(bf16[1,896,896]{2,1,0:T(8,128)(2,1)} %all-gather.3.cloned.1.call-done) | copy-start | bytes 4816900
  80.3 38.6 %collective-permute-start = (bf16[1,896,896]{2,1,0:T(8,128)(2,1)}, bf16[1,896,896]{2,1,0:T(8,128)(2,1)}, u32[]{:S(2)}, u32[]{:S(2)}) collective-permute-start(bf16[1,896,896]{2,1,0:T(8,128)(2,1)} %all-gather.3.cloned.1.call-done), channel_id=1, source_target_pairs={{0,8},{8,16},{16,24},{1,9},{9,17},{17,25},{2,10},{10,18},{18,26},{... | collective-permute-start | bytes 4816904 | tf_op jit(solution)/shard_map/ppermute | solution.py:17
  85.0 70.1 %collective-permute-start.1 = (bf16[1,896,896]{2,1,0:T(8,128)(2,1)}, bf16[1,896,896]{2,1,0:T(8,128)(2,1)S(1)}, u32[]{:S(2)}, u32[]{:S(2)}) collective-permute-start(bf16[1,896,896]{2,1,0:T(8,128)(2,1)} %all-gather.3.cloned.1.call-done), channel_id=1, source_target_pairs={{8,0},{16,8},{24,16},{9,1},{17,9},{25,17},{10,2},{18,10},{26,18},{... | collective-permute-start | bytes 4816904 | tf_op jit(solution)/shard_map/ppermute | solution.py:20
  156.4 8.2 %copy-start.3 = (bf16[2,1,896,896]{3,2,1,0:T(8,128)(2,1)S(1)}, bf16[2,1,896,896]{3,2,1,0:T(8,128)(2,1)}, u32[]{:S(2)}) copy-start(bf16[2,1,896,896]{3,2,1,0:T(8,128)(2,1)} %param.9) | copy-start | bytes 9633796
  174.7 76.8 %copy-start = (bf16[1,112,896]{2,1,0:T(8,128)(2,1)S(1)}, bf16[1,112,896]{2,1,0:T(8,128)(2,1)}, u32[]{:S(2)}) copy-start(bf16[1,112,896]{2,1,0:T(8,128)(2,1)} %param.7) | copy-start | bytes 602116
  174.7 190.4 %all-gather.5.cloned.1.call-start = ((), (), s32[]{:S(2)}) async-start(), calls=%async_computation.2 | async-start | bytes 1806336 | tf_op jit(solution)/shard_map/all_gather | solution.py:47
  338.9 197.9 %all-reduce.5.cloned.1.call-start = ((), (), s32[]{:S(2)}) async-start(), calls=%async_computation.3 | async-start | bytes 6422528 | tf_op jit(solution)/shard_map/psum | solution.py:72
  365.2 39.9 %copy-start.2 = (bf16[1,896,896]{2,1,0:T(8,128)(2,1)S(1)}, bf16[1,896,896]{2,1,0:T(8,128)(2,1)}, u32[]{:S(2)}) copy-start(bf16[1,896,896]{2,1,0:T(8,128)(2,1)} %all-gather.5.cloned.1.call-done) | copy-start | bytes 4816900
  365.2 38.5 %collective-permute-start.2 = (bf16[1,896,896]{2,1,0:T(8,128)(2,1)}, bf16[1,896,896]{2,1,0:T(8,128)(2,1)S(1)}, u32[]{:S(2)}, u32[]{:S(2)}) collective-permute-start(bf16[1,896,896]{2,1,0:T(8,128)(2,1)} %all-gather.5.cloned.1.call-done), channel_id=1, source_target_pairs={{0,8},{8,16},{16,24},{1,9},{9,17},{17,25},{2,10},{10,18},{18,26},{... | collective-permute-start | bytes 4816904 | tf_op jit(solution)/shard_map/ppermute | solution.py:17
  368.8 71.2 %collective-permute-start.3 = (bf16[1,896,896]{2,1,0:T(8,128)(2,1)}, bf16[1,896,896]{2,1,0:T(8,128)(2,1)S(1)}, u32[]{:S(2)}, u32[]{:S(2)}) collective-permute-start(bf16[1,896,896]{2,1,0:T(8,128)(2,1)} %all-gather.5.cloned.1.call-done), channel_id=1, source_target_pairs={{8,0},{16,8},{24,16},{9,1},{17,9},{25,17},{10,2},{18,10},{26,18},{... | collective-permute-start | bytes 4816904 | tf_op jit(solution)/shard_map/ppermute | solution.py:20
Sparse Core Ops, SparseCore 0:
  55.0 25.2 all-gather.2
  174.8 76.6 all-reduce.2
  339.0 26.1 all-gather.4
  460.0 76.6 all-reduce.4
where the time goes:
time: 634 us; the launch traced here: 633 us
  waiting for transfers between devices  332 us (52%)
  blocking collectives  202 us (32%)
  matrix products  36.9 us (6%)
  between operations  19.8 us (3%)
  other arithmetic  19.6 us (3%)
  starting transfers between devices  11.2 us (2%)
  local copies, waits for them, and re-layouts  11.1 us (2%)
    psum x2, waiting for transfers between devices, on_device(): summed = lax.psum(total.reshape(full_count, sectors * width), 'term')  154 us
    psum x2, blocking collectives, on_device(): alpha = lax.psum(jnp.sum(vector * image), ('sec', 'term'))  80.8 us
    psum x2, blocking collectives, on_device(): beta_square = lax.psum(jnp.sum(residual * residual), ('sec', 'term'))  79.1 us
    ppermute x2, waiting for transfers between devices, extended(): lax.ppermute(lax.slice_in_dim(block, 0, width, axis=dim), axis, backward)  65.8 us
    ppermute x2, waiting for transfers between devices, extended(): lax.ppermute(lax.slice_in_dim(block, block.shape[dim] - width, None, axis...  61.1 us
    all_gather x2, waiting for transfers between devices, on_device(): full_rows = lax.all_gather(vector_bf, 'term', axis=1, tiled=True)  51.4 us
    psum x1, blocking collectives, on_device(): norm_start = lax.psum(jnp.sum(start * start), ('sec', 'term'))  42.2 us
    dot_general x4, matrix products, on_device(): jnp.einsum('sij,sjk->isk', product, right_env[partial_term_index], prefer...  36.9 us
  transfers between devices with their start and end apart: 8, of which 8 were waited for; matrix products, arithmetic and copies ran while one was open for 1% of the time, Pallas kernels for 0%

commit v1 on v0

v1 whole, which is shorter than its diff:
```python
import functools

import jax
import jax.numpy as jnp
from jax import lax
from jax.experimental import pallas as pl
from jax.experimental.pallas import tpu as pltpu
from jax.sharding import PartitionSpec as P

ITERS = 2


EPS = 1e-06

SCALE = 2.0**-10


def along_term(x, partner, count):
    return lax.ppermute(x, "term", [(i, partner(i)) for i in range(count)])


def pair_exchange(x, count):
    return lax.ppermute(x, "sec", [(i, i ^ 1) for i in range(count) if (i ^ 1) < count])


def pair_forward(x, count):
    pairs = [(i, i + 2) for i in range(0, count, 2) if i + 2 < count]
    pairs += [(i, i - 2) for i in range(1, count, 2) if i >= 2]
    return lax.ppermute(x, "sec", pairs)


def gather_pieces(shard, sec_count, term_count):
    chips = term_count // 2
    own = {0: shard}
    order = sorted(range(1, chips), key=lambda i: (bin(i).count("1"), i))
    for i in order:
        bit = i & -i
        own[i] = along_term(own[i ^ bit], lambda t, b=bit: t ^ (2 * b), term_count)
    pair = {i: pair_exchange(own[i], sec_count) for i in range(chips)}
    beyond = {i: pair_forward(pair[i], sec_count) for i in range(chips)}
    pieces = []
    for table in (own, pair, beyond):
        for i in range(chips):
            pieces.append(table[i])
            pieces.append(along_term(table[i], lambda t: t ^ 1, term_count))
    return pieces


def apply_kernel(chips, terms, rows, scal, left, right, *refs):
    pieces = refs[: 6 * chips]
    mine, theirs, x_s, l_s, r_s, a_s, x_sem, l_sem, r_sem = refs[6 * chips :]
    width = x_s.shape[2]
    z, c = scal[2 * terms], scal[2 * terms + 1]
    block_rows, block_cols = scal[2 * terms + 2], scal[2 * terms + 3]

    def offset(i, other):
        t = jnp.bitwise_xor(z, i) * 2 + jnp.bitwise_xor(c, other)
        return pl.multiple_of(t * rows, rows)

    def piece_copy(w, source, i, other):
        return pltpu.make_async_copy(
            pieces[source * 2 * chips + 2 * i + other].at[0],
            x_s.at[w, pl.ds(offset(i, other), rows)],
            x_sem.at[w],
        )

    def l_copy(w):
        return pltpu.make_async_copy(left.at[w, 0], l_s.at[w], l_sem.at[w])

    def r_copy(w):
        return pltpu.make_async_copy(right.at[w, 0], r_s.at[pl.ds(w * width, width)], r_sem.at[w])

    for w in range(terms):
        l_copy(w).start()
        for source in range(3):

            @pl.when(scal[w] == source)
            def _():
                for i in range(chips):
                    for other in range(2):
                        piece_copy(w, source, i, other).start()

    for w in range(terms):
        r_copy(w).start()

    for w in range(terms):
        l_copy(w).wait()
        for i in range(chips):
            for other in range(2):
                piece_copy(w, 0, i, other).wait()
        on = scal[terms + w].astype(jnp.float32)
        for i in range(chips):
            band = slice(i * 2 * rows, (i + 1) * 2 * rows)
            product = jnp.dot(l_s[w, band, :], x_s[w], preferred_element_type=jnp.float32)
            a_s[band, w * width : (w + 1) * width] = (product * on).astype(jnp.bfloat16)
    for w in range(terms):
        r_copy(w).wait()
    col = lax.broadcasted_iota(jnp.int32, (2 * rows, width), 1)
    row = lax.broadcasted_iota(jnp.int32, (2 * rows, width), 0)
    for i in range(chips):
        start = pl.multiple_of(jnp.bitwise_xor(z, i) * 2 * rows, 2 * rows)
        total = jnp.dot(a_s[pl.ds(start, 2 * rows), :], r_s[...], preferred_element_type=jnp.float32)
        inside = (row + start < block_rows) & (col < block_cols)
        total = jnp.where(inside, total, 0.0)
        first = c == 0
        mine[i] = jnp.where(first, total[:rows], total[rows:])
        theirs[i] = jnp.where(first, total[rows:], total[:rows]).astype(jnp.bfloat16)


def apply_terms(scal, left_env, right_env, pieces, chips, rows):
    terms, _, width, _ = left_env.shape
    return pl.pallas_call(
        functools.partial(apply_kernel, chips, terms, rows),
        out_shape=(
            jax.ShapeDtypeStruct((chips, rows, width), jnp.float32),
            jax.ShapeDtypeStruct((chips, rows, width), jnp.bfloat16),
        ),
        in_specs=[pl.BlockSpec(memory_space=pltpu.SMEM)]
        + [pl.BlockSpec(memory_space=pl.ANY)] * (2 + len(pieces)),
        out_specs=(pl.BlockSpec(memory_space=pltpu.VMEM),) * 2,
        scratch_shapes=[
            pltpu.VMEM((terms, width, width), jnp.bfloat16),
            pltpu.VMEM((terms, width, width), jnp.bfloat16),
            pltpu.VMEM((terms * width, width), jnp.bfloat16),
            pltpu.VMEM((width, terms * width), jnp.bfloat16),
            pltpu.SemaphoreType.DMA((terms,)),
            pltpu.SemaphoreType.DMA((terms,)),
            pltpu.SemaphoreType.DMA((terms,)),
        ],
        compiler_params=pltpu.CompilerParams(vmem_limit_bytes=40 * 2**20),
        name="apply_terms",
    )(scal, left_env, right_env, *pieces)


def reduce_rows(mine, theirs, term_count):
    got = along_term(theirs, lambda t: t ^ 1, term_count)
    chips = term_count // 2
    total = mine[0] + got[0].astype(jnp.float32)
    for i in range(1, chips):
        part = (mine[i] + got[i].astype(jnp.float32)).astype(jnp.bfloat16)
        part = along_term(part, lambda t, b=i: t ^ (2 * b), term_count)
        total = total + part.astype(jnp.float32)
    return total


def sum_all(values, sec_count, term_count):
    tile = jnp.broadcast_to(jnp.stack(values)[:, None], (len(values), 128))
    tile = jnp.pad(tile, ((0, 8 - len(values)), (0, 0)))
    bit = 1
    while bit < term_count:
        tile = tile + along_term(tile, lambda t, b=bit: t ^ b, term_count)
        bit *= 2
    bit = 1
    while bit < sec_count:
        tile = tile + lax.ppermute(tile, "sec", [(i, i ^ bit) for i in range(sec_count)])
        bit *= 2
    return [tile[i, 0] for i in range(len(values))]


def on_device(theta, left_env, right_env, term_shift, term_on, block_rows, block_cols):
    rows, width = theta.shape[1:]
    sec_count, term_count = lax.axis_size("sec"), lax.axis_size("term")
    sec, term = lax.axis_index("sec"), lax.axis_index("term")
    chips = term_count // 2
    row = term * rows + lax.broadcasted_iota(jnp.int32, (1, rows, width), 1)
    col = lax.broadcasted_iota(jnp.int32, (1, rows, width), 2)
    start = jnp.where((row < block_rows[0]) & (col < block_cols[0]), theta, jnp.zeros_like(theta))
    toward_pair = 1 - 2 * (sec % 2)
    source = jnp.where(term_shift == 0, 0, jnp.where(term_shift == toward_pair, 1, 2))
    scal = jnp.concatenate(
        [source, term_on[:, 0], jnp.stack([term // 2, term % 2]), block_rows, block_cols]
    ).astype(jnp.int32)

    def apply(shard):
        pieces = gather_pieces(shard, sec_count, term_count)
        mine, theirs = apply_terms(scal, left_env, right_env, pieces, chips, rows)
        return reduce_rows(mine, theirs, term_count)

    x = start[0].astype(jnp.float32)
    y = apply(start) * SCALE
    h = apply(y.astype(jnp.bfloat16)[None])
    pairs = ((x, x), (x, y), (y, y), (x, h), (y, h), (h, h))
    xx, xy, yy, xh, yh, hh = sum_all([jnp.sum(a * b) for a, b in pairs], sec_count, term_count)
    cx = 1.0 / jnp.sqrt(xx + EPS)
    cy = cx / SCALE
    vv, vi, ii = xx * cx * cx, xy * cx * cy, yy * cy * cy
    vh, ih, hh = xh * cx * cy, yh * cy * cy, hh * cy * cy
    alpha0 = vi
    beta0 = jnp.sqrt(jnp.maximum(ii - 2.0 * alpha0 * vi + alpha0 * alpha0 * vv, 0.0) + EPS)
    inv = 1.0 / beta0
    ui = (ii - alpha0 * vi) * inv
    uh = (ih - alpha0 * vh) * inv
    uv = (vi - alpha0 * vv) * inv
    uu = (ui - alpha0 * uv) * inv
    jv = (vh - alpha0 * vi) * inv
    jj = (hh - 2.0 * alpha0 * ih + alpha0 * alpha0 * ii) * inv * inv
    alpha1 = (uh - alpha0 * ui) * inv
    square = (
        jj + alpha1 * alpha1 * uu + beta0 * beta0 * vv
        - 2.0 * alpha1 * alpha1 - 2.0 * beta0 * jv + 2.0 * alpha1 * beta0 * uv
    )
    beta1 = jnp.sqrt(jnp.maximum(square, 0.0) + EPS)
    last = 1.0 / beta1
    ch = inv * last * cy
    ci = -(alpha0 + alpha1) * inv * last * cy
    cv = (alpha1 * alpha0 * inv - beta0) * last * cx
    vector = ch * h + ci * y + cv * x
    return (vector[None], jnp.stack([alpha0, alpha1]), jnp.stack([beta0, beta1]))


def solution(mesh):
    return jax.shard_map(
        on_device,
        mesh=mesh,
        in_specs=(
            P("sec", "term", None),
            P("term", "sec", None, None),
            P("term", "sec", None, None),
            P("term"),
            P("term", "sec"),
            P("sec"),
            P("sec"),
        ),
        out_specs=(P("sec", "term", None), P(), P()),
        check_vma=False,
    )
```

time: 634 us -> 193 us (0.30)
  waiting for transfers between devices: 332 us -> 86.8 us
  blocking collectives: 202 us -> 0 us
  starting transfers between devices: 11.2 us -> 58.4 us
  matrix products: 36.9 us -> 0 us
  Pallas kernels: 0 us -> 25.7 us
  other arithmetic: 19.6 us -> 5.02 us
  between operations: 19.8 us -> 6.85 us
    psum x5 -> x0, blocking collectives: 202 us -> none  [the longest x2 80.8 us: on_device(): alpha = lax.psum(jnp.sum(vector * image), ('sec', 'term'))]
    psum x2 -> x0, waiting for transfers between devices: 154 us -> none  [on_device(): summed = lax.psum(total.reshape(full_count, sectors * width), 'term')]
    all_gather x2 -> x0, waiting for transfers between devices: 51.4 us -> none  [on_device(): full_rows = lax.all_gather(vector_bf, 'term', axis=1, tiled=True)]
    ppermute x4 -> x59, starting transfers between devices: 10.8 us -> 58.4 us  [the longest x8 21.2 us: pair_forward(): return lax.ppermute(x, 'sec', pairs)]
    ppermute x4 -> x59, waiting for transfers between devices: 127 us -> 86.8 us  [the longest x41 57.5 us: along_term(): return lax.ppermute(x, 'term', [(i, partner(i)) for i in range(count)])]
    dot_general x4 -> x0, matrix products: 36.9 us -> none  [on_device(): jnp.einsum('sij,sjk->isk', product, right_env[partial_term_index], prefer...]
    pallas_call x0 -> x2, Pallas kernels: none -> 25.7 us  [apply_terms(): pl.pallas_call(functools.partial(apply_kernel, chips, terms, rows), out_s...]
    reduce_sum x5 -> x1, other arithmetic: 11.6 us -> 1.25 us  [on_device(): jnp.sum(a * b)]
  transfers between devices with their start and end apart: 8 -> 59, of which waited for: 8 -> 27; matrix products, arithmetic and copies ran while one was open for 1% -> 1% of each run, Pallas kernels for 0% -> 0%
where the time goes in v1:
time: 193 us; the launch traced here: 192 us
  waiting for transfers between devices  86.8 us (45%)
  starting transfers between devices  58.4 us (30%)
  Pallas kernels  25.7 us (13%)
  local copies, waits for them, and re-layouts  9.1 us (5%)
  between operations  6.85 us (4%)
  other arithmetic  5.02 us (3%)
    ppermute x41, waiting for transfers between devices, along_term(): return lax.ppermute(x, 'term', [(i, partner(i)) for i in range(count)])  57.5 us
    pallas_call x2, Pallas kernels, apply_terms(): pl.pallas_call(functools.partial(apply_kernel, chips, terms, rows), out_s...  25.7 us
    ppermute x8, starting transfers between devices, pair_forward(): return lax.ppermute(x, 'sec', pairs)  21.2 us
    ppermute x41, starting transfers between devices, along_term(): return lax.ppermute(x, 'term', [(i, partner(i)) for i in range(count)])  20.2 us
    ppermute x8, waiting for transfers between devices, pair_exchange(): lax.ppermute(x, 'sec', [(i, i ^ 1) for i in range(count) if i ^ 1 < count])  14 us
    ppermute x8, starting transfers between devices, pair_exchange(): lax.ppermute(x, 'sec', [(i, i ^ 1) for i in range(count) if i ^ 1 < count])  12.6 us
    ppermute x8, waiting for transfers between devices, pair_forward(): return lax.ppermute(x, 'sec', pairs)  11.1 us
    ppermute x2, starting transfers between devices, sum_all(): lax.ppermute(tile, 'sec', [(i, i ^ bit) for i in range(sec_count)])  4.5 us
  transfers between devices with their start and end apart: 59, of which 27 were waited for; matrix products, arithmetic and copies ran while one was open for 1% of the time, Pallas kernels for 0%

profile of v1, /device:TPU:0, one launch (start us, length us, event | category | flops | bytes accessed | tf_op | source)
XLA Modules:
  0.0 191.9 jit_solution(8535005460433093743)
XLA Ops:
  3.0 3.0 %collective-permute-start.7 = (bf16[1,112,896]{2,1,0:T(8,128)(2,1)S(1)}, bf16[1,112,896]{2,1,0:T(8,128)(2,1)S(1)}, u32[]{:S(2)}, u32[]{:S(2)}) collective-permute-start(bf16[1,112,896]{2,1,0:T(8,128)(2,1)S(1)} %and_select_fusion.refs_0_), channel_id=1, source_target_pairs={{0,8},{8,0},{16,24},{24,16},{1,9},{9,1},{17,25},{25,17},{2,10},{10... | collective-permute-start | bytes 602120 | tf_op jit(solution)/shard_map/ppermute | solution.py:23
  6.0 2.6 %collective-permute-start.3 = (bf16[1,112,896]{2,1,0:T(8,128)(2,1)S(1)}, bf16[1,112,896]{2,1,0:T(8,128)(2,1)S(1)}, u32[]{:S(2)}, u32[]{:S(2)}) collective-permute-start(bf16[1,112,896]{2,1,0:T(8,128)(2,1)S(1)} %and_select_fusion.refs_0_), channel_id=1, source_target_pairs={{0,4},{1,5},{2,6},{3,7},{4,0},{5,1},{6,2},{7,3},{8,12},{9,13},{10,... | collective-permute-start | bytes 602120 | tf_op jit(solution)/shard_map/ppermute | solution.py:19
  8.6 1.6 collective-permute-start.1
  11.0 3.7 %collective-permute-start.15 = (bf16[1,112,896]{2,1,0:T(8,128)(2,1)S(1)}, bf16[1,112,896]{2,1,0:T(8,128)(2,1)S(1)}, u32[]{:S(2)}, u32[]{:S(2)}) collective-permute-start(bf16[1,112,896]{2,1,0:T(8,128)(2,1)S(1)} %collective-permute-done.7.refs_8_), channel_id=1, source_target_pairs={{0,16},{24,8},{1,17},{25,9},{2,18},{26,10},{3,19},{27,11},{4,20},{... | collective-permute-start | bytes 602120 | tf_op jit(solution)/shard_map/ppermute | solution.py:29
  14.8 3.0 %collective-permute-done.3.refs_4_ = bf16[1,112,896]{2,1,0:T(8,128)(2,1)S(1)} collective-permute-done((bf16[1,112,896]{2,1,0:T(8,128)(2,1)S(1)}, bf16[1,112,896]{2,1,0:T(8,128)(2,1)S(1)}, u32[]{:S(2)}, u32[]{:S(2)}) %collective-permute-start.3) | collective-permute-done | bytes 200736 | tf_op jit(solution)/shard_map/ppermute | solution.py:19
  18.3 1.1 collective-permute-start.5
  20.6 3.8 %collective-permute-done.11.refs_12_ = bf16[1,112,896]{2,1,0:T(8,128)(2,1)S(1)} collective-permute-done((bf16[1,112,896]{2,1,0:T(8,128)(2,1)S(1)}, bf16[1,112,896]{2,1,0:T(8,128)(2,1)S(1)}, u32[]{:S(2)}, u32[]{:S(2)}) %collective-permute-start.11) | collective-permute-done | bytes 200736 | tf_op jit(solution)/shard_map/ppermute | solution.py:23
  25.5 3.4 %collective-permute-start.19 = (bf16[1,112,896]{2,1,0:T(8,128)(2,1)S(1)}, bf16[1,112,896]{2,1,0:T(8,128)(2,1)S(1)}, u32[]{:S(2)}, u32[]{:S(2)}) collective-permute-start(bf16[1,112,896]{2,1,0:T(8,128)(2,1)S(1)} %collective-permute-done.11.refs_12_), channel_id=1, source_target_pairs={{0,16},{24,8},{1,17},{25,9},{2,18},{26,10},{3,19},{27,11},{4,20},{... | collective-permute-start | bytes 602120 | tf_op jit(solution)/shard_map/ppermute | solution.py:29
  29.6 3.0 %collective-permute-start.17 = (bf16[1,112,896]{2,1,0:T(8,128)(2,1)S(1)}, bf16[1,112,896]{2,1,0:T(8,128)(2,1)}, u32[]{:S(2)}, u32[]{:S(2)}) collective-permute-start(bf16[1,112,896]{2,1,0:T(8,128)(2,1)S(1)} %collective-permute-done.9.refs_10_), channel_id=1, source_target_pairs={{0,16},{24,8},{1,17},{25,9},{2,18},{26,10},{3,19},{27,11},{4,20},{... | collective-permute-start | bytes 602120 | tf_op jit(solution)/shard_map/ppermute | solution.py:29
  32.6 3.6 %collective-permute-start.21 = (bf16[1,112,896]{2,1,0:T(8,128)(2,1)S(1)}, bf16[1,112,896]{2,1,0:T(8,128)(2,1)}, u32[]{:S(2)}, u32[]{:S(2)}) collective-permute-start(bf16[1,112,896]{2,1,0:T(8,128)(2,1)S(1)} %collective-permute-done.13.refs_14_), channel_id=1, source_target_pairs={{0,16},{24,8},{1,17},{25,9},{2,18},{26,10},{3,19},{27,11},{4,20},{... | collective-permute-start | bytes 602120 | tf_op jit(solution)/shard_map/ppermute | solution.py:29
  36.8 1.1 collective-permute-done.17.refs_18_
  37.9 3.6 %collective-permute-done.21.refs_22_ = bf16[1,112,896]{2,1,0:T(8,128)(2,1)} collective-permute-done((bf16[1,112,896]{2,1,0:T(8,128)(2,1)S(1)}, bf16[1,112,896]{2,1,0:T(8,128)(2,1)}, u32[]{:S(2)}, u32[]{:S(2)}) %collective-permute-start.21) | collective-permute-done | bytes 200736 | tf_op jit(solution)/shard_map/ppermute | solution.py:29
  43.2 1.9 copy-done
  45.1 1.9 copy-done.1
  47.0 12.2 %apply_terms.2 = (f32[4,112,896]{2,1,0:T(8,128)S(1)}, bf16[4,112,896]{2,1,0:T(8,128)(2,1)S(1)}) custom-call(s32[8]{0:T(128)S(1)} %concatenate.3.scal, bf16[2,1,896,896]{3,2,1,0:T(8,128)(2,1)S(1)} %copy-done, bf16[2,1,896,896]{3,2,1,0:T(8,128)(2,1)S(1)} %copy-done.1, bf16[1,112,896]{2,1,0:T(8,128)(2,1)S(1)} %and_select_fusion.refs_0_, ...), custom_call_target="tpu_custom_call" | custom-call | tf_op jit(solution)/shard_map/apply_terms/pallas_call | solution.py:112
  59.4 2.3 %collective-permute-done.23 = bf16[4,112,896]{2,1,0:T(8,128)(2,1)S(1)} collective-permute-done((bf16[4,112,896]{2,1,0:T(8,128)(2,1)S(1)}, bf16[4,112,896]{2,1,0:T(8,128)(2,1)S(1)}, u32[]{:S(2)}, u32[]{:S(2)}) %collective-permute-start.23) | collective-permute-done | bytes 802848 | tf_op jit(solution)/shard_map/ppermute | solution.py:19
  62.7 4.0 %collective-permute-start.26 = (bf16[112,896]{1,0:T(8,128)(2,1)S(1)}, bf16[112,896]{1,0:T(8,128)(2,1)S(1)}, u32[]{:S(2)}, u32[]{:S(2)}) collective-permute-start(bf16[112,896]{1,0:T(8,128)(2,1)S(1)} %get-tuple-element.24), channel_id=1, source_target_pairs={{0,6},{1,7},{2,4},{3,5},{4,2},{5,3},{6,0},{7,1},{8,14},{9,15},{10,... | collective-permute-start | bytes 602120 | tf_op jit(solution)/shard_map/ppermute | solution.py:19
  66.7 2.2 %collective-permute-done.24 = bf16[112,896]{1,0:T(8,128)(2,1)S(1)} collective-permute-done((bf16[112,896]{1,0:T(8,128)(2,1)S(1)}, bf16[112,896]{1,0:T(8,128)(2,1)S(1)}, u32[]{:S(2)}, u32[]{:S(2)}) %collective-permute-start.24) | collective-permute-done | bytes 200736 | tf_op jit(solution)/shard_map/ppermute | solution.py:19
  68.9 8.0 %collective-permute-done.26 = bf16[112,896]{1,0:T(8,128)(2,1)S(1)} collective-permute-done((bf16[112,896]{1,0:T(8,128)(2,1)S(1)}, bf16[112,896]{1,0:T(8,128)(2,1)S(1)}, u32[]{:S(2)}, u32[]{:S(2)}) %collective-permute-start.26) | collective-permute-done | bytes 200736 | tf_op jit(solution)/shard_map/ppermute | solution.py:19
  76.9 7.4 %collective-permute-done.25 = bf16[112,896]{1,0:T(8,128)(2,1)S(1)} collective-permute-done((bf16[112,896]{1,0:T(8,128)(2,1)S(1)}, bf16[112,896]{1,0:T(8,128)(2,1)S(1)}, u32[]{:S(2)}, u32[]{:S(2)}) %collective-permute-start.25) | collective-permute-done | bytes 200736 | tf_op jit(solution)/shard_map/ppermute | solution.py:19
  84.4 3.5 %collective-permute-start.34 = (bf16[1,112,896]{2,1,0:T(8,128)(2,1)S(1)}, bf16[1,112,896]{2,1,0:T(8,128)(2,1)S(1)}, u32[]{:S(2)}, u32[]{:S(2)}) collective-permute-start(bf16[1,112,896]{2,1,0:T(8,128)(2,1)S(1)} %get-tuple-element.18.refs_0_), channel_id=1, source_target_pairs={{0,8},{8,0},{16,24},{24,16},{1,9},{9,1},{17,25},{25,17},{2,10},{10... | collective-permute-start | bytes 602120 | tf_op jit(solution)/shard_map/ppermute | solution.py:23
  87.9 3.2 %collective-permute-start.28 = (bf16[1,112,896]{2,1,0:T(8,128)(2,1)S(1)}, bf16[1,112,896]{2,1,0:T(8,128)(2,1)S(1)}, u32[]{:S(2)}, u32[]{:S(2)}) collective-permute-start(bf16[1,112,896]{2,1,0:T(8,128)(2,1)S(1)} %get-tuple-element.18.refs_0_), channel_id=1, source_target_pairs={{0,2},{1,3},{2,0},{3,1},{4,6},{5,7},{6,4},{7,5},{8,10},{9,11},{10,... | collective-permute-start | bytes 602120 | tf_op jit(solution)/shard_map/ppermute | solution.py:19
  91.1 1.5 collective-permute-done.34.refs_8_
  92.6 2.6 %collective-permute-start.42 = (bf16[1,112,896]{2,1,0:T(8,128)(2,1)S(1)}, bf16[1,112,896]{2,1,0:T(8,128)(2,1)S(1)}, u32[]{:S(2)}, u32[]{:S(2)}) collective-permute-start(bf16[1,112,896]{2,1,0:T(8,128)(2,1)S(1)} %collective-permute-done.34.refs_8_), channel_id=1, source_target_pairs={{0,16},{24,8},{1,17},{25,9},{2,18},{26,10},{3,19},{27,11},{4,20},{... | collective-permute-start | bytes 602120 | tf_op jit(solution)/shard_map/ppermute | solution.py:29
  95.3 3.8 %collective-permute-done.30.refs_4_ = bf16[1,112,896]{2,1,0:T(8,128)(2,1)S(1)} collective-permute-done((bf16[1,112,896]{2,1,0:T(8,128)(2,1)S(1)}, bf16[1,112,896]{2,1,0:T(8,128)(2,1)S(1)}, u32[]{:S(2)}, u32[]{:S(2)}) %collective-permute-start.30) | collective-permute-done | bytes 200736 | tf_op jit(solution)/shard_map/ppermute | solution.py:19
  99.5 2.4 %collective-permute-start.36 = (bf16[1,112,896]{2,1,0:T(8,128)(2,1)S(1)}, bf16[1,112,896]{2,1,0:T(8,128)(2,1)S(1)}, u32[]{:S(2)}, u32[]{:S(2)}) collective-permute-start(bf16[1,112,896]{2,1,0:T(8,128)(2,1)S(1)} %collective-permute-done.28.refs_2_), channel_id=1, source_target_pairs={{0,8},{8,0},{16,24},{24,16},{1,9},{9,1},{17,25},{25,17},{2,10},{10... | collective-permute-start | bytes 602120 | tf_op jit(solution)/shard_map/ppermute | solution.py:23
  101.9 5.0 %collective-permute-done.38.refs_12_ = bf16[1,112,896]{2,1,0:T(8,128)(2,1)S(1)} collective-permute-done((bf16[1,112,896]{2,1,0:T(8,128)(2,1)S(1)}, bf16[1,112,896]{2,1,0:T(8,128)(2,1)S(1)}, u32[]{:S(2)}, u32[]{:S(2)}) %collective-permute-start.38) | collective-permute-done | bytes 200736 | tf_op jit(solution)/shard_map/ppermute | solution.py:23
  107.6 2.1 %collective-permute-start.46 = (bf16[1,112,896]{2,1,0:T(8,128)(2,1)S(1)}, bf16[1,112,896]{2,1,0:T(8,128)(2,1)S(1)}, u32[]{:S(2)}, u32[]{:S(2)}) collective-permute-start(bf16[1,112,896]{2,1,0:T(8,128)(2,1)S(1)} %collective-permute-done.38.refs_12_), channel_id=1, source_target_pairs={{0,16},{24,8},{1,17},{25,9},{2,18},{26,10},{3,19},{27,11},{4,20},{... | collective-permute-start | bytes 602120 | tf_op jit(solution)/shard_map/ppermute | solution.py:29
  110.8 1.3 collective-permute-start.44
  112.2 2.3 %collective-permute-done.40.refs_14_ = bf16[1,112,896]{2,1,0:T(8,128)(2,1)S(1)} collective-permute-done((bf16[1,112,896]{2,1,0:T(8,128)(2,1)S(1)}, bf16[1,112,896]{2,1,0:T(8,128)(2,1)S(1)}, u32[]{:S(2)}, u32[]{:S(2)}) %collective-permute-start.40) | collective-permute-done | bytes 200736 | tf_op jit(solution)/shard_map/ppermute | solution.py:23
  114.5 1.3 collective-permute-start.48
  116.5 2.9 %collective-permute-done.44.refs_18_ = bf16[1,112,896]{2,1,0:T(8,128)(2,1)S(1)} collective-permute-done((bf16[1,112,896]{2,1,0:T(8,128)(2,1)S(1)}, bf16[1,112,896]{2,1,0:T(8,128)(2,1)S(1)}, u32[]{:S(2)}, u32[]{:S(2)}) %collective-permute-start.44) | collective-permute-done | bytes 200736 | tf_op jit(solution)/shard_map/ppermute | solution.py:29
  119.4 3.6 %collective-permute-done.48.refs_22_ = bf16[1,112,896]{2,1,0:T(8,128)(2,1)S(1)} collective-permute-done((bf16[1,112,896]{2,1,0:T(8,128)(2,1)S(1)}, bf16[1,112,896]{2,1,0:T(8,128)(2,1)S(1)}, u32[]{:S(2)}, u32[]{:S(2)}) %collective-permute-start.48) | collective-permute-done | bytes 200736 | tf_op jit(solution)/shard_map/ppermute | solution.py:29
  123.0 1.4 collective-permute-done.49.refs_23_
  124.5 13.5 %apply_terms.3 = (f32[4,112,896]{2,1,0:T(8,128)S(1)}, bf16[4,112,896]{2,1,0:T(8,128)(2,1)S(1)}) custom-call(s32[8]{0:T(128)S(1)} %concatenate.3.scal, bf16[2,1,896,896]{3,2,1,0:T(8,128)(2,1)S(1)} %copy-done, bf16[2,1,896,896]{3,2,1,0:T(8,128)(2,1)S(1)} %copy-done.1, bf16[1,112,896]{2,1,0:T(8,128)(2,1)S(1)} %get-tuple-element.18.refs_0_, ...), custom_call_target="tpu_custom_call" | custom-call | tf_op jit(solution)/shard_map/apply_terms/pallas_call | solution.py:112
  138.3 2.0 %collective-permute-done.50 = bf16[4,112,896]{2,1,0:T(8,128)(2,1)S(1)} collective-permute-done((bf16[4,112,896]{2,1,0:T(8,128)(2,1)S(1)}, bf16[4,112,896]{2,1,0:T(8,128)(2,1)S(1)}, u32[]{:S(2)}, u32[]{:S(2)}) %collective-permute-start.50) | collective-permute-done | bytes 802848 | tf_op jit(solution)/shard_map/ppermute | solution.py:19
  140.5 1.7 collective-permute-start.53
  142.2 1.8 collective-permute-start.52
  144.0 7.8 %collective-permute-done.51 = bf16[112,896]{1,0:T(8,128)(2,1)S(1)} collective-permute-done((bf16[112,896]{1,0:T(8,128)(2,1)S(1)}, bf16[112,896]{1,0:T(8,128)(2,1)S(1)}, u32[]{:S(2)}, u32[]{:S(2)}) %collective-permute-start.51) | collective-permute-done | bytes 200736 | tf_op jit(solution)/shard_map/ppermute | solution.py:19
  152.3 9.5 %collective-permute-done.52 = bf16[112,896]{1,0:T(8,128)(2,1)S(1)} collective-permute-done((bf16[112,896]{1,0:T(8,128)(2,1)S(1)}, bf16[112,896]{1,0:T(8,128)(2,1)S(1)}, u32[]{:S(2)}, u32[]{:S(2)}) %collective-permute-start.52) | collective-permute-done | bytes 200736 | tf_op jit(solution)/shard_map/ppermute | solution.py:19
  161.8 1.2 multiply_reduce_fusion
  163.1 3.9 %stack.53 = f32[6]{0:T(128)S(1)} concatenate(f32[1]{0:T(128)} %bitcast.3, f32[1]{0:T(128)} %bitcast.12, f32[1]{0:T(128)} %bitcast.13, f32[1]{0:T(128)} %bitcast.19, f32[1]{0:T(128)} %bitcast.20, f32[1]{0:T(128)} %bitcast.21), dimensions={0} | concatenate | bytes 48 | tf_op jit(solution)/shard_map/stack | solution.py:147
  167.0 1.2 collective-permute-done.54
  168.3 3.6 %collective-permute-done.55 = f32[8,128]{1,0:T(8,128)S(1)} collective-permute-done((f32[8,128]{1,0:T(8,128)S(1)}, f32[8,128]{1,0:T(8,128)S(1)}, u32[]{:S(2)}, u32[]{:S(2)}) %collective-permute-start.55) | collective-permute-done | bytes 4128 | tf_op jit(solution)/shard_map/ppermute | solution.py:19
  172.0 4.4 %collective-permute-done.56 = f32[8,128]{1,0:T(8,128)S(1)} collective-permute-done((f32[8,128]{1,0:T(8,128)S(1)}, f32[8,128]{1,0:T(8,128)S(1)}, u32[]{:S(2)}, u32[]{:S(2)}) %collective-permute-start.56) | collective-permute-done | bytes 4128 | tf_op jit(solution)/shard_map/ppermute | solution.py:19
  176.4 3.5 %collective-permute-start.57 = (f32[8,128]{1,0:T(8,128)S(1)}, f32[8,128]{1,0:T(8,128)S(1)}, u32[]{:S(2)}, u32[]{:S(2)}) collective-permute-start(f32[8,128]{1,0:T(8,128)S(1)} %add.141), channel_id=1, source_target_pairs={{0,8},{8,0},{16,24},{24,16},{1,9},{9,1},{17,25},{25,17},{2,10},{10... | collective-permute-start | bytes 12296 | tf_op jit(solution)/shard_map/ppermute | solution.py:155
  180.0 1.6 collective-permute-done.57
  182.5 2.6 %collective-permute-done.58 = f32[8,128]{1,0:T(8,128)S(1)} collective-permute-done((f32[8,128]{1,0:T(8,128)S(1)}, f32[8,128]{1,0:T(8,128)S(1)}, u32[]{:S(2)}, u32[]{:S(2)}) %collective-permute-start.58) | collective-permute-done | bytes 4128 | tf_op jit(solution)/shard_map/ppermute | solution.py:155
  (98 shorter events, 16.5 us)
Async XLA Ops:
  3.0 8.0 %collective-permute-start.7 = (bf16[1,112,896]{2,1,0:T(8,128)(2,1)S(1)}, bf16[1,112,896]{2,1,0:T(8,128)(2,1)S(1)}, u32[]{:S(2)}, u32[]{:S(2)}) collective-permute-start(bf16[1,112,896]{2,1,0:T(8,128)(2,1)S(1)} %and_select_fusion.refs_0_), channel_id=1, source_target_pairs={{0,8},{8,0},{16,24},{24,16},{1,9},{9,1},{17,25},{25,17},{2,10},{10... | collective-permute-start | bytes 602120 | tf_op jit(solution)/shard_map/ppermute | solution.py:23
  6.0 11.8 %collective-permute-start.3 = (bf16[1,112,896]{2,1,0:T(8,128)(2,1)S(1)}, bf16[1,112,896]{2,1,0:T(8,128)(2,1)S(1)}, u32[]{:S(2)}, u32[]{:S(2)}) collective-permute-start(bf16[1,112,896]{2,1,0:T(8,128)(2,1)S(1)} %and_select_fusion.refs_0_), channel_id=1, source_target_pairs={{0,4},{1,5},{2,6},{3,7},{4,0},{5,1},{6,2},{7,3},{8,12},{9,13},{10,... | collective-permute-start | bytes 602120 | tf_op jit(solution)/shard_map/ppermute | solution.py:19
  8.6 9.7 %collective-permute-start.1 = (bf16[1,112,896]{2,1,0:T(8,128)(2,1)S(1)}, bf16[1,112,896]{2,1,0:T(8,128)(2,1)S(1)}, u32[]{:S(2)}, u32[]{:S(2)}) collective-permute-start(bf16[1,112,896]{2,1,0:T(8,128)(2,1)S(1)} %and_select_fusion.refs_0_), channel_id=1, source_target_pairs={{0,2},{1,3},{2,0},{3,1},{4,6},{5,7},{6,4},{7,5},{8,10},{9,11},{10,... | collective-permute-start | bytes 602120 | tf_op jit(solution)/shard_map/ppermute | solution.py:19
  10.2 9.2 %collective-permute-start = (bf16[1,112,896]{2,1,0:T(8,128)(2,1)S(1)}, bf16[1,112,896]{2,1,0:T(8,128)(2,1)S(1)}, u32[]{:S(2)}, u32[]{:S(2)}) collective-permute-start(bf16[1,112,896]{2,1,0:T(8,128)(2,1)S(1)} %and_select_fusion.refs_0_), channel_id=1, source_target_pairs={{0,1},{1,0},{2,3},{3,2},{4,5},{5,4},{6,7},{7,6},{8,9},{9,8},{10,11... | collective-permute-start | bytes 602120 | tf_op jit(solution)/shard_map/ppermute | solution.py:19
  11.0 8.4 %collective-permute-start.15 = (bf16[1,112,896]{2,1,0:T(8,128)(2,1)S(1)}, bf16[1,112,896]{2,1,0:T(8,128)(2,1)S(1)}, u32[]{:S(2)}, u32[]{:S(2)}) collective-permute-start(bf16[1,112,896]{2,1,0:T(8,128)(2,1)S(1)} %collective-permute-done.7.refs_8_), channel_id=1, source_target_pairs={{0,16},{24,8},{1,17},{25,9},{2,18},{26,10},{3,19},{27,11},{4,20},{... | collective-permute-start | bytes 602120 | tf_op jit(solution)/shard_map/ppermute | solution.py:29
  14.7 5.8 %collective-permute-start.8 = (bf16[1,112,896]{2,1,0:T(8,128)(2,1)S(1)}, bf16[1,112,896]{2,1,0:T(8,128)(2,1)S(1)}, u32[]{:S(2)}, u32[]{:S(2)}) collective-permute-start(bf16[1,112,896]{2,1,0:T(8,128)(2,1)S(1)} %collective-permute-done.7.refs_8_), channel_id=1, source_target_pairs={{0,1},{1,0},{2,3},{3,2},{4,5},{5,4},{6,7},{7,6},{8,9},{9,8},{10,11... | collective-permute-start | bytes 602120 | tf_op jit(solution)/shard_map/ppermute | solution.py:19
  17.8 6.7 %collective-permute-start.11 = (bf16[1,112,896]{2,1,0:T(8,128)(2,1)S(1)}, bf16[1,112,896]{2,1,0:T(8,128)(2,1)S(1)}, u32[]{:S(2)}, u32[]{:S(2)}) collective-permute-start(bf16[1,112,896]{2,1,0:T(8,128)(2,1)S(1)} %collective-permute-done.3.refs_4_), channel_id=1, source_target_pairs={{0,8},{8,0},{16,24},{24,16},{1,9},{9,1},{17,25},{25,17},{2,10},{10... | collective-permute-start | bytes 602120 | tf_op jit(solution)/shard_map/ppermute | solution.py:23
  18.3 6.2 %collective-permute-start.5 = (bf16[1,112,896]{2,1,0:T(8,128)(2,1)S(1)}, bf16[1,112,896]{2,1,0:T(8,128)(2,1)S(1)}, u32[]{:S(2)}, u32[]{:S(2)}) collective-permute-start(bf16[1,112,896]{2,1,0:T(8,128)(2,1)S(1)} %collective-permute-done.3.refs_4_), channel_id=1, source_target_pairs={{0,2},{1,3},{2,0},{3,1},{4,6},{5,7},{6,4},{7,5},{8,10},{9,11},{10,... | collective-permute-start | bytes 602120 | tf_op jit(solution)/shard_map/ppermute | solution.py:19
  19.4 6.1 %collective-permute-start.4 = (bf16[1,112,896]{2,1,0:T(8,128)(2,1)S(1)}, bf16[1,112,896]{2,1,0:T(8,128)(2,1)S(1)}, u32[]{:S(2)}, u32[]{:S(2)}) collective-permute-start(bf16[1,112,896]{2,1,0:T(8,128)(2,1)S(1)} %collective-permute-done.3.refs_4_), channel_id=1, source_target_pairs={{0,1},{1,0},{2,3},{3,2},{4,5},{5,4},{6,7},{7,6},{8,9},{9,8},{10,11... | collective-permute-start | bytes 602120 | tf_op jit(solution)/shard_map/ppermute | solution.py:19
  19.4 9.5 %collective-permute-start.9 = (bf16[1,112,896]{2,1,0:T(8,128)(2,1)S(1)}, bf16[1,112,896]{2,1,0:T(8,128)(2,1)S(1)}, u32[]{:S(2)}, u32[]{:S(2)}) collective-permute-start(bf16[1,112,896]{2,1,0:T(8,128)(2,1)S(1)} %collective-permute-done.1.refs_2_), channel_id=1, source_target_pairs={{0,8},{8,0},{16,24},{24,16},{1,9},{9,1},{17,25},{25,17},{2,10},{10... | collective-permute-start | bytes 602120 | tf_op jit(solution)/shard_map/ppermute | solution.py:23
  20.5 8.6 %collective-permute-start.2 = (bf16[1,112,896]{2,1,0:T(8,128)(2,1)S(1)}, bf16[1,112,896]{2,1,0:T(8,128)(2,1)S(1)}, u32[]{:S(2)}, u32[]{:S(2)}) collective-permute-start(bf16[1,112,896]{2,1,0:T(8,128)(2,1)S(1)} %collective-permute-done.1.refs_2_), channel_id=1, source_target_pairs={{0,1},{1,0},{2,3},{3,2},{4,5},{5,4},{6,7},{7,6},{8,9},{9,8},{10,11... | collective-permute-start | bytes 602120 | tf_op jit(solution)/shard_map/ppermute | solution.py:19
  24.5 5.1 %collective-permute-start.16 = (bf16[1,112,896]{2,1,0:T(8,128)(2,1)S(1)}, bf16[1,112,896]{2,1,0:T(8,128)(2,1)S(1)}, u32[]{:S(2)}, u32[]{:S(2)}) collective-permute-start(bf16[1,112,896]{2,1,0:T(8,128)(2,1)S(1)} %collective-permute-done.15.refs_16_), channel_id=1, source_target_pairs={{0,1},{1,0},{2,3},{3,2},{4,5},{5,4},{6,7},{7,6},{8,9},{9,8},{10,11... | collective-permute-start | bytes 602120 | tf_op jit(solution)/shard_map/ppermute | solution.py:19
  24.5 8.1 %collective-permute-start.13 = (bf16[1,112,896]{2,1,0:T(8,128)(2,1)S(1)}, bf16[1,112,896]{2,1,0:T(8,128)(2,1)S(1)}, u32[]{:S(2)}, u32[]{:S(2)}) collective-permute-start(bf16[1,112,896]{2,1,0:T(8,128)(2,1)S(1)} %collective-permute-done.5.refs_6_), channel_id=1, source_target_pairs={{0,8},{8,0},{16,24},{24,16},{1,9},{9,1},{17,25},{25,17},{2,10},{10... | collective-permute-start | bytes 602120 | tf_op jit(solution)/shard_map/ppermute | solution.py:23
  25.5 10.7 %collective-permute-start.19 = (bf16[1,112,896]{2,1,0:T(8,128)(2,1)S(1)}, bf16[1,112,896]{2,1,0:T(8,128)(2,1)S(1)}, u32[]{:S(2)}, u32[]{:S(2)}) collective-permute-start(bf16[1,112,896]{2,1,0:T(8,128)(2,1)S(1)} %collective-permute-done.11.refs_12_), channel_id=1, source_target_pairs={{0,16},{24,8},{1,17},{25,9},{2,18},{26,10},{3,19},{27,11},{4,20},{... | collective-permute-start | bytes 602120 | tf_op jit(solution)/shard_map/ppermute | solution.py:29
  29.0 7.2 %collective-permute-start.12 = (bf16[1,112,896]{2,1,0:T(8,128)(2,1)S(1)}, bf16[1,112,896]{2,1,0:T(8,128)(2,1)S(1)}, u32[]{:S(2)}, u32[]{:S(2)}) collective-permute-start(bf16[1,112,896]{2,1,0:T(8,128)(2,1)S(1)} %collective-permute-done.11.refs_12_), channel_id=1, source_target_pairs={{0,1},{1,0},{2,3},{3,2},{4,5},{5,4},{6,7},{7,6},{8,9},{9,8},{10,11... | collective-permute-start | bytes 602120 | tf_op jit(solution)/shard_map/ppermute | solution.py:19
  29.1 7.7 %collective-permute-start.6 = (bf16[1,112,896]{2,1,0:T(8,128)(2,1)S(1)}, bf16[1,112,896]{2,1,0:T(8,128)(2,1)S(1)}, u32[]{:S(2)}, u32[]{:S(2)}) collective-permute-start(bf16[1,112,896]{2,1,0:T(8,128)(2,1)S(1)} %collective-permute-done.5.refs_6_), channel_id=1, source_target_pairs={{0,1},{1,0},{2,3},{3,2},{4,5},{5,4},{6,7},{7,6},{8,9},{9,8},{10,11... | collective-permute-start | bytes 602120 | tf_op jit(solution)/shard_map/ppermute | solution.py:19
  29.6 8.3 %collective-permute-start.17 = (bf16[1,112,896]{2,1,0:T(8,128)(2,1)S(1)}, bf16[1,112,896]{2,1,0:T(8,128)(2,1)}, u32[]{:S(2)}, u32[]{:S(2)}) collective-permute-start(bf16[1,112,896]{2,1,0:T(8,128)(2,1)S(1)} %collective-permute-done.9.refs_10_), channel_id=1, source_target_pairs={{0,16},{24,8},{1,17},{25,9},{2,18},{26,10},{3,19},{27,11},{4,20},{... | collective-permute-start | bytes 602120 | tf_op jit(solution)/shard_map/ppermute | solution.py:29
  32.6 8.8 %collective-permute-start.21 = (bf16[1,112,896]{2,1,0:T(8,128)(2,1)S(1)}, bf16[1,112,896]{2,1,0:T(8,128)(2,1)}, u32[]{:S(2)}, u32[]{:S(2)}) collective-permute-start(bf16[1,112,896]{2,1,0:T(8,128)(2,1)S(1)} %collective-permute-done.13.refs_14_), channel_id=1, source_target_pairs={{0,16},{24,8},{1,17},{25,9},{2,18},{26,10},{3,19},{27,11},{4,20},{... | collective-permute-start | bytes 602120 | tf_op jit(solution)/shard_map/ppermute | solution.py:29
  36.2 6.6 %collective-permute-start.10 = (bf16[1,112,896]{2,1,0:T(8,128)(2,1)S(1)}, bf16[1,112,896]{2,1,0:T(8,128)(2,1)}, u32[]{:S(2)}, u32[]{:S(2)}) collective-permute-start(bf16[1,112,896]{2,1,0:T(8,128)(2,1)S(1)} %collective-permute-done.9.refs_10_), channel_id=1, source_target_pairs={{0,1},{1,0},{2,3},{3,2},{4,5},{5,4},{6,7},{7,6},{8,9},{9,8},{10,11... | collective-permute-start | bytes 602120 | tf_op jit(solution)/shard_map/ppermute | solution.py:19
  36.2 6.6 %collective-permute-start.14 = (bf16[1,112,896]{2,1,0:T(8,128)(2,1)S(1)}, bf16[1,112,896]{2,1,0:T(8,128)(2,1)}, u32[]{:S(2)}, u32[]{:S(2)}) collective-permute-start(bf16[1,112,896]{2,1,0:T(8,128)(2,1)S(1)} %collective-permute-done.13.refs_14_), channel_id=1, source_target_pairs={{0,1},{1,0},{2,3},{3,2},{4,5},{5,4},{6,7},{7,6},{8,9},{9,8},{10,11... | collective-permute-start | bytes 602120 | tf_op jit(solution)/shard_map/ppermute | solution.py:19
  36.7 6.1 %collective-permute-start.20 = (bf16[1,112,896]{2,1,0:T(8,128)(2,1)S(1)}, bf16[1,112,896]{2,1,0:T(8,128)(2,1)}, u32[]{:S(2)}, u32[]{:S(2)}) collective-permute-start(bf16[1,112,896]{2,1,0:T(8,128)(2,1)S(1)} %collective-permute-done.19.refs_20_), channel_id=1, source_target_pairs={{0,1},{1,0},{2,3},{3,2},{4,5},{5,4},{6,7},{7,6},{8,9},{9,8},{10,11... | collective-permute-start | bytes 602120 | tf_op jit(solution)/shard_map/ppermute | solution.py:19
  61.8 7.1 %collective-permute-start.24 = (bf16[112,896]{1,0:T(8,128)(2,1)S(1)}, bf16[112,896]{1,0:T(8,128)(2,1)S(1)}, u32[]{:S(2)}, u32[]{:S(2)}) collective-permute-start(bf16[112,896]{1,0:T(8,128)(2,1)S(1)} %get-tuple-element.23), channel_id=1, source_target_pairs={{0,2},{1,3},{2,0},{3,1},{4,6},{5,7},{6,4},{7,5},{8,10},{9,11},{10,... | collective-permute-start | bytes 602120 | tf_op jit(solution)/shard_map/ppermute | solution.py:19
  62.7 14.2 %collective-permute-start.26 = (bf16[112,896]{1,0:T(8,128)(2,1)S(1)}, bf16[112,896]{1,0:T(8,128)(2,1)S(1)}, u32[]{:S(2)}, u32[]{:S(2)}) collective-permute-start(bf16[112,896]{1,0:T(8,128)(2,1)S(1)} %get-tuple-element.24), channel_id=1, source_target_pairs={{0,6},{1,7},{2,4},{3,5},{4,2},{5,3},{6,0},{7,1},{8,14},{9,15},{10,... | collective-permute-start | bytes 602120 | tf_op jit(solution)/shard_map/ppermute | solution.py:19
  66.7 17.6 %collective-permute-start.25 = (bf16[112,896]{1,0:T(8,128)(2,1)S(1)}, bf16[112,896]{1,0:T(8,128)(2,1)S(1)}, u32[]{:S(2)}, u32[]{:S(2)}) collective-permute-start(bf16[112,896]{1,0:T(8,128)(2,1)S(1)} %get-tuple-element.25), channel_id=1, source_target_pairs={{0,4},{1,5},{2,6},{3,7},{4,0},{5,1},{6,2},{7,3},{8,12},{9,13},{10,... | collective-permute-start | bytes 602120 | tf_op jit(solution)/shard_map/ppermute | solution.py:19
  84.4 8.2 %collective-permute-start.34 = (bf16[1,112,896]{2,1,0:T(8,128)(2,1)S(1)}, bf16[1,112,896]{2,1,0:T(8,128)(2,1)S(1)}, u32[]{:S(2)}, u32[]{:S(2)}) collective-permute-start(bf16[1,112,896]{2,1,0:T(8,128)(2,1)S(1)} %get-tuple-element.18.refs_0_), channel_id=1, source_target_pairs={{0,8},{8,0},{16,24},{24,16},{1,9},{9,1},{17,25},{25,17},{2,10},{10... | collective-permute-start | bytes 602120 | tf_op jit(solution)/shard_map/ppermute | solution.py:23
  87.9 11.2 %collective-permute-start.30 = (bf16[1,112,896]{2,1,0:T(8,128)(2,1)S(1)}, bf16[1,112,896]{2,1,0:T(8,128)(2,1)S(1)}, u32[]{:S(2)}, u32[]{:S(2)}) collective-permute-start(bf16[1,112,896]{2,1,0:T(8,128)(2,1)S(1)} %get-tuple-element.18.refs_0_), channel_id=1, source_target_pairs={{0,4},{1,5},{2,6},{3,7},{4,0},{5,1},{6,2},{7,3},{8,12},{9,13},{10,... | collective-permute-start | bytes 602120 | tf_op jit(solution)/shard_map/ppermute | solution.py:19
  87.9 11.5 %collective-permute-start.28 = (bf16[1,112,896]{2,1,0:T(8,128)(2,1)S(1)}, bf16[1,112,896]{2,1,0:T(8,128)(2,1)S(1)}, u32[]{:S(2)}, u32[]{:S(2)}) collective-permute-start(bf16[1,112,896]{2,1,0:T(8,128)(2,1)S(1)} %get-tuple-element.18.refs_0_), channel_id=1, source_target_pairs={{0,2},{1,3},{2,0},{3,1},{4,6},{5,7},{6,4},{7,5},{8,10},{9,11},{10,... | collective-permute-start | bytes 602120 | tf_op jit(solution)/shard_map/ppermute | solution.py:19
  91.1 8.3 %collective-permute-start.27 = (bf16[1,112,896]{2,1,0:T(8,128)(2,1)S(1)}, bf16[1,112,896]{2,1,0:T(8,128)(2,1)S(1)}, u32[]{:S(2)}, u32[]{:S(2)}) collective-permute-start(bf16[1,112,896]{2,1,0:T(8,128)(2,1)S(1)} %get-tuple-element.18.refs_0_), channel_id=1, source_target_pairs={{0,1},{1,0},{2,3},{3,2},{4,5},{5,4},{6,7},{7,6},{8,9},{9,8},{10,11... | collective-permute-start | bytes 602120 | tf_op jit(solution)/shard_map/ppermute | solution.py:19
  92.6 6.9 %collective-permute-start.42 = (bf16[1,112,896]{2,1,0:T(8,128)(2,1)S(1)}, bf16[1,112,896]{2,1,0:T(8,128)(2,1)S(1)}, u32[]{:S(2)}, u32[]{:S(2)}) collective-permute-start(bf16[1,112,896]{2,1,0:T(8,128)(2,1)S(1)} %collective-permute-done.34.refs_8_), channel_id=1, source_target_pairs={{0,16},{24,8},{1,17},{25,9},{2,18},{26,10},{3,19},{27,11},{4,20},{... | collective-permute-start | bytes 602120 | tf_op jit(solution)/shard_map/ppermute | solution.py:29
  95.2 6.7 %collective-permute-start.35 = (bf16[1,112,896]{2,1,0:T(8,128)(2,1)S(1)}, bf16[1,112,896]{2,1,0:T(8,128)(2,1)S(1)}, u32[]{:S(2)}, u32[]{:S(2)}) collective-permute-start(bf16[1,112,896]{2,1,0:T(8,128)(2,1)S(1)} %collective-permute-done.34.refs_8_), channel_id=1, source_target_pairs={{0,1},{1,0},{2,3},{3,2},{4,5},{5,4},{6,7},{7,6},{8,9},{9,8},{10,11... | collective-permute-start | bytes 602120 | tf_op jit(solution)/shard_map/ppermute | solution.py:19
  99.0 7.9 %collective-permute-start.38 = (bf16[1,112,896]{2,1,0:T(8,128)(2,1)S(1)}, bf16[1,112,896]{2,1,0:T(8,128)(2,1)S(1)}, u32[]{:S(2)}, u32[]{:S(2)}) collective-permute-start(bf16[1,112,896]{2,1,0:T(8,128)(2,1)S(1)} %collective-permute-done.30.refs_4_), channel_id=1, source_target_pairs={{0,8},{8,0},{16,24},{24,16},{1,9},{9,1},{17,25},{25,17},{2,10},{10... | collective-permute-start | bytes 602120 | tf_op jit(solution)/shard_map/ppermute | solution.py:23
  99.4 7.5 %collective-permute-start.32 = (bf16[1,112,896]{2,1,0:T(8,128)(2,1)S(1)}, bf16[1,112,896]{2,1,0:T(8,128)(2,1)S(1)}, u32[]{:S(2)}, u32[]{:S(2)}) collective-permute-start(bf16[1,112,896]{2,1,0:T(8,128)(2,1)S(1)} %collective-permute-done.30.refs_4_), channel_id=1, source_target_pairs={{0,2},{1,3},{2,0},{3,1},{4,6},{5,7},{6,4},{7,5},{8,10},{9,11},{10,... | collective-permute-start | bytes 602120 | tf_op jit(solution)/shard_map/ppermute | solution.py:19
  99.4 8.2 %collective-permute-start.31 = (bf16[1,112,896]{2,1,0:T(8,128)(2,1)S(1)}, bf16[1,112,896]{2,1,0:T(8,128)(2,1)S(1)}, u32[]{:S(2)}, u32[]{:S(2)}) collective-permute-start(bf16[1,112,896]{2,1,0:T(8,128)(2,1)S(1)} %collective-permute-done.30.refs_4_), channel_id=1, source_target_pairs={{0,1},{1,0},{2,3},{3,2},{4,5},{5,4},{6,7},{7,6},{8,9},{9,8},{10,11... | collective-permute-start | bytes 602120 | tf_op jit(solution)/shard_map/ppermute | solution.py:19
  99.5 10.8 %collective-permute-start.36 = (bf16[1,112,896]{2,1,0:T(8,128)(2,1)S(1)}, bf16[1,112,896]{2,1,0:T(8,128)(2,1)S(1)}, u32[]{:S(2)}, u32[]{:S(2)}) collective-permute-start(bf16[1,112,896]{2,1,0:T(8,128)(2,1)S(1)} %collective-permute-done.28.refs_2_), channel_id=1, source_target_pairs={{0,8},{8,0},{16,24},{24,16},{1,9},{9,1},{17,25},{25,17},{2,10},{10... | collective-permute-start | bytes 602120 | tf_op jit(solution)/shard_map/ppermute | solution.py:23
  101.9 8.4 %collective-permute-start.29 = (bf16[1,112,896]{2,1,0:T(8,128)(2,1)S(1)}, bf16[1,112,896]{2,1,0:T(8,128)(2,1)S(1)}, u32[]{:S(2)}, u32[]{:S(2)}) collective-permute-start(bf16[1,112,896]{2,1,0:T(8,128)(2,1)S(1)} %collective-permute-done.28.refs_2_), channel_id=1, source_target_pairs={{0,1},{1,0},{2,3},{3,2},{4,5},{5,4},{6,7},{7,6},{8,9},{9,8},{10,11... | collective-permute-start | bytes 602120 | tf_op jit(solution)/shard_map/ppermute | solution.py:19
  106.9 7.6 %collective-permute-start.40 = (bf16[1,112,896]{2,1,0:T(8,128)(2,1)S(1)}, bf16[1,112,896]{2,1,0:T(8,128)(2,1)S(1)}, u32[]{:S(2)}, u32[]{:S(2)}) collective-permute-start(bf16[1,112,896]{2,1,0:T(8,128)(2,1)S(1)} %collective-permute-done.32.refs_6_), channel_id=1, source_target_pairs={{0,8},{8,0},{16,24},{24,16},{1,9},{9,1},{17,25},{25,17},{2,10},{10... | collective-permute-start | bytes 602120 | tf_op jit(solution)/shard_map/ppermute | solution.py:23
  107.6 8.2 %collective-permute-start.46 = (bf16[1,112,896]{2,1,0:T(8,128)(2,1)S(1)}, bf16[1,112,896]{2,1,0:T(8,128)(2,1)S(1)}, u32[]{:S(2)}, u32[]{:S(2)}) collective-permute-start(bf16[1,112,896]{2,1,0:T(8,128)(2,1)S(1)} %collective-permute-done.38.refs_12_), channel_id=1, source_target_pairs={{0,16},{24,8},{1,17},{25,9},{2,18},{26,10},{3,19},{27,11},{4,20},{... | collective-permute-start | bytes 602120 | tf_op jit(solution)/shard_map/ppermute | solution.py:29
  110.3 5.6 %collective-permute-start.39 = (bf16[1,112,896]{2,1,0:T(8,128)(2,1)S(1)}, bf16[1,112,896]{2,1,0:T(8,128)(2,1)S(1)}, u32[]{:S(2)}, u32[]{:S(2)}) collective-permute-start(bf16[1,112,896]{2,1,0:T(8,128)(2,1)S(1)} %collective-permute-done.38.refs_12_), channel_id=1, source_target_pairs={{0,1},{1,0},{2,3},{3,2},{4,5},{5,4},{6,7},{7,6},{8,9},{9,8},{10,11... | collective-permute-start | bytes 602120 | tf_op jit(solution)/shard_map/ppermute | solution.py:19
  110.3 6.1 %collective-permute-start.33 = (bf16[1,112,896]{2,1,0:T(8,128)(2,1)S(1)}, bf16[1,112,896]{2,1,0:T(8,128)(2,1)S(1)}, u32[]{:S(2)}, u32[]{:S(2)}) collective-permute-start(bf16[1,112,896]{2,1,0:T(8,128)(2,1)S(1)} %collective-permute-done.32.refs_6_), channel_id=1, source_target_pairs={{0,1},{1,0},{2,3},{3,2},{4,5},{5,4},{6,7},{7,6},{8,9},{9,8},{10,11... | collective-permute-start | bytes 602120 | tf_op jit(solution)/shard_map/ppermute | solution.py:19
  110.8 8.6 %collective-permute-start.44 = (bf16[1,112,896]{2,1,0:T(8,128)(2,1)S(1)}, bf16[1,112,896]{2,1,0:T(8,128)(2,1)S(1)}, u32[]{:S(2)}, u32[]{:S(2)}) collective-permute-start(bf16[1,112,896]{2,1,0:T(8,128)(2,1)S(1)} %collective-permute-done.36.refs_10_), channel_id=1, source_target_pairs={{0,16},{24,8},{1,17},{25,9},{2,18},{26,10},{3,19},{27,11},{4,20},{... | collective-permute-start | bytes 602120 | tf_op jit(solution)/shard_map/ppermute | solution.py:29
  114.5 8.5 %collective-permute-start.48 = (bf16[1,112,896]{2,1,0:T(8,128)(2,1)S(1)}, bf16[1,112,896]{2,1,0:T(8,128)(2,1)S(1)}, u32[]{:S(2)}, u32[]{:S(2)}) collective-permute-start(bf16[1,112,896]{2,1,0:T(8,128)(2,1)S(1)} %collective-permute-done.40.refs_14_), channel_id=1, source_target_pairs={{0,16},{24,8},{1,17},{25,9},{2,18},{26,10},{3,19},{27,11},{4,20},{... | collective-permute-start | bytes 602120 | tf_op jit(solution)/shard_map/ppermute | solution.py:29
  115.9 7.2 %collective-permute-start.37 = (bf16[1,112,896]{2,1,0:T(8,128)(2,1)S(1)}, bf16[1,112,896]{2,1,0:T(8,128)(2,1)S(1)}, u32[]{:S(2)}, u32[]{:S(2)}) collective-permute-start(bf16[1,112,896]{2,1,0:T(8,128)(2,1)S(1)} %collective-permute-done.36.refs_10_), channel_id=1, source_target_pairs={{0,1},{1,0},{2,3},{3,2},{4,5},{5,4},{6,7},{7,6},{8,9},{9,8},{10,11... | collective-permute-start | bytes 602120 | tf_op jit(solution)/shard_map/ppermute | solution.py:19
  115.9 7.1 %collective-permute-start.41 = (bf16[1,112,896]{2,1,0:T(8,128)(2,1)S(1)}, bf16[1,112,896]{2,1,0:T(8,128)(2,1)S(1)}, u32[]{:S(2)}, u32[]{:S(2)}) collective-permute-start(bf16[1,112,896]{2,1,0:T(8,128)(2,1)S(1)} %collective-permute-done.40.refs_14_), channel_id=1, source_target_pairs={{0,1},{1,0},{2,3},{3,2},{4,5},{5,4},{6,7},{7,6},{8,9},{9,8},{10,11... | collective-permute-start | bytes 602120 | tf_op jit(solution)/shard_map/ppermute | solution.py:19
  116.4 6.6 %collective-permute-start.47 = (bf16[1,112,896]{2,1,0:T(8,128)(2,1)S(1)}, bf16[1,112,896]{2,1,0:T(8,128)(2,1)S(1)}, u32[]{:S(2)}, u32[]{:S(2)}) collective-permute-start(bf16[1,112,896]{2,1,0:T(8,128)(2,1)S(1)} %collective-permute-done.46.refs_20_), channel_id=1, source_target_pairs={{0,1},{1,0},{2,3},{3,2},{4,5},{5,4},{6,7},{7,6},{8,9},{9,8},{10,11... | collective-permute-start | bytes 602120 | tf_op jit(solution)/shard_map/ppermute | solution.py:19
  140.4 11.3 %collective-permute-start.51 = (bf16[112,896]{1,0:T(8,128)(2,1)S(1)}, bf16[112,896]{1,0:T(8,128)(2,1)S(1)}, u32[]{:S(2)}, u32[]{:S(2)}) collective-permute-start(bf16[112,896]{1,0:T(8,128)(2,1)S(1)} %get-tuple-element.20), channel_id=1, source_target_pairs={{0,2},{1,3},{2,0},{3,1},{4,6},{5,7},{6,4},{7,5},{8,10},{9,11},{10,... | collective-permute-start | bytes 602120 | tf_op jit(solution)/shard_map/ppermute | solution.py:19
  140.5 11.8 %collective-permute-start.53 = (bf16[112,896]{1,0:T(8,128)(2,1)S(1)}, bf16[112,896]{1,0:T(8,128)(2,1)S(1)}, u32[]{:S(2)}, u32[]{:S(2)}) collective-permute-start(bf16[112,896]{1,0:T(8,128)(2,1)S(1)} %get-tuple-element.21), channel_id=1, source_target_pairs={{0,6},{1,7},{2,4},{3,5},{4,2},{5,3},{6,0},{7,1},{8,14},{9,15},{10,... | collective-permute-start | bytes 602120 | tf_op jit(solution)/shard_map/ppermute | solution.py:19
  142.2 19.6 %collective-permute-start.52 = (bf16[112,896]{1,0:T(8,128)(2,1)S(1)}, bf16[112,896]{1,0:T(8,128)(2,1)S(1)}, u32[]{:S(2)}, u32[]{:S(2)}) collective-permute-start(bf16[112,896]{1,0:T(8,128)(2,1)S(1)} %get-tuple-element.22), channel_id=1, source_target_pairs={{0,4},{1,5},{2,6},{3,7},{4,0},{5,1},{6,2},{7,3},{8,12},{9,13},{10,... | collective-permute-start | bytes 602120 | tf_op jit(solution)/shard_map/ppermute | solution.py:19
  176.4 5.1 %collective-permute-start.57 = (f32[8,128]{1,0:T(8,128)S(1)}, f32[8,128]{1,0:T(8,128)S(1)}, u32[]{:S(2)}, u32[]{:S(2)}) collective-permute-start(f32[8,128]{1,0:T(8,128)S(1)} %add.141), channel_id=1, source_target_pairs={{0,8},{8,0},{16,24},{24,16},{1,9},{9,1},{17,25},{25,17},{2,10},{10... | collective-permute-start | bytes 12296 | tf_op jit(solution)/shard_map/ppermute | solution.py:155
  (14 other events, 61.1 us)

commit v2 on v1

v2 whole, which is shorter than its diff:
```python
import functools

import jax
import jax.numpy as jnp
from jax import lax
from jax.experimental import pallas as pl
from jax.experimental.pallas import tpu as pltpu
from jax.sharding import PartitionSpec as P

ITERS = 2


EPS = 1e-06

SCALE = 2.0**-10


def along_term(x, partner, count):
    return lax.ppermute(x, "term", [(i, partner(i)) for i in range(count)])


def pair_exchange(x, count):
    return lax.ppermute(x, "sec", [(i, i ^ 1) for i in range(count) if (i ^ 1) < count])


def pair_forward(x, count):
    pairs = [(i, i + 2) for i in range(0, count, 2) if i + 2 < count]
    pairs += [(i, i - 2) for i in range(1, count, 2) if i >= 2]
    return lax.ppermute(x, "sec", pairs)


def gather_pieces(shard, beside, sec_count, term_count):
    chips = term_count // 2
    own = {0: shard}
    order = sorted(range(1, chips), key=lambda i: (bin(i).count("1"), i))
    for i in order:
        bit = i & -i
        own[i] = along_term(own[i ^ bit], lambda t, b=bit: t ^ (2 * b), term_count)
    pair, beyond = {}, {}
    held, beside = lax.optimization_barrier((own[1], beside))
    own[1] = held
    for i in range(chips):
        pair[i] = pair_exchange(own[i], sec_count)
    for i in range(chips):
        beyond[i] = pair_forward(pair[i], sec_count)
    pieces = []
    for table in (own, pair, beyond):
        for i in range(chips):
            pieces.append(table[i])
            pieces.append(along_term(table[i], lambda t: t ^ 1, term_count))
    return pieces, beside


def apply_kernel(chips, terms, rows, scal, left, right, *refs):
    pieces = refs[: 6 * chips]
    mine, theirs, x_s, l_s, r_s, a_s, l_sem, r_sem = refs[6 * chips :]
    width = x_s.shape[2]
    z, c = scal[2 * terms], scal[2 * terms + 1]
    block_rows, block_cols = scal[2 * terms + 2], scal[2 * terms + 3]

    def l_copy(w):
        return pltpu.make_async_copy(left.at[w, 0], l_s.at[w], l_sem.at[w])

    def r_copy(w):
        return pltpu.make_async_copy(right.at[w, 0], r_s.at[pl.ds(w * width, width)], r_sem.at[w])

    for w in range(terms):
        l_copy(w).start()
    for w in range(terms):
        r_copy(w).start()
    for w in range(terms):
        for source in range(3):

            @pl.when(scal[w] == source)
            def _():
                for i in range(chips):
                    for other in range(2):
                        t = jnp.bitwise_xor(z, i) * 2 + jnp.bitwise_xor(c, other)
                        piece = pieces[source * 2 * chips + 2 * i + other]
                        x_s[w, pl.ds(pl.multiple_of(t * rows, rows), rows), :] = piece[0]

    for w in range(terms):
        on = scal[terms + w].astype(jnp.float32)
        l_copy(w).wait()
        product = jnp.dot(l_s[w], x_s[w], preferred_element_type=jnp.float32)
        a_s[:, w * width : (w + 1) * width] = (product * on).astype(jnp.bfloat16)
    for w in range(terms):
        r_copy(w).wait()
    col = lax.broadcasted_iota(jnp.int32, (2 * rows, width), 1)
    row = lax.broadcasted_iota(jnp.int32, (2 * rows, width), 0)
    for i in range(chips):
        start = pl.multiple_of(jnp.bitwise_xor(z, i) * 2 * rows, 2 * rows)
        total = jnp.dot(
            a_s[pl.ds(start, 2 * rows), :], r_s[...], preferred_element_type=jnp.float32
        )
        inside = (row + start < block_rows) & (col < block_cols)
        total = jnp.where(inside, total, 0.0)
        first = c == 0
        mine[i] = jnp.where(first, total[:rows], total[rows:])
        theirs[i] = jnp.where(first, total[rows:], total[:rows]).astype(theirs.dtype)


def apply_terms(scal, left_env, right_env, pieces, rows):
    terms, _, width, _ = left_env.shape
    chips = len(pieces) // 6
    smem, hbm, vmem = (
        pl.BlockSpec(memory_space=m) for m in (pltpu.SMEM, pltpu.HBM, pltpu.VMEM)
    )
    return pl.pallas_call(
        functools.partial(apply_kernel, chips, terms, rows),
        out_shape=(
            jax.ShapeDtypeStruct((chips, rows, width), jnp.float32),
            jax.ShapeDtypeStruct((chips, rows, width), jnp.bfloat16),
        ),
        in_specs=[smem, hbm, hbm] + [vmem] * len(pieces),
        out_specs=(vmem, vmem),
        scratch_shapes=[
            pltpu.VMEM((terms, width, width), jnp.bfloat16),
            pltpu.VMEM((terms, width, width), jnp.bfloat16),
            pltpu.VMEM((terms * width, width), jnp.bfloat16),
            pltpu.VMEM((width, terms * width), jnp.bfloat16),
            pltpu.SemaphoreType.DMA((terms,)),
            pltpu.SemaphoreType.DMA((terms,)),
        ],
        compiler_params=pltpu.CompilerParams(vmem_limit_bytes=46 * 2**20),
        name="apply_terms",
    )(scal, left_env, right_env, *pieces)


def reduce_parts(mine, theirs, term_count):
    other = along_term(theirs, lambda t: t ^ 1, term_count)
    totals = [mine[i] + other[i].astype(jnp.float32) for i in range(term_count // 2)]
    parts = [
        along_term(totals[i].astype(jnp.bfloat16), lambda t, b=i: t ^ (2 * b), term_count)
        for i in range(1, term_count // 2)
    ]
    return totals[0], parts


def all_sum(tile, sec_count, term_count):
    bit = 1
    while bit < term_count:
        tile = tile + along_term(tile, lambda t, b=bit: t ^ b, term_count)
        bit *= 2
    bit = 1
    while bit < sec_count:
        tile = tile + lax.ppermute(tile, "sec", [(i, i ^ bit) for i in range(sec_count)])
        bit *= 2
    return tile


def lane_sums(tile, products):
    for k, (a, b) in products.items():
        line = jnp.sum(a * b, axis=0, keepdims=True)
        tile[k : k + 1, :] = sum(line[:, j : j + 128] for j in range(0, line.shape[1], 128))


def first_gram_kernel(x_ref, y_ref, tile):
    x, y = x_ref[0].astype(jnp.float32), y_ref[...]
    tile[...] = jnp.zeros_like(tile)
    lane_sums(tile, {0: (x, x), 1: (x, y), 2: (y, y)})


def gram_kernel(before, x_ref, y_ref, own, *refs):
    h_ref, tile = refs[-2:]
    h = own[...]
    for part in refs[:-2]:
        h = h + part[...].astype(jnp.float32)
    h_ref[...] = h
    x, y = x_ref[0].astype(jnp.float32), y_ref[...]
    tile[...] = before[...]
    lane_sums(tile, {3: (x, h), 4: (y, h), 5: (h, h)})


def finish_kernel(tile, x_ref, y_ref, h_ref, vector, alphas, betas):
    sums = jnp.sum(tile[...], axis=1, keepdims=True)
    xx, xy, yy, xh, yh, hh = (sums[k : k + 1, :] for k in range(6))
    cx = 1.0 / jnp.sqrt(xx + EPS)
    cy = cx / SCALE
    vv, vi, ii = xx * cx * cx, xy * cx * cy, yy * cy * cy
    vh, ih, hh = xh * cx * cy, yh * cy * cy, hh * cy * cy
    alpha0 = vi
    square0 = ii - 2.0 * alpha0 * vi + alpha0 * alpha0 * vv
    beta0 = jnp.sqrt(jnp.maximum(square0, 0.0) + EPS)
    inv = 1.0 / beta0
    ui = (ii - alpha0 * vi) * inv
    uh = (ih - alpha0 * vh) * inv
    uv = (vi - alpha0 * vv) * inv
    uu = (ui - alpha0 * uv) * inv
    jv = (vh - alpha0 * vi) * inv
    jj = (hh - 2.0 * alpha0 * ih + alpha0 * alpha0 * ii) * inv * inv
    alpha1 = (uh - alpha0 * ui) * inv
    square1 = (
        jj + alpha1 * alpha1 * uu + beta0 * beta0 * vv
        - 2.0 * alpha1 * alpha1 - 2.0 * beta0 * jv + 2.0 * alpha1 * beta0 * uv
    )
    beta1 = jnp.sqrt(jnp.maximum(square1, 0.0) + EPS)
    last = 1.0 / beta1
    ch = inv * last * cy
    ci = -(alpha0 + alpha1) * inv * last * cy
    cv = (alpha1 * alpha0 * inv - beta0) * last * cx
    vector[0] = ch * h_ref[...] + ci * y_ref[...] + cv * x_ref[0].astype(jnp.float32)
    alphas[0], alphas[1] = alpha0[0, 0], alpha1[0, 0]
    betas[0], betas[1] = beta0[0, 0], beta1[0, 0]


def on_device(theta, left_env, right_env, term_shift, term_on, block_rows, block_cols):
    rows, width = theta.shape[1:]
    sec_count, term_count = lax.axis_size("sec"), lax.axis_size("term")
    sec, term = lax.axis_index("sec"), lax.axis_index("term")
    row = term * rows + lax.broadcasted_iota(jnp.int32, (1, rows, width), 1)
    col = lax.broadcasted_iota(jnp.int32, (1, rows, width), 2)
    start = jnp.where((row < block_rows[0]) & (col < block_cols[0]), theta, jnp.zeros_like(theta))
    toward_pair = 1 - 2 * (sec % 2)
    source = jnp.where(term_shift == 0, 0, jnp.where(term_shift == toward_pair, 1, 2))
    scal = jnp.concatenate(
        [source, term_on[:, 0], jnp.stack([term // 2, term % 2]), block_rows, block_cols]
    ).astype(jnp.int32)

    vmem, smem = (pl.BlockSpec(memory_space=m) for m in (pltpu.VMEM, pltpu.SMEM))
    small = pltpu.CompilerParams(vmem_limit_bytes=8 * 2**20)
    block = jax.ShapeDtypeStruct((rows, width), jnp.float32)
    tile = jax.ShapeDtypeStruct((8, 128), jnp.float32)
    pair = jax.ShapeDtypeStruct((2,), jnp.float32)

    pieces, scal = gather_pieces(start, scal, sec_count, term_count)
    mine, theirs = apply_terms(scal, left_env, right_env, pieces, rows)
    own, got = reduce_parts(mine, theirs, term_count)
    y = (own + sum(part.astype(jnp.float32) for part in got)) * SCALE
    sums = pl.pallas_call(
        first_gram_kernel, out_shape=tile, in_specs=[vmem] * 2, out_specs=vmem,
        compiler_params=small, name="first_gram",
    )(start, y)
    shard = y.astype(jnp.bfloat16)[None]
    pieces, sums = gather_pieces(shard, sums, sec_count, term_count)
    mine, theirs = apply_terms(scal, left_env, right_env, pieces, rows)
    own, got = reduce_parts(mine, theirs, term_count)
    h, sums = pl.pallas_call(
        gram_kernel,
        out_shape=(block, tile),
        in_specs=[vmem] * (4 + len(got)),
        out_specs=(vmem, vmem),
        compiler_params=small,
        name="gram",
    )(sums, start, y, own, *got)
    sums = all_sum(sums, sec_count, term_count)
    vector, alphas, betas = pl.pallas_call(
        finish_kernel,
        out_shape=(jax.ShapeDtypeStruct((1, rows, width), jnp.float32), pair, pair),
        in_specs=[vmem] * 4,
        out_specs=(vmem, smem, smem),
        compiler_params=small,
        name="finish",
    )(sums, start, y, h)
    return (vector, alphas, betas)


def solution(mesh):
    return jax.shard_map(
        on_device,
        mesh=mesh,
        in_specs=(
            P("sec", "term", None),
            P("term", "sec", None, None),
            P("term", "sec", None, None),
            P("term"),
            P("term", "sec"),
            P("sec"),
            P("sec"),
        ),
        out_specs=(P("sec", "term", None), P(), P()),
        check_vma=False,
    )
```

time: 193 us -> 167 us (0.87)
  waiting for transfers between devices: 86.8 us -> 77.8 us
  local copies, waits for them, and re-layouts: 9.1 us -> 0.73 us
  Pallas kernels: 25.7 us -> 20.8 us
  starting transfers between devices: 58.4 us -> 63.1 us
  between operations: 6.85 us -> 2.44 us
  other arithmetic: 5.02 us -> 2.2 us
    pallas_call x2, Pallas kernels: 25.7 us -> 19.3 us  [apply_terms(): pl.pallas_call(functools.partial(apply_kernel, chips, terms, rows), out_s...]
    ppermute x41, waiting for transfers between devices: 57.5 us -> 52.9 us  [along_term(): return lax.ppermute(x, 'term', [(i, partner(i)) for i in range(count)])]
    another operation x1 -> x0, local copies, waits for them, and re-layouts: 3.87 us -> none  [sum_all(): tile = jnp.broadcast_to(jnp.stack(values)[:, None], (len(values), 128))]
    unnamed x6 -> x0, local copies, waits for them, and re-layouts: 3.82 us -> none
    ppermute x8, waiting for transfers between devices: 14 us -> 10.2 us  [pair_exchange(): lax.ppermute(x, 'sec', [(i, i ^ 1) for i in range(count) if i ^ 1 < count])]
    ppermute x8, starting transfers between devices: 21.2 us -> 23.9 us  [pair_forward(): return lax.ppermute(x, 'sec', pairs)]
    ppermute x41, starting transfers between devices: 20.2 us -> 22.8 us  [along_term(): return lax.ppermute(x, 'term', [(i, partner(i)) for i in range(count)])]
  transfers between devices with their start and end apart: 59 -> 59, of which waited for: 27 -> 26; matrix products, arithmetic and copies ran while one was open for 1% -> 1% of each run, Pallas kernels for 0% -> 0%
where the time goes in v2:
time: 167 us
  waiting for transfers between devices  77.8 us (47%)
  starting transfers between devices  63.1 us (38%)
  Pallas kernels  20.8 us (12%)
  between operations  2.44 us (1%)
  other arithmetic  2.2 us (1%)
    ppermute x41, waiting for transfers between devices, along_term(): return lax.ppermute(x, 'term', [(i, partner(i)) for i in range(count)])  52.9 us
    ppermute x8, starting transfers between devices, pair_forward(): return lax.ppermute(x, 'sec', pairs)  23.9 us
    ppermute x41, starting transfers between devices, along_term(): return lax.ppermute(x, 'term', [(i, partner(i)) for i in range(count)])  22.8 us
    pallas_call x2, Pallas kernels, apply_terms(): pl.pallas_call(functools.partial(apply_kernel, chips, terms, rows), out_s...  19.3 us
    ppermute x8, starting transfers between devices, pair_exchange(): lax.ppermute(x, 'sec', [(i, i ^ 1) for i in range(count) if i ^ 1 < count])  11.9 us
    ppermute x8, waiting for transfers between devices, pair_forward(): return lax.ppermute(x, 'sec', pairs)  11.3 us
    ppermute x8, waiting for transfers between devices, pair_exchange(): lax.ppermute(x, 'sec', [(i, i ^ 1) for i in range(count) if i ^ 1 < count])  10.2 us
    ppermute x2, starting transfers between devices, all_sum(): lax.ppermute(tile, 'sec', [(i, i ^ bit) for i in range(sec_count)])  4.51 us
  transfers between devices with their start and end apart: 59, of which 26 were waited for; matrix products, arithmetic and copies ran while one was open for 1% of the time, Pallas kernels for 0%

profile of v2, /device:TPU:0, one launch (start us, length us, event | category | flops | bytes accessed | tf_op | source)
XLA Modules:
  0.0 167.0 jit_solution(11432029485509093184)
XLA Ops:
  3.0 3.0 %collective-permute-start.7 = (bf16[1,112,896]{2,1,0:T(8,128)(2,1)S(1)}, bf16[1,112,896]{2,1,0:T(8,128)(2,1)S(1)}, u32[]{:S(2)}, u32[]{:S(2)}) collective-permute-start(bf16[1,112,896]{2,1,0:T(8,128)(2,1)S(1)} %and_select_fusion.refs_0_.x_ref), channel_id=1, source_target_pairs={{0,8},{8,0},{16,24},{24,16},{1,9},{9,1},{17,25},{25,17},{2,10},{10... | collective-permute-start | bytes 602120 | tf_op jit(solution)/shard_map/ppermute | solution.py:23
  6.0 2.6 %collective-permute-start.3 = (bf16[1,112,896]{2,1,0:T(8,128)(2,1)S(1)}, bf16[1,112,896]{2,1,0:T(8,128)(2,1)S(1)}, u32[]{:S(2)}, u32[]{:S(2)}) collective-permute-start(bf16[1,112,896]{2,1,0:T(8,128)(2,1)S(1)} %and_select_fusion.refs_0_.x_ref), channel_id=1, source_target_pairs={{0,4},{1,5},{2,6},{3,7},{4,0},{5,1},{6,2},{7,3},{8,12},{9,13},{10,... | collective-permute-start | bytes 602120 | tf_op jit(solution)/shard_map/ppermute | solution.py:19
  8.6 1.6 collective-permute-start
  11.0 3.7 %collective-permute-start.15 = (bf16[1,112,896]{2,1,0:T(8,128)(2,1)S(1)}, bf16[1,112,896]{2,1,0:T(8,128)(2,1)S(1)}, u32[]{:S(2)}, u32[]{:S(2)}) collective-permute-start(bf16[1,112,896]{2,1,0:T(8,128)(2,1)S(1)} %collective-permute-done.7.refs_8_), channel_id=1, source_target_pairs={{0,16},{24,8},{1,17},{25,9},{2,18},{26,10},{3,19},{27,11},{4,20},{... | collective-permute-start | bytes 602120 | tf_op jit(solution)/shard_map/ppermute | solution.py:29
  14.8 3.0 %collective-permute-done.3.refs_4_ = bf16[1,112,896]{2,1,0:T(8,128)(2,1)S(1)} collective-permute-done((bf16[1,112,896]{2,1,0:T(8,128)(2,1)S(1)}, bf16[1,112,896]{2,1,0:T(8,128)(2,1)S(1)}, u32[]{:S(2)}, u32[]{:S(2)}) %collective-permute-start.3) | collective-permute-done | bytes 200736 | tf_op jit(solution)/shard_map/ppermute | solution.py:19
  18.3 1.1 collective-permute-start.5
  22.0 1.5 collective-permute-done.11.refs_12_
  24.0 1.5 collective-permute-start.13
  25.5 3.4 %collective-permute-start.19 = (bf16[1,112,896]{2,1,0:T(8,128)(2,1)S(1)}, bf16[1,112,896]{2,1,0:T(8,128)(2,1)S(1)}, u32[]{:S(2)}, u32[]{:S(2)}) collective-permute-start(bf16[1,112,896]{2,1,0:T(8,128)(2,1)S(1)} %collective-permute-done.11.refs_12_), channel_id=1, source_target_pairs={{0,16},{24,8},{1,17},{25,9},{2,18},{26,10},{3,19},{27,11},{4,20},{... | collective-permute-start | bytes 602120 | tf_op jit(solution)/shard_map/ppermute | solution.py:29
  29.6 3.1 %collective-permute-start.17 = (bf16[1,112,896]{2,1,0:T(8,128)(2,1)S(1)}, bf16[1,112,896]{2,1,0:T(8,128)(2,1)S(1)}, u32[]{:S(2)}, u32[]{:S(2)}) collective-permute-start(bf16[1,112,896]{2,1,0:T(8,128)(2,1)S(1)} %collective-permute-done.9.refs_10_), channel_id=1, source_target_pairs={{0,16},{24,8},{1,17},{25,9},{2,18},{26,10},{3,19},{27,11},{4,20},{... | collective-permute-start | bytes 602120 | tf_op jit(solution)/shard_map/ppermute | solution.py:29
  32.7 3.3 %collective-permute-start.21 = (bf16[1,112,896]{2,1,0:T(8,128)(2,1)S(1)}, bf16[1,112,896]{2,1,0:T(8,128)(2,1)S(1)}, u32[]{:S(2)}, u32[]{:S(2)}) collective-permute-start(bf16[1,112,896]{2,1,0:T(8,128)(2,1)S(1)} %collective-permute-done.13.refs_14_), channel_id=1, source_target_pairs={{0,16},{24,8},{1,17},{25,9},{2,18},{26,10},{3,19},{27,11},{4,20},{... | collective-permute-start | bytes 602120 | tf_op jit(solution)/shard_map/ppermute | solution.py:29
  36.7 1.3 collective-permute-done.17.refs_18_
  38.0 3.4 %collective-permute-done.21.refs_22_ = bf16[1,112,896]{2,1,0:T(8,128)(2,1)S(1)} collective-permute-done((bf16[1,112,896]{2,1,0:T(8,128)(2,1)S(1)}, bf16[1,112,896]{2,1,0:T(8,128)(2,1)S(1)}, u32[]{:S(2)}, u32[]{:S(2)}) %collective-permute-start.21) | collective-permute-done | bytes 200736 | tf_op jit(solution)/shard_map/ppermute | solution.py:29
  41.4 1.4 collective-permute-done.22.refs_23_
  42.8 9.7 %apply_terms.2 = (f32[4,112,896]{2,1,0:T(8,128)S(1)}, bf16[4,112,896]{2,1,0:T(8,128)(2,1)S(1)}) custom-call(s32[8]{0:T(128)S(1)} %concatenate.3.scal, bf16[2,1,896,896]{3,2,1,0:T(8,128)(2,1)} %left.3, bf16[2,1,896,896]{3,2,1,0:T(8,128)(2,1)} %right.3, bf16[1,112,896]{2,1,0:T(8,128)(2,1)S(1)} %and_select_fusion.refs_0_.x_ref, ...), custom_call_target="tpu_custom_call" | custom-call | tf_op jit(solution)/shard_map/apply_terms/pallas_call | solution.py:109
  52.7 2.2 %collective-permute-done.23 = bf16[4,112,896]{2,1,0:T(8,128)(2,1)S(1)} collective-permute-done((bf16[4,112,896]{2,1,0:T(8,128)(2,1)S(1)}, bf16[4,112,896]{2,1,0:T(8,128)(2,1)S(1)}, u32[]{:S(2)}, u32[]{:S(2)}) %collective-permute-start.23) | collective-permute-done | bytes 802848 | tf_op jit(solution)/shard_map/ppermute | solution.py:19
  55.0 1.2 collective-permute-start.24
  56.2 3.6 %collective-permute-start.26 = (bf16[112,896]{1,0:T(8,128)(2,1)S(1)}, bf16[112,896]{1,0:T(8,128)(2,1)S(1)}, u32[]{:S(2)}, u32[]{:S(2)}) collective-permute-start(bf16[112,896]{1,0:T(8,128)(2,1)S(1)} %get-tuple-element.30), channel_id=1, source_target_pairs={{0,6},{1,7},{2,4},{3,5},{4,2},{5,3},{6,0},{7,1},{8,14},{9,15},{10,... | collective-permute-start | bytes 602120 | tf_op jit(solution)/shard_map/ppermute | solution.py:19
  60.3 1.8 %collective-permute-done.24 = bf16[112,896]{1,0:T(8,128)(2,1)S(1)} collective-permute-done((bf16[112,896]{1,0:T(8,128)(2,1)S(1)}, bf16[112,896]{1,0:T(8,128)(2,1)S(1)}, u32[]{:S(2)}, u32[]{:S(2)}) %collective-permute-start.24) | collective-permute-done | bytes 200736 | tf_op jit(solution)/shard_map/ppermute | solution.py:19
  62.1 7.8 %collective-permute-done.26 = bf16[112,896]{1,0:T(8,128)(2,1)S(1)} collective-permute-done((bf16[112,896]{1,0:T(8,128)(2,1)S(1)}, bf16[112,896]{1,0:T(8,128)(2,1)S(1)}, u32[]{:S(2)}, u32[]{:S(2)}) %collective-permute-start.26) | collective-permute-done | bytes 200736 | tf_op jit(solution)/shard_map/ppermute | solution.py:19
  69.9 8.3 %collective-permute-done.25 = bf16[112,896]{1,0:T(8,128)(2,1)S(1)} collective-permute-done((bf16[112,896]{1,0:T(8,128)(2,1)S(1)}, bf16[112,896]{1,0:T(8,128)(2,1)S(1)}, u32[]{:S(2)}, u32[]{:S(2)}) %collective-permute-start.25) | collective-permute-done | bytes 200736 | tf_op jit(solution)/shard_map/ppermute | solution.py:19
  78.4 2.7 %collective-permute-start.34 = (bf16[1,112,896]{2,1,0:T(8,128)(2,1)S(1)}, bf16[1,112,896]{2,1,0:T(8,128)(2,1)S(1)}, u32[]{:S(2)}, u32[]{:S(2)}) collective-permute-start(bf16[1,112,896]{2,1,0:T(8,128)(2,1)S(1)} %get-tuple-element.23.refs_0_), channel_id=1, source_target_pairs={{0,8},{8,0},{16,24},{24,16},{1,9},{9,1},{17,25},{25,17},{2,10},{10... | collective-permute-start | bytes 602120 | tf_op jit(solution)/shard_map/ppermute | solution.py:23
  81.1 3.2 %collective-permute-start.27 = (bf16[1,112,896]{2,1,0:T(8,128)(2,1)S(1)}, bf16[1,112,896]{2,1,0:T(8,128)(2,1)S(1)}, u32[]{:S(2)}, u32[]{:S(2)}) collective-permute-start(bf16[1,112,896]{2,1,0:T(8,128)(2,1)S(1)} %get-tuple-element.23.refs_0_), channel_id=1, source_target_pairs={{0,2},{1,3},{2,0},{3,1},{4,6},{5,7},{6,4},{7,5},{8,10},{9,11},{10,... | collective-permute-start | bytes 602120 | tf_op jit(solution)/shard_map/ppermute | solution.py:19
  84.3 1.3 collective-permute-done.34.refs_8_
  85.5 3.5 %collective-permute-start.42 = (bf16[1,112,896]{2,1,0:T(8,128)(2,1)S(1)}, bf16[1,112,896]{2,1,0:T(8,128)(2,1)S(1)}, u32[]{:S(2)}, u32[]{:S(2)}) collective-permute-start(bf16[1,112,896]{2,1,0:T(8,128)(2,1)S(1)} %collective-permute-done.34.refs_8_), channel_id=1, source_target_pairs={{0,16},{24,8},{1,17},{25,9},{2,18},{26,10},{3,19},{27,11},{4,20},{... | collective-permute-start | bytes 602120 | tf_op jit(solution)/shard_map/ppermute | solution.py:29
  89.1 3.0 %collective-permute-done.30.refs_4_ = bf16[1,112,896]{2,1,0:T(8,128)(2,1)S(1)} collective-permute-done((bf16[1,112,896]{2,1,0:T(8,128)(2,1)S(1)}, bf16[1,112,896]{2,1,0:T(8,128)(2,1)S(1)}, u32[]{:S(2)}, u32[]{:S(2)}) %collective-permute-start.30) | collective-permute-done | bytes 200736 | tf_op jit(solution)/shard_map/ppermute | solution.py:19
  92.7 2.1 %collective-permute-start.36 = (bf16[1,112,896]{2,1,0:T(8,128)(2,1)S(1)}, bf16[1,112,896]{2,1,0:T(8,128)(2,1)S(1)}, u32[]{:S(2)}, u32[]{:S(2)}) collective-permute-start(bf16[1,112,896]{2,1,0:T(8,128)(2,1)S(1)} %collective-permute-done.27.refs_2_), channel_id=1, source_target_pairs={{0,8},{8,0},{16,24},{24,16},{1,9},{9,1},{17,25},{25,17},{2,10},{10... | collective-permute-start | bytes 602120 | tf_op jit(solution)/shard_map/ppermute | solution.py:23
  94.9 5.2 %collective-permute-done.38.refs_12_ = bf16[1,112,896]{2,1,0:T(8,128)(2,1)S(1)} collective-permute-done((bf16[1,112,896]{2,1,0:T(8,128)(2,1)S(1)}, bf16[1,112,896]{2,1,0:T(8,128)(2,1)S(1)}, u32[]{:S(2)}, u32[]{:S(2)}) %collective-permute-start.38) | collective-permute-done | bytes 200736 | tf_op jit(solution)/shard_map/ppermute | solution.py:23
  100.8 3.1 %collective-permute-start.46 = (bf16[1,112,896]{2,1,0:T(8,128)(2,1)S(1)}, bf16[1,112,896]{2,1,0:T(8,128)(2,1)S(1)}, u32[]{:S(2)}, u32[]{:S(2)}) collective-permute-start(bf16[1,112,896]{2,1,0:T(8,128)(2,1)S(1)} %collective-permute-done.38.refs_12_), channel_id=1, source_target_pairs={{0,16},{24,8},{1,17},{25,9},{2,18},{26,10},{3,19},{27,11},{4,20},{... | collective-permute-start | bytes 602120 | tf_op jit(solution)/shard_map/ppermute | solution.py:29
  104.4 1.6 collective-permute-start.44
  106.1 1.5 collective-permute-done.40.refs_14_
  107.6 2.1 %collective-permute-start.48 = (bf16[1,112,896]{2,1,0:T(8,128)(2,1)S(1)}, bf16[1,112,896]{2,1,0:T(8,128)(2,1)S(1)}, u32[]{:S(2)}, u32[]{:S(2)}) collective-permute-start(bf16[1,112,896]{2,1,0:T(8,128)(2,1)S(1)} %collective-permute-done.40.refs_14_), channel_id=1, source_target_pairs={{0,16},{24,8},{1,17},{25,9},{2,18},{26,10},{3,19},{27,11},{4,20},{... | collective-permute-start | bytes 602120 | tf_op jit(solution)/shard_map/ppermute | solution.py:29
  110.4 3.0 %collective-permute-done.44.refs_18_ = bf16[1,112,896]{2,1,0:T(8,128)(2,1)S(1)} collective-permute-done((bf16[1,112,896]{2,1,0:T(8,128)(2,1)S(1)}, bf16[1,112,896]{2,1,0:T(8,128)(2,1)S(1)}, u32[]{:S(2)}, u32[]{:S(2)}) %collective-permute-start.44) | collective-permute-done | bytes 200736 | tf_op jit(solution)/shard_map/ppermute | solution.py:29
  113.5 3.6 %collective-permute-done.48.refs_22_ = bf16[1,112,896]{2,1,0:T(8,128)(2,1)S(1)} collective-permute-done((bf16[1,112,896]{2,1,0:T(8,128)(2,1)S(1)}, bf16[1,112,896]{2,1,0:T(8,128)(2,1)S(1)}, u32[]{:S(2)}, u32[]{:S(2)}) %collective-permute-start.48) | collective-permute-done | bytes 200736 | tf_op jit(solution)/shard_map/ppermute | solution.py:29
  117.1 1.4 collective-permute-done.49.refs_23_
  118.5 9.7 %apply_terms.3 = (f32[4,112,896]{2,1,0:T(8,128)S(1)}, bf16[4,112,896]{2,1,0:T(8,128)(2,1)S(1)}) custom-call(s32[8]{0:T(128)S(1)} %concatenate.3.scal, bf16[2,1,896,896]{3,2,1,0:T(8,128)(2,1)} %left.3, bf16[2,1,896,896]{3,2,1,0:T(8,128)(2,1)} %right.3, bf16[1,112,896]{2,1,0:T(8,128)(2,1)S(1)} %get-tuple-element.23.refs_0_, ...), custom_call_target="tpu_custom_call" | custom-call | tf_op jit(solution)/shard_map/apply_terms/pallas_call | solution.py:109
  128.4 2.2 %collective-permute-done.50 = bf16[4,112,896]{2,1,0:T(8,128)(2,1)S(1)} collective-permute-done((bf16[4,112,896]{2,1,0:T(8,128)(2,1)S(1)}, bf16[4,112,896]{2,1,0:T(8,128)(2,1)S(1)}, u32[]{:S(2)}, u32[]{:S(2)}) %collective-permute-start.50) | collective-permute-done | bytes 802848 | tf_op jit(solution)/shard_map/ppermute | solution.py:19
  130.7 1.4 collective-permute-start.53
  132.2 3.0 %collective-permute-start.51 = (bf16[112,896]{1,0:T(8,128)(2,1)S(1)}, bf16[112,896]{1,0:T(8,128)(2,1)S(1)}, u32[]{:S(2)}, u32[]{:S(2)}) collective-permute-start(bf16[112,896]{1,0:T(8,128)(2,1)S(1)} %get-tuple-element.27), channel_id=1, source_target_pairs={{0,2},{1,3},{2,0},{3,1},{4,6},{5,7},{6,4},{7,5},{8,10},{9,11},{10,... | collective-permute-start | bytes 602120 | tf_op jit(solution)/shard_map/ppermute | solution.py:19
  135.2 5.4 %collective-permute-done.53.refs_2_ = bf16[112,896]{1,0:T(8,128)(2,1)S(1)} collective-permute-done((bf16[112,896]{1,0:T(8,128)(2,1)S(1)}, bf16[112,896]{1,0:T(8,128)(2,1)S(1)}, u32[]{:S(2)}, u32[]{:S(2)}) %collective-permute-start.53) | collective-permute-done | bytes 200736 | tf_op jit(solution)/shard_map/ppermute | solution.py:19
  140.6 7.8 %collective-permute-done.52.refs_1_ = bf16[112,896]{1,0:T(8,128)(2,1)S(1)} collective-permute-done((bf16[112,896]{1,0:T(8,128)(2,1)S(1)}, bf16[112,896]{1,0:T(8,128)(2,1)S(1)}, u32[]{:S(2)}, u32[]{:S(2)}) %collective-permute-start.52) | collective-permute-done | bytes 200736 | tf_op jit(solution)/shard_map/ppermute | solution.py:19
  149.9 3.6 %collective-permute-done.55 = f32[8,128]{1,0:T(8,128)S(1)} collective-permute-done((f32[8,128]{1,0:T(8,128)S(1)}, f32[8,128]{1,0:T(8,128)S(1)}, u32[]{:S(2)}, u32[]{:S(2)}) %collective-permute-start.55) | collective-permute-done | bytes 4128 | tf_op jit(solution)/shard_map/ppermute | solution.py:19
  154.6 3.4 %collective-permute-done.56 = f32[8,128]{1,0:T(8,128)S(1)} collective-permute-done((f32[8,128]{1,0:T(8,128)S(1)}, f32[8,128]{1,0:T(8,128)S(1)}, u32[]{:S(2)}, u32[]{:S(2)}) %collective-permute-start.56) | collective-permute-done | bytes 4128 | tf_op jit(solution)/shard_map/ppermute | solution.py:19
  158.0 2.6 %collective-permute-start.57 = (f32[8,128]{1,0:T(8,128)S(1)}, f32[8,128]{1,0:T(8,128)S(1)}, u32[]{:S(2)}, u32[]{:S(2)}) collective-permute-start(f32[8,128]{1,0:T(8,128)S(1)} %add.93), channel_id=1, source_target_pairs={{0,8},{8,0},{16,24},{24,16},{1,9},{9,1},{17,25},{25,17},{2,10},{10... | collective-permute-start | bytes 12296 | tf_op jit(solution)/shard_map/ppermute | solution.py:147
  160.6 1.6 collective-permute-done.57
  162.2 1.9 %collective-permute-start.58 = (f32[8,128]{1,0:T(8,128)S(1)}, f32[8,128]{1,0:T(8,128)S(1)}, u32[]{:S(2)}, u32[]{:S(2)}) collective-permute-start(f32[8,128]{1,0:T(8,128)S(1)} %add.94), channel_id=1, source_target_pairs={{0,16},{8,24},{16,0},{24,8},{1,17},{9,25},{17,1},{25,9},{2,18},{10... | collective-permute-start | bytes 12296 | tf_op jit(solution)/shard_map/ppermute | solution.py:147
  164.1 1.7 %collective-permute-done.58 = f32[8,128]{1,0:T(8,128)S(1)} collective-permute-done((f32[8,128]{1,0:T(8,128)S(1)}, f32[8,128]{1,0:T(8,128)S(1)}, u32[]{:S(2)}, u32[]{:S(2)}) %collective-permute-start.58) | collective-permute-done | bytes 4128 | tf_op jit(solution)/shard_map/ppermute | solution.py:147
  165.8 1.1 finish.1
  (88 shorter events, 13.3 us)
Async XLA Ops:
  3.0 8.0 %collective-permute-start.7 = (bf16[1,112,896]{2,1,0:T(8,128)(2,1)S(1)}, bf16[1,112,896]{2,1,0:T(8,128)(2,1)S(1)}, u32[]{:S(2)}, u32[]{:S(2)}) collective-permute-start(bf16[1,112,896]{2,1,0:T(8,128)(2,1)S(1)} %and_select_fusion.refs_0_.x_ref), channel_id=1, source_target_pairs={{0,8},{8,0},{16,24},{24,16},{1,9},{9,1},{17,25},{25,17},{2,10},{10... | collective-permute-start | bytes 602120 | tf_op jit(solution)/shard_map/ppermute | solution.py:23
  6.0 11.8 %collective-permute-start.3 = (bf16[1,112,896]{2,1,0:T(8,128)(2,1)S(1)}, bf16[1,112,896]{2,1,0:T(8,128)(2,1)S(1)}, u32[]{:S(2)}, u32[]{:S(2)}) collective-permute-start(bf16[1,112,896]{2,1,0:T(8,128)(2,1)S(1)} %and_select_fusion.refs_0_.x_ref), channel_id=1, source_target_pairs={{0,4},{1,5},{2,6},{3,7},{4,0},{5,1},{6,2},{7,3},{8,12},{9,13},{10,... | collective-permute-start | bytes 602120 | tf_op jit(solution)/shard_map/ppermute | solution.py:19
  8.6 9.7 %collective-permute-start = (bf16[1,112,896]{2,1,0:T(8,128)(2,1)S(1)}, bf16[1,112,896]{2,1,0:T(8,128)(2,1)S(1)}, u32[]{:S(2)}, u32[]{:S(2)}) collective-permute-start(bf16[1,112,896]{2,1,0:T(8,128)(2,1)S(1)} %and_select_fusion.refs_0_.x_ref), channel_id=1, source_target_pairs={{0,2},{1,3},{2,0},{3,1},{4,6},{5,7},{6,4},{7,5},{8,10},{9,11},{10,... | collective-permute-start | bytes 602120 | tf_op jit(solution)/shard_map/ppermute | solution.py:19
  10.2 10.6 %collective-permute-start.1 = (bf16[1,112,896]{2,1,0:T(8,128)(2,1)S(1)}, bf16[1,112,896]{2,1,0:T(8,128)(2,1)S(1)}, u32[]{:S(2)}, u32[]{:S(2)}) collective-permute-start(bf16[1,112,896]{2,1,0:T(8,128)(2,1)S(1)} %and_select_fusion.refs_0_.x_ref), channel_id=1, source_target_pairs={{0,1},{1,0},{2,3},{3,2},{4,5},{5,4},{6,7},{7,6},{8,9},{9,8},{10,11... | collective-permute-start | bytes 602120 | tf_op jit(solution)/shard_map/ppermute | solution.py:19
  11.0 9.8 %collective-permute-start.15 = (bf16[1,112,896]{2,1,0:T(8,128)(2,1)S(1)}, bf16[1,112,896]{2,1,0:T(8,128)(2,1)S(1)}, u32[]{:S(2)}, u32[]{:S(2)}) collective-permute-start(bf16[1,112,896]{2,1,0:T(8,128)(2,1)S(1)} %collective-permute-done.7.refs_8_), channel_id=1, source_target_pairs={{0,16},{24,8},{1,17},{25,9},{2,18},{26,10},{3,19},{27,11},{4,20},{... | collective-permute-start | bytes 602120 | tf_op jit(solution)/shard_map/ppermute | solution.py:29
  14.7 7.2 %collective-permute-start.8 = (bf16[1,112,896]{2,1,0:T(8,128)(2,1)S(1)}, bf16[1,112,896]{2,1,0:T(8,128)(2,1)S(1)}, u32[]{:S(2)}, u32[]{:S(2)}) collective-permute-start(bf16[1,112,896]{2,1,0:T(8,128)(2,1)S(1)} %collective-permute-done.7.refs_8_), channel_id=1, source_target_pairs={{0,1},{1,0},{2,3},{3,2},{4,5},{5,4},{6,7},{7,6},{8,9},{9,8},{10,11... | collective-permute-start | bytes 602120 | tf_op jit(solution)/shard_map/ppermute | solution.py:19
  17.8 5.7 %collective-permute-start.11 = (bf16[1,112,896]{2,1,0:T(8,128)(2,1)S(1)}, bf16[1,112,896]{2,1,0:T(8,128)(2,1)S(1)}, u32[]{:S(2)}, u32[]{:S(2)}) collective-permute-start(bf16[1,112,896]{2,1,0:T(8,128)(2,1)S(1)} %collective-permute-done.3.refs_4_), channel_id=1, source_target_pairs={{0,8},{8,0},{16,24},{24,16},{1,9},{9,1},{17,25},{25,17},{2,10},{10... | collective-permute-start | bytes 602120 | tf_op jit(solution)/shard_map/ppermute | solution.py:23
  18.3 5.7 %collective-permute-start.5 = (bf16[1,112,896]{2,1,0:T(8,128)(2,1)S(1)}, bf16[1,112,896]{2,1,0:T(8,128)(2,1)S(1)}, u32[]{:S(2)}, u32[]{:S(2)}) collective-permute-start(bf16[1,112,896]{2,1,0:T(8,128)(2,1)S(1)} %collective-permute-done.3.refs_4_), channel_id=1, source_target_pairs={{0,2},{1,3},{2,0},{3,1},{4,6},{5,7},{6,4},{7,5},{8,10},{9,11},{10,... | collective-permute-start | bytes 602120 | tf_op jit(solution)/shard_map/ppermute | solution.py:19
  20.8 4.7 %collective-permute-start.4 = (bf16[1,112,896]{2,1,0:T(8,128)(2,1)S(1)}, bf16[1,112,896]{2,1,0:T(8,128)(2,1)S(1)}, u32[]{:S(2)}, u32[]{:S(2)}) collective-permute-start(bf16[1,112,896]{2,1,0:T(8,128)(2,1)S(1)} %collective-permute-done.3.refs_4_), channel_id=1, source_target_pairs={{0,1},{1,0},{2,3},{3,2},{4,5},{5,4},{6,7},{7,6},{8,9},{9,8},{10,11... | collective-permute-start | bytes 602120 | tf_op jit(solution)/shard_map/ppermute | solution.py:19
  20.9 8.1 %collective-permute-start.9 = (bf16[1,112,896]{2,1,0:T(8,128)(2,1)S(1)}, bf16[1,112,896]{2,1,0:T(8,128)(2,1)S(1)}, u32[]{:S(2)}, u32[]{:S(2)}) collective-permute-start(bf16[1,112,896]{2,1,0:T(8,128)(2,1)S(1)} %collective-permute-done.refs_2_), channel_id=1, source_target_pairs={{0,8},{8,0},{16,24},{24,16},{1,9},{9,1},{17,25},{25,17},{2,10},{10... | collective-permute-start | bytes 602120 | tf_op jit(solution)/shard_map/ppermute | solution.py:23
  21.9 7.2 %collective-permute-start.2 = (bf16[1,112,896]{2,1,0:T(8,128)(2,1)S(1)}, bf16[1,112,896]{2,1,0:T(8,128)(2,1)S(1)}, u32[]{:S(2)}, u32[]{:S(2)}) collective-permute-start(bf16[1,112,896]{2,1,0:T(8,128)(2,1)S(1)} %collective-permute-done.refs_2_), channel_id=1, source_target_pairs={{0,1},{1,0},{2,3},{3,2},{4,5},{5,4},{6,7},{7,6},{8,9},{9,8},{10,11... | collective-permute-start | bytes 602120 | tf_op jit(solution)/shard_map/ppermute | solution.py:19
  23.5 6.0 %collective-permute-start.16 = (bf16[1,112,896]{2,1,0:T(8,128)(2,1)S(1)}, bf16[1,112,896]{2,1,0:T(8,128)(2,1)S(1)}, u32[]{:S(2)}, u32[]{:S(2)}) collective-permute-start(bf16[1,112,896]{2,1,0:T(8,128)(2,1)S(1)} %collective-permute-done.15.refs_16_), channel_id=1, source_target_pairs={{0,1},{1,0},{2,3},{3,2},{4,5},{5,4},{6,7},{7,6},{8,9},{9,8},{10,11... | collective-permute-start | bytes 602120 | tf_op jit(solution)/shard_map/ppermute | solution.py:19
  24.0 8.7 %collective-permute-start.13 = (bf16[1,112,896]{2,1,0:T(8,128)(2,1)S(1)}, bf16[1,112,896]{2,1,0:T(8,128)(2,1)S(1)}, u32[]{:S(2)}, u32[]{:S(2)}) collective-permute-start(bf16[1,112,896]{2,1,0:T(8,128)(2,1)S(1)} %collective-permute-done.5.refs_6_), channel_id=1, source_target_pairs={{0,8},{8,0},{16,24},{24,16},{1,9},{9,1},{17,25},{25,17},{2,10},{10... | collective-permute-start | bytes 602120 | tf_op jit(solution)/shard_map/ppermute | solution.py:23
  25.5 10.5 %collective-permute-start.19 = (bf16[1,112,896]{2,1,0:T(8,128)(2,1)S(1)}, bf16[1,112,896]{2,1,0:T(8,128)(2,1)S(1)}, u32[]{:S(2)}, u32[]{:S(2)}) collective-permute-start(bf16[1,112,896]{2,1,0:T(8,128)(2,1)S(1)} %collective-permute-done.11.refs_12_), channel_id=1, source_target_pairs={{0,16},{24,8},{1,17},{25,9},{2,18},{26,10},{3,19},{27,11},{4,20},{... | collective-permute-start | bytes 602120 | tf_op jit(solution)/shard_map/ppermute | solution.py:29
  29.0 7.1 %collective-permute-start.12 = (bf16[1,112,896]{2,1,0:T(8,128)(2,1)S(1)}, bf16[1,112,896]{2,1,0:T(8,128)(2,1)S(1)}, u32[]{:S(2)}, u32[]{:S(2)}) collective-permute-start(bf16[1,112,896]{2,1,0:T(8,128)(2,1)S(1)} %collective-permute-done.11.refs_12_), channel_id=1, source_target_pairs={{0,1},{1,0},{2,3},{3,2},{4,5},{5,4},{6,7},{7,6},{8,9},{9,8},{10,11... | collective-permute-start | bytes 602120 | tf_op jit(solution)/shard_map/ppermute | solution.py:19
  29.1 7.5 %collective-permute-start.6 = (bf16[1,112,896]{2,1,0:T(8,128)(2,1)S(1)}, bf16[1,112,896]{2,1,0:T(8,128)(2,1)S(1)}, u32[]{:S(2)}, u32[]{:S(2)}) collective-permute-start(bf16[1,112,896]{2,1,0:T(8,128)(2,1)S(1)} %collective-permute-done.5.refs_6_), channel_id=1, source_target_pairs={{0,1},{1,0},{2,3},{3,2},{4,5},{5,4},{6,7},{7,6},{8,9},{9,8},{10,11... | collective-permute-start | bytes 602120 | tf_op jit(solution)/shard_map/ppermute | solution.py:19
  29.6 8.4 %collective-permute-start.17 = (bf16[1,112,896]{2,1,0:T(8,128)(2,1)S(1)}, bf16[1,112,896]{2,1,0:T(8,128)(2,1)S(1)}, u32[]{:S(2)}, u32[]{:S(2)}) collective-permute-start(bf16[1,112,896]{2,1,0:T(8,128)(2,1)S(1)} %collective-permute-done.9.refs_10_), channel_id=1, source_target_pairs={{0,16},{24,8},{1,17},{25,9},{2,18},{26,10},{3,19},{27,11},{4,20},{... | collective-permute-start | bytes 602120 | tf_op jit(solution)/shard_map/ppermute | solution.py:29
  32.7 8.7 %collective-permute-start.21 = (bf16[1,112,896]{2,1,0:T(8,128)(2,1)S(1)}, bf16[1,112,896]{2,1,0:T(8,128)(2,1)S(1)}, u32[]{:S(2)}, u32[]{:S(2)}) collective-permute-start(bf16[1,112,896]{2,1,0:T(8,128)(2,1)S(1)} %collective-permute-done.13.refs_14_), channel_id=1, source_target_pairs={{0,16},{24,8},{1,17},{25,9},{2,18},{26,10},{3,19},{27,11},{4,20},{... | collective-permute-start | bytes 602120 | tf_op jit(solution)/shard_map/ppermute | solution.py:29
  36.0 5.4 %collective-permute-start.10 = (bf16[1,112,896]{2,1,0:T(8,128)(2,1)S(1)}, bf16[1,112,896]{2,1,0:T(8,128)(2,1)S(1)}, u32[]{:S(2)}, u32[]{:S(2)}) collective-permute-start(bf16[1,112,896]{2,1,0:T(8,128)(2,1)S(1)} %collective-permute-done.9.refs_10_), channel_id=1, source_target_pairs={{0,1},{1,0},{2,3},{3,2},{4,5},{5,4},{6,7},{7,6},{8,9},{9,8},{10,11... | collective-permute-start | bytes 602120 | tf_op jit(solution)/shard_map/ppermute | solution.py:19
  36.1 5.3 %collective-permute-start.14 = (bf16[1,112,896]{2,1,0:T(8,128)(2,1)S(1)}, bf16[1,112,896]{2,1,0:T(8,128)(2,1)S(1)}, u32[]{:S(2)}, u32[]{:S(2)}) collective-permute-start(bf16[1,112,896]{2,1,0:T(8,128)(2,1)S(1)} %collective-permute-done.13.refs_14_), channel_id=1, source_target_pairs={{0,1},{1,0},{2,3},{3,2},{4,5},{5,4},{6,7},{7,6},{8,9},{9,8},{10,11... | collective-permute-start | bytes 602120 | tf_op jit(solution)/shard_map/ppermute | solution.py:19
  36.6 4.8 %collective-permute-start.20 = (bf16[1,112,896]{2,1,0:T(8,128)(2,1)S(1)}, bf16[1,112,896]{2,1,0:T(8,128)(2,1)S(1)}, u32[]{:S(2)}, u32[]{:S(2)}) collective-permute-start(bf16[1,112,896]{2,1,0:T(8,128)(2,1)S(1)} %collective-permute-done.19.refs_20_), channel_id=1, source_target_pairs={{0,1},{1,0},{2,3},{3,2},{4,5},{5,4},{6,7},{7,6},{8,9},{9,8},{10,11... | collective-permute-start | bytes 602120 | tf_op jit(solution)/shard_map/ppermute | solution.py:19
  55.0 7.1 %collective-permute-start.24 = (bf16[112,896]{1,0:T(8,128)(2,1)S(1)}, bf16[112,896]{1,0:T(8,128)(2,1)S(1)}, u32[]{:S(2)}, u32[]{:S(2)}) collective-permute-start(bf16[112,896]{1,0:T(8,128)(2,1)S(1)} %get-tuple-element.29), channel_id=1, source_target_pairs={{0,2},{1,3},{2,0},{3,1},{4,6},{5,7},{6,4},{7,5},{8,10},{9,11},{10,... | collective-permute-start | bytes 602120 | tf_op jit(solution)/shard_map/ppermute | solution.py:19
  56.2 13.7 %collective-permute-start.26 = (bf16[112,896]{1,0:T(8,128)(2,1)S(1)}, bf16[112,896]{1,0:T(8,128)(2,1)S(1)}, u32[]{:S(2)}, u32[]{:S(2)}) collective-permute-start(bf16[112,896]{1,0:T(8,128)(2,1)S(1)} %get-tuple-element.30), channel_id=1, source_target_pairs={{0,6},{1,7},{2,4},{3,5},{4,2},{5,3},{6,0},{7,1},{8,14},{9,15},{10,... | collective-permute-start | bytes 602120 | tf_op jit(solution)/shard_map/ppermute | solution.py:19
  59.8 18.4 %collective-permute-start.25 = (bf16[112,896]{1,0:T(8,128)(2,1)S(1)}, bf16[112,896]{1,0:T(8,128)(2,1)S(1)}, u32[]{:S(2)}, u32[]{:S(2)}) collective-permute-start(bf16[112,896]{1,0:T(8,128)(2,1)S(1)} %get-tuple-element.31), channel_id=1, source_target_pairs={{0,4},{1,5},{2,6},{3,7},{4,0},{5,1},{6,2},{7,3},{8,12},{9,13},{10,... | collective-permute-start | bytes 602120 | tf_op jit(solution)/shard_map/ppermute | solution.py:19
  78.4 7.1 %collective-permute-start.34 = (bf16[1,112,896]{2,1,0:T(8,128)(2,1)S(1)}, bf16[1,112,896]{2,1,0:T(8,128)(2,1)S(1)}, u32[]{:S(2)}, u32[]{:S(2)}) collective-permute-start(bf16[1,112,896]{2,1,0:T(8,128)(2,1)S(1)} %get-tuple-element.23.refs_0_), channel_id=1, source_target_pairs={{0,8},{8,0},{16,24},{24,16},{1,9},{9,1},{17,25},{25,17},{2,10},{10... | collective-permute-start | bytes 602120 | tf_op jit(solution)/shard_map/ppermute | solution.py:23
  81.0 11.1 %collective-permute-start.30 = (bf16[1,112,896]{2,1,0:T(8,128)(2,1)S(1)}, bf16[1,112,896]{2,1,0:T(8,128)(2,1)S(1)}, u32[]{:S(2)}, u32[]{:S(2)}) collective-permute-start(bf16[1,112,896]{2,1,0:T(8,128)(2,1)S(1)} %get-tuple-element.23.refs_0_), channel_id=1, source_target_pairs={{0,4},{1,5},{2,6},{3,7},{4,0},{5,1},{6,2},{7,3},{8,12},{9,13},{10,... | collective-permute-start | bytes 602120 | tf_op jit(solution)/shard_map/ppermute | solution.py:19
  81.1 11.5 %collective-permute-start.27 = (bf16[1,112,896]{2,1,0:T(8,128)(2,1)S(1)}, bf16[1,112,896]{2,1,0:T(8,128)(2,1)S(1)}, u32[]{:S(2)}, u32[]{:S(2)}) collective-permute-start(bf16[1,112,896]{2,1,0:T(8,128)(2,1)S(1)} %get-tuple-element.23.refs_0_), channel_id=1, source_target_pairs={{0,2},{1,3},{2,0},{3,1},{4,6},{5,7},{6,4},{7,5},{8,10},{9,11},{10,... | collective-permute-start | bytes 602120 | tf_op jit(solution)/shard_map/ppermute | solution.py:19
  84.3 8.4 %collective-permute-start.28 = (bf16[1,112,896]{2,1,0:T(8,128)(2,1)S(1)}, bf16[1,112,896]{2,1,0:T(8,128)(2,1)S(1)}, u32[]{:S(2)}, u32[]{:S(2)}) collective-permute-start(bf16[1,112,896]{2,1,0:T(8,128)(2,1)S(1)} %get-tuple-element.23.refs_0_), channel_id=1, source_target_pairs={{0,1},{1,0},{2,3},{3,2},{4,5},{5,4},{6,7},{7,6},{8,9},{9,8},{10,11... | collective-permute-start | bytes 602120 | tf_op jit(solution)/shard_map/ppermute | solution.py:19
  85.5 7.2 %collective-permute-start.42 = (bf16[1,112,896]{2,1,0:T(8,128)(2,1)S(1)}, bf16[1,112,896]{2,1,0:T(8,128)(2,1)S(1)}, u32[]{:S(2)}, u32[]{:S(2)}) collective-permute-start(bf16[1,112,896]{2,1,0:T(8,128)(2,1)S(1)} %collective-permute-done.34.refs_8_), channel_id=1, source_target_pairs={{0,16},{24,8},{1,17},{25,9},{2,18},{26,10},{3,19},{27,11},{4,20},{... | collective-permute-start | bytes 602120 | tf_op jit(solution)/shard_map/ppermute | solution.py:29
  89.1 5.8 %collective-permute-start.35 = (bf16[1,112,896]{2,1,0:T(8,128)(2,1)S(1)}, bf16[1,112,896]{2,1,0:T(8,128)(2,1)S(1)}, u32[]{:S(2)}, u32[]{:S(2)}) collective-permute-start(bf16[1,112,896]{2,1,0:T(8,128)(2,1)S(1)} %collective-permute-done.34.refs_8_), channel_id=1, source_target_pairs={{0,1},{1,0},{2,3},{3,2},{4,5},{5,4},{6,7},{7,6},{8,9},{9,8},{10,11... | collective-permute-start | bytes 602120 | tf_op jit(solution)/shard_map/ppermute | solution.py:19
  92.2 7.9 %collective-permute-start.38 = (bf16[1,112,896]{2,1,0:T(8,128)(2,1)S(1)}, bf16[1,112,896]{2,1,0:T(8,128)(2,1)S(1)}, u32[]{:S(2)}, u32[]{:S(2)}) collective-permute-start(bf16[1,112,896]{2,1,0:T(8,128)(2,1)S(1)} %collective-permute-done.30.refs_4_), channel_id=1, source_target_pairs={{0,8},{8,0},{16,24},{24,16},{1,9},{9,1},{17,25},{25,17},{2,10},{10... | collective-permute-start | bytes 602120 | tf_op jit(solution)/shard_map/ppermute | solution.py:23
  92.5 7.5 %collective-permute-start.32 = (bf16[1,112,896]{2,1,0:T(8,128)(2,1)S(1)}, bf16[1,112,896]{2,1,0:T(8,128)(2,1)S(1)}, u32[]{:S(2)}, u32[]{:S(2)}) collective-permute-start(bf16[1,112,896]{2,1,0:T(8,128)(2,1)S(1)} %collective-permute-done.30.refs_4_), channel_id=1, source_target_pairs={{0,2},{1,3},{2,0},{3,1},{4,6},{5,7},{6,4},{7,5},{8,10},{9,11},{10,... | collective-permute-start | bytes 602120 | tf_op jit(solution)/shard_map/ppermute | solution.py:19
  92.6 8.1 %collective-permute-start.31 = (bf16[1,112,896]{2,1,0:T(8,128)(2,1)S(1)}, bf16[1,112,896]{2,1,0:T(8,128)(2,1)S(1)}, u32[]{:S(2)}, u32[]{:S(2)}) collective-permute-start(bf16[1,112,896]{2,1,0:T(8,128)(2,1)S(1)} %collective-permute-done.30.refs_4_), channel_id=1, source_target_pairs={{0,1},{1,0},{2,3},{3,2},{4,5},{5,4},{6,7},{7,6},{8,9},{9,8},{10,11... | collective-permute-start | bytes 602120 | tf_op jit(solution)/shard_map/ppermute | solution.py:19
  92.7 11.1 %collective-permute-start.36 = (bf16[1,112,896]{2,1,0:T(8,128)(2,1)S(1)}, bf16[1,112,896]{2,1,0:T(8,128)(2,1)S(1)}, u32[]{:S(2)}, u32[]{:S(2)}) collective-permute-start(bf16[1,112,896]{2,1,0:T(8,128)(2,1)S(1)} %collective-permute-done.27.refs_2_), channel_id=1, source_target_pairs={{0,8},{8,0},{16,24},{24,16},{1,9},{9,1},{17,25},{25,17},{2,10},{10... | collective-permute-start | bytes 602120 | tf_op jit(solution)/shard_map/ppermute | solution.py:23
  94.9 9.1 %collective-permute-start.29 = (bf16[1,112,896]{2,1,0:T(8,128)(2,1)S(1)}, bf16[1,112,896]{2,1,0:T(8,128)(2,1)S(1)}, u32[]{:S(2)}, u32[]{:S(2)}) collective-permute-start(bf16[1,112,896]{2,1,0:T(8,128)(2,1)S(1)} %collective-permute-done.27.refs_2_), channel_id=1, source_target_pairs={{0,1},{1,0},{2,3},{3,2},{4,5},{5,4},{6,7},{7,6},{8,9},{9,8},{10,11... | collective-permute-start | bytes 602120 | tf_op jit(solution)/shard_map/ppermute | solution.py:19
  100.0 7.6 %collective-permute-start.40 = (bf16[1,112,896]{2,1,0:T(8,128)(2,1)S(1)}, bf16[1,112,896]{2,1,0:T(8,128)(2,1)S(1)}, u32[]{:S(2)}, u32[]{:S(2)}) collective-permute-start(bf16[1,112,896]{2,1,0:T(8,128)(2,1)S(1)} %collective-permute-done.32.refs_6_), channel_id=1, source_target_pairs={{0,8},{8,0},{16,24},{24,16},{1,9},{9,1},{17,25},{25,17},{2,10},{10... | collective-permute-start | bytes 602120 | tf_op jit(solution)/shard_map/ppermute | solution.py:23
  100.8 9.0 %collective-permute-start.46 = (bf16[1,112,896]{2,1,0:T(8,128)(2,1)S(1)}, bf16[1,112,896]{2,1,0:T(8,128)(2,1)S(1)}, u32[]{:S(2)}, u32[]{:S(2)}) collective-permute-start(bf16[1,112,896]{2,1,0:T(8,128)(2,1)S(1)} %collective-permute-done.38.refs_12_), channel_id=1, source_target_pairs={{0,16},{24,8},{1,17},{25,9},{2,18},{26,10},{3,19},{27,11},{4,20},{... | collective-permute-start | bytes 602120 | tf_op jit(solution)/shard_map/ppermute | solution.py:29
  103.9 6.0 %collective-permute-start.39 = (bf16[1,112,896]{2,1,0:T(8,128)(2,1)S(1)}, bf16[1,112,896]{2,1,0:T(8,128)(2,1)S(1)}, u32[]{:S(2)}, u32[]{:S(2)}) collective-permute-start(bf16[1,112,896]{2,1,0:T(8,128)(2,1)S(1)} %collective-permute-done.38.refs_12_), channel_id=1, source_target_pairs={{0,1},{1,0},{2,3},{3,2},{4,5},{5,4},{6,7},{7,6},{8,9},{9,8},{10,11... | collective-permute-start | bytes 602120 | tf_op jit(solution)/shard_map/ppermute | solution.py:19
  103.9 6.4 %collective-permute-start.33 = (bf16[1,112,896]{2,1,0:T(8,128)(2,1)S(1)}, bf16[1,112,896]{2,1,0:T(8,128)(2,1)S(1)}, u32[]{:S(2)}, u32[]{:S(2)}) collective-permute-start(bf16[1,112,896]{2,1,0:T(8,128)(2,1)S(1)} %collective-permute-done.32.refs_6_), channel_id=1, source_target_pairs={{0,1},{1,0},{2,3},{3,2},{4,5},{5,4},{6,7},{7,6},{8,9},{9,8},{10,11... | collective-permute-start | bytes 602120 | tf_op jit(solution)/shard_map/ppermute | solution.py:19
  104.4 9.0 %collective-permute-start.44 = (bf16[1,112,896]{2,1,0:T(8,128)(2,1)S(1)}, bf16[1,112,896]{2,1,0:T(8,128)(2,1)S(1)}, u32[]{:S(2)}, u32[]{:S(2)}) collective-permute-start(bf16[1,112,896]{2,1,0:T(8,128)(2,1)S(1)} %collective-permute-done.36.refs_10_), channel_id=1, source_target_pairs={{0,16},{24,8},{1,17},{25,9},{2,18},{26,10},{3,19},{27,11},{4,20},{... | collective-permute-start | bytes 602120 | tf_op jit(solution)/shard_map/ppermute | solution.py:29
  107.6 9.4 %collective-permute-start.48 = (bf16[1,112,896]{2,1,0:T(8,128)(2,1)S(1)}, bf16[1,112,896]{2,1,0:T(8,128)(2,1)S(1)}, u32[]{:S(2)}, u32[]{:S(2)}) collective-permute-start(bf16[1,112,896]{2,1,0:T(8,128)(2,1)S(1)} %collective-permute-done.40.refs_14_), channel_id=1, source_target_pairs={{0,16},{24,8},{1,17},{25,9},{2,18},{26,10},{3,19},{27,11},{4,20},{... | collective-permute-start | bytes 602120 | tf_op jit(solution)/shard_map/ppermute | solution.py:29
  109.8 7.3 %collective-permute-start.37 = (bf16[1,112,896]{2,1,0:T(8,128)(2,1)S(1)}, bf16[1,112,896]{2,1,0:T(8,128)(2,1)S(1)}, u32[]{:S(2)}, u32[]{:S(2)}) collective-permute-start(bf16[1,112,896]{2,1,0:T(8,128)(2,1)S(1)} %collective-permute-done.36.refs_10_), channel_id=1, source_target_pairs={{0,1},{1,0},{2,3},{3,2},{4,5},{5,4},{6,7},{7,6},{8,9},{9,8},{10,11... | collective-permute-start | bytes 602120 | tf_op jit(solution)/shard_map/ppermute | solution.py:19
  109.9 7.2 %collective-permute-start.41 = (bf16[1,112,896]{2,1,0:T(8,128)(2,1)S(1)}, bf16[1,112,896]{2,1,0:T(8,128)(2,1)S(1)}, u32[]{:S(2)}, u32[]{:S(2)}) collective-permute-start(bf16[1,112,896]{2,1,0:T(8,128)(2,1)S(1)} %collective-permute-done.40.refs_14_), channel_id=1, source_target_pairs={{0,1},{1,0},{2,3},{3,2},{4,5},{5,4},{6,7},{7,6},{8,9},{9,8},{10,11... | collective-permute-start | bytes 602120 | tf_op jit(solution)/shard_map/ppermute | solution.py:19
  110.3 6.7 %collective-permute-start.47 = (bf16[1,112,896]{2,1,0:T(8,128)(2,1)S(1)}, bf16[1,112,896]{2,1,0:T(8,128)(2,1)S(1)}, u32[]{:S(2)}, u32[]{:S(2)}) collective-permute-start(bf16[1,112,896]{2,1,0:T(8,128)(2,1)S(1)} %collective-permute-done.46.refs_20_), channel_id=1, source_target_pairs={{0,1},{1,0},{2,3},{3,2},{4,5},{5,4},{6,7},{7,6},{8,9},{9,8},{10,11... | collective-permute-start | bytes 602120 | tf_op jit(solution)/shard_map/ppermute | solution.py:19
  130.7 9.8 %collective-permute-start.53 = (bf16[112,896]{1,0:T(8,128)(2,1)S(1)}, bf16[112,896]{1,0:T(8,128)(2,1)S(1)}, u32[]{:S(2)}, u32[]{:S(2)}) collective-permute-start(bf16[112,896]{1,0:T(8,128)(2,1)S(1)} %get-tuple-element.25), channel_id=1, source_target_pairs={{0,6},{1,7},{2,4},{3,5},{4,2},{5,3},{6,0},{7,1},{8,14},{9,15},{10,... | collective-permute-start | bytes 602120 | tf_op jit(solution)/shard_map/ppermute | solution.py:19
  132.2 16.2 %collective-permute-start.52 = (bf16[112,896]{1,0:T(8,128)(2,1)S(1)}, bf16[112,896]{1,0:T(8,128)(2,1)S(1)}, u32[]{:S(2)}, u32[]{:S(2)}) collective-permute-start(bf16[112,896]{1,0:T(8,128)(2,1)S(1)} %get-tuple-element.26), channel_id=1, source_target_pairs={{0,4},{1,5},{2,6},{3,7},{4,0},{5,1},{6,2},{7,3},{8,12},{9,13},{10,... | collective-permute-start | bytes 602120 | tf_op jit(solution)/shard_map/ppermute | solution.py:19
  132.2 16.2 %collective-permute-start.51 = (bf16[112,896]{1,0:T(8,128)(2,1)S(1)}, bf16[112,896]{1,0:T(8,128)(2,1)S(1)}, u32[]{:S(2)}, u32[]{:S(2)}) collective-permute-start(bf16[112,896]{1,0:T(8,128)(2,1)S(1)} %get-tuple-element.27), channel_id=1, source_target_pairs={{0,2},{1,3},{2,0},{3,1},{4,6},{5,7},{6,4},{7,5},{8,10},{9,11},{10,... | collective-permute-start | bytes 602120 | tf_op jit(solution)/shard_map/ppermute | solution.py:19
  153.5 4.5 %collective-permute-start.56 = (f32[8,128]{1,0:T(8,128)S(1)}, f32[8,128]{1,0:T(8,128)S(1)}, u32[]{:S(2)}, u32[]{:S(2)}) collective-permute-start(f32[8,128]{1,0:T(8,128)S(1)} %add.92), channel_id=1, source_target_pairs={{0,4},{1,5},{2,6},{3,7},{4,0},{5,1},{6,2},{7,3},{8,12},{9,13},{10,... | collective-permute-start | bytes 12296 | tf_op jit(solution)/shard_map/ppermute | solution.py:19
  (11 other events, 31.7 us)

commit v3 on v2

--- a/solution.py
+++ b/solution.py
@@ -29,20 +29,35 @@
     return lax.ppermute(x, "sec", pairs)
 
 
+def across_pairs(x, count):
+    pairs = [(i, i + 1) for i in range(1, count - 1, 2)]
+    return lax.ppermute(x, "sec", pairs + [(j, i) for i, j in pairs])
+
+
+def after(x, *others):
+    return lax.optimization_barrier((x,) + others)[0]
+
+
 def gather_pieces(shard, beside, sec_count, term_count):
     chips = term_count // 2
+
+    def hop(x, bit):
+        return along_term(x, lambda t: t ^ (2 * bit), term_count)
+
     own = {0: shard}
-    order = sorted(range(1, chips), key=lambda i: (bin(i).count("1"), i))
-    for i in order:
-        bit = i & -i
-        own[i] = along_term(own[i ^ bit], lambda t, b=bit: t ^ (2 * b), term_count)
-    pair, beyond = {}, {}
-    held, beside = lax.optimization_barrier((own[1], beside))
-    own[1] = held
-    for i in range(chips):
-        pair[i] = pair_exchange(own[i], sec_count)
-    for i in range(chips):
-        beyond[i] = pair_forward(pair[i], sec_count)
+    for i in sorted(range(1, chips), key=lambda i: (bin(i).count("1"), i)):
+        own[i] = hop(own[i ^ (i & -i)], i & -i)
+    own[1], beside = lax.optimization_barrier((own[1], beside))
+    last = chips - 1
+    pair = {i: pair_exchange(own[i], sec_count) for i in range(last)}
+    pair[last] = hop(pair[last ^ 1], 1)
+    beyond = {}
+    for i in range(last):
+        if i >= chips // 2:
+            beyond[i] = pair_forward(pair[i], sec_count)
+        else:
+            beyond[i] = across_pairs(after(own[i], own[last]) if i else own[i], sec_count)
+    beyond[last] = hop(beyond[last ^ 1], 1)
     pieces = []
     for table in (own, pair, beyond):
         for i in range(chips):
@@ -137,16 +152,8 @@
     return totals[0], parts
 
 
-def all_sum(tile, sec_count, term_count):
-    bit = 1
-    while bit < term_count:
-        tile = tile + along_term(tile, lambda t, b=bit: t ^ b, term_count)
-        bit *= 2
-    bit = 1
-    while bit < sec_count:
-        tile = tile + lax.ppermute(tile, "sec", [(i, i ^ bit) for i in range(sec_count)])
-        bit *= 2
-    return tile
+def everyones(tile, count):
+    return lax.all_to_all(jnp.broadcast_to(tile, (count,) + tile.shape), ("sec", "term"), 0, 0)
 
 
 def lane_sums(tile, products):
@@ -155,8 +162,15 @@
         tile[k : k + 1, :] = sum(line[:, j : j + 128] for j in range(0, line.shape[1], 128))
 
 
-def first_gram_kernel(x_ref, y_ref, tile):
-    x, y = x_ref[0].astype(jnp.float32), y_ref[...]
+def image_kernel(x_ref, own, *refs):
+    y_ref, shard, tile = refs[-3:]
+    y = own[...]
+    for part in refs[:-3]:
+        y = y + part[...].astype(jnp.float32)
+    y = y * SCALE
+    y_ref[...] = y
+    shard[0] = y.astype(jnp.bfloat16)
+    x = x_ref[0].astype(jnp.float32)
     tile[...] = jnp.zeros_like(tile)
     lane_sums(tile, {0: (x, x), 1: (x, y), 2: (y, y)})
 
@@ -172,8 +186,8 @@
     lane_sums(tile, {3: (x, h), 4: (y, h), 5: (h, h)})
 
 
-def finish_kernel(tile, x_ref, y_ref, h_ref, vector, alphas, betas):
-    sums = jnp.sum(tile[...], axis=1, keepdims=True)
+def finish_kernel(tiles, x_ref, y_ref, h_ref, vector, alphas, betas):
+    sums = jnp.sum(jnp.sum(tiles[...], axis=0), axis=1, keepdims=True)
     xx, xy, yy, xh, yh, hh = (sums[k : k + 1, :] for k in range(6))
     cx = 1.0 / jnp.sqrt(xx + EPS)
     cy = cx / SCALE
@@ -226,13 +240,15 @@
     pieces, scal = gather_pieces(start, scal, sec_count, term_count)
     mine, theirs = apply_terms(scal, left_env, right_env, pieces, rows)
     own, got = reduce_parts(mine, theirs, term_count)
-    y = (own + sum(part.astype(jnp.float32) for part in got)) * SCALE
-    sums = pl.pallas_call(
-        first_gram_kernel, out_shape=tile, in_specs=[vmem] * 2, out_specs=vmem,
-        compiler_params=small, name="first_gram",
-    )(start, y)
-    shard = y.astype(jnp.bfloat16)[None]
-    pieces, sums = gather_pieces(shard, sums, sec_count, term_count)
+    y, shard, sums = pl.pallas_call(
+        image_kernel,
+        out_shape=(block, jax.ShapeDtypeStruct((1, rows, width), jnp.bfloat16), tile),
+        in_specs=[vmem] * (2 + len(got)),
+        out_specs=(vmem,) * 3,
+        compiler_params=small,
+        name="image",
+    )(start, own, *got)
+    pieces, _ = gather_pieces(shard, (), sec_count, term_count)
     mine, theirs = apply_terms(scal, left_env, right_env, pieces, rows)
     own, got = reduce_parts(mine, theirs, term_count)
     h, sums = pl.pallas_call(
@@ -243,7 +259,7 @@
         compiler_params=small,
         name="gram",
     )(sums, start, y, own, *got)
-    sums = all_sum(sums, sec_count, term_count)
+    sums = everyones(sums, sec_count * term_count)
     vector, alphas, betas = pl.pallas_call(
         finish_kernel,
         out_shape=(jax.ShapeDtypeStruct((1, rows, width), jnp.float32), pair, pair),

time: 167 us -> 162 us (0.970)
  blocking collectives: 0 us -> 14.8 us
  starting transfers between devices: 63.1 us -> 52.4 us
  waiting for transfers between devices: 77.8 us -> 68.1 us
    ppermute x8 -> x2, starting transfers between devices: 23.9 us -> 5.67 us  [pair_forward(): return lax.ppermute(x, 'sec', pairs)]
    all_to_all x0 -> x1, blocking collectives: none -> 14.8 us  [everyones(): lax.all_to_all(jnp.broadcast_to(tile, (count,) + tile.shape), ('sec', 'te...]
    ppermute x8 -> x2, waiting for transfers between devices: 11.3 us -> 4.55 us  [pair_forward(): return lax.ppermute(x, 'sec', pairs)]
    ppermute x8 -> x6, starting transfers between devices: 11.9 us -> 18.4 us  [pair_exchange(): lax.ppermute(x, 'sec', [(i, i ^ 1) for i in range(count) if i ^ 1 < count])]
    ppermute x2 -> x4, waiting for transfers between devices: 3.29 us -> 0.01 us  [across_pairs(): return lax.ppermute(x, 'sec', pairs + [(j, i) for i, j in pairs])]
    ppermute x41 -> x42, starting transfers between devices: 22.8 us -> 25.7 us  [along_term(): return lax.ppermute(x, 'term', [(i, partner(i)) for i in range(count)])]
    ppermute x2 -> x4, starting transfers between devices: 4.51 us -> 2.66 us  [across_pairs(): return lax.ppermute(x, 'sec', pairs + [(j, i) for i, j in pairs])]
    ppermute x41 -> x42, waiting for transfers between devices: 52.9 us -> 54.5 us  [along_term(): return lax.ppermute(x, 'term', [(i, partner(i)) for i in range(count)])]
  transfers between devices with their start and end apart: 59 -> 54, of which waited for: 26 -> 21; matrix products, arithmetic and copies ran while one was open for 1% -> 1% of each run, Pallas kernels for 0% -> 0%
where the time goes in v3:
time: 162 us; the launch traced here: 161 us
  waiting for transfers between devices  68.1 us (42%)
  starting transfers between devices  52.4 us (32%)
  Pallas kernels  20.9 us (13%)
  blocking collectives  14.8 us (9%)
  between operations  2.34 us (1%)
  other arithmetic  2 us (1%)
    ppermute x42, waiting for transfers between devices, along_term(): return lax.ppermute(x, 'term', [(i, partner(i)) for i in range(count)])  54.5 us
    ppermute x42, starting transfers between devices, along_term(): return lax.ppermute(x, 'term', [(i, partner(i)) for i in range(count)])  25.7 us
    pallas_call x2, Pallas kernels, apply_terms(): pl.pallas_call(functools.partial(apply_kernel, chips, terms, rows), out_s...  19.3 us
    ppermute x6, starting transfers between devices, pair_exchange(): lax.ppermute(x, 'sec', [(i, i ^ 1) for i in range(count) if i ^ 1 < count])  18.4 us
    all_to_all x1, blocking collectives, everyones(): lax.all_to_all(jnp.broadcast_to(tile, (count,) + tile.shape), ('sec', 'te...  14.8 us
    ppermute x6, waiting for transfers between devices, pair_exchange(): lax.ppermute(x, 'sec', [(i, i ^ 1) for i in range(count) if i ^ 1 < count])  9.03 us
    ppermute x2, starting transfers between devices, pair_forward(): return lax.ppermute(x, 'sec', pairs)  5.67 us
    ppermute x2, waiting for transfers between devices, pair_forward(): return lax.ppermute(x, 'sec', pairs)  4.55 us
  transfers between devices with their start and end apart: 54, of which 21 were waited for; matrix products, arithmetic and copies ran while one was open for 1% of the time, Pallas kernels for 0%

profile of v3, /device:TPU:0, one launch (start us, length us, event | category | flops | bytes accessed | tf_op | source)
XLA Modules:
  0.0 161.3 jit_solution(1040913750784540521)
XLA Ops:
  2.0 1.1 and_select_fusion.refs_0_.x_ref
  3.0 4.1 %collective-permute-start.3 = (bf16[1,112,896]{2,1,0:T(8,128)(2,1)S(1)}, bf16[1,112,896]{2,1,0:T(8,128)(2,1)S(1)}, u32[]{:S(2)}, u32[]{:S(2)}) collective-permute-start(bf16[1,112,896]{2,1,0:T(8,128)(2,1)S(1)} %and_select_fusion.refs_0_.x_ref), channel_id=1, source_target_pairs={{0,4},{1,5},{2,6},{3,7},{4,0},{5,1},{6,2},{7,3},{8,12},{9,13},{10,... | collective-permute-start | bytes 602120 | tf_op jit(solution)/shard_map/ppermute | solution.py:19
  7.1 0.7 collective-permute-start.15
  7.8 1.6 %collective-permute-start = (bf16[1,112,896]{2,1,0:T(8,128)(2,1)S(1)}, bf16[1,112,896]{2,1,0:T(8,128)(2,1)S(1)}, u32[]{:S(2)}, u32[]{:S(2)}) collective-permute-start(bf16[1,112,896]{2,1,0:T(8,128)(2,1)S(1)} %and_select_fusion.refs_0_.x_ref), channel_id=1, source_target_pairs={{0,2},{1,3},{2,0},{3,1},{4,6},{5,7},{6,4},{7,5},{8,10},{9,11},{10,... | collective-permute-start | bytes 602120 | tf_op jit(solution)/shard_map/ppermute | solution.py:19
  9.4 4.2 %collective-permute-start.7 = (bf16[1,112,896]{2,1,0:T(8,128)(2,1)S(1)}, bf16[1,112,896]{2,1,0:T(8,128)(2,1)S(1)}, u32[]{:S(2)}, u32[]{:S(2)}) collective-permute-start(bf16[1,112,896]{2,1,0:T(8,128)(2,1)S(1)} %and_select_fusion.refs_0_.x_ref), channel_id=1, source_target_pairs={{0,8},{8,0},{16,24},{24,16},{1,9},{9,1},{17,25},{25,17},{2,10},{10... | collective-permute-start | bytes 602120 | tf_op jit(solution)/shard_map/ppermute | solution.py:23
  13.7 2.9 %collective-permute-done.3.refs_4_ = bf16[1,112,896]{2,1,0:T(8,128)(2,1)S(1)} collective-permute-done((bf16[1,112,896]{2,1,0:T(8,128)(2,1)S(1)}, bf16[1,112,896]{2,1,0:T(8,128)(2,1)S(1)}, u32[]{:S(2)}, u32[]{:S(2)}) %collective-permute-start.3) | collective-permute-done | bytes 200736 | tf_op jit(solution)/shard_map/ppermute | solution.py:19
  16.5 1.5 collective-permute-start.11
  18.7 0.7 compare_select_fusion.1
  19.3 0.7 concatenate.3.scal
  20.1 2.1 %collective-permute-done.7.refs_8_ = bf16[1,112,896]{2,1,0:T(8,128)(2,1)S(1)} collective-permute-done((bf16[1,112,896]{2,1,0:T(8,128)(2,1)S(1)}, bf16[1,112,896]{2,1,0:T(8,128)(2,1)S(1)}, u32[]{:S(2)}, u32[]{:S(2)}) %collective-permute-start.7) | collective-permute-done | bytes 200736 | tf_op jit(solution)/shard_map/ppermute | solution.py:23
  22.7 1.6 %collective-permute-start.9 = (bf16[1,112,896]{2,1,0:T(8,128)(2,1)S(1)}, bf16[1,112,896]{2,1,0:T(8,128)(2,1)S(1)}, u32[]{:S(2)}, u32[]{:S(2)}) collective-permute-start(bf16[1,112,896]{2,1,0:T(8,128)(2,1)S(1)} %collective-permute-done.refs_2_), channel_id=1, source_target_pairs={{0,8},{8,0},{16,24},{24,16},{1,9},{9,1},{17,25},{25,17},{2,10},{10... | collective-permute-start | bytes 602120 | tf_op jit(solution)/shard_map/ppermute | solution.py:23
  24.3 0.7 collective-permute-done.11.refs_12_
  25.0 2.6 %collective-permute-start.19 = (bf16[1,112,896]{2,1,0:T(8,128)(2,1)S(1)}, bf16[1,112,896]{2,1,0:T(8,128)(2,1)S(1)}, u32[]{:S(2)}, u32[]{:S(2)}) collective-permute-start(bf16[1,112,896]{2,1,0:T(8,128)(2,1)S(1)} %collective-permute-done.11.refs_12_), channel_id=1, source_target_pairs={{0,16},{24,8},{1,17},{25,9},{2,18},{26,10},{3,19},{27,11},{4,20},{... | collective-permute-start | bytes 602120 | tf_op jit(solution)/shard_map/ppermute | solution.py:29
  27.6 1.2 collective-permute-start.13
  28.8 1.1 collective-permute-done.9.refs_10_
  29.9 0.7 collective-permute-start.17
  30.6 0.9 collective-permute-done.19.refs_20_
  31.5 1.6 collective-permute-start.21
  33.1 0.7 collective-permute-done.13.refs_14_
  34.8 3.3 %collective-permute-done.21.refs_22_ = bf16[1,112,896]{2,1,0:T(8,128)(2,1)S(1)} collective-permute-done((bf16[1,112,896]{2,1,0:T(8,128)(2,1)S(1)}, bf16[1,112,896]{2,1,0:T(8,128)(2,1)S(1)}, u32[]{:S(2)}, u32[]{:S(2)}) %collective-permute-start.21) | collective-permute-done | bytes 200736 | tf_op jit(solution)/shard_map/ppermute | solution.py:19
  38.1 1.4 collective-permute-done.22.refs_23_
  39.6 9.7 %apply_terms.2 = (f32[4,112,896]{2,1,0:T(8,128)S(1)}, bf16[4,112,896]{2,1,0:T(8,128)(2,1)S(1)}) custom-call(s32[8]{0:T(128)S(1)} %concatenate.3.scal, bf16[2,1,896,896]{3,2,1,0:T(8,128)(2,1)} %left.3, bf16[2,1,896,896]{3,2,1,0:T(8,128)(2,1)} %right.3, bf16[1,112,896]{2,1,0:T(8,128)(2,1)S(1)} %and_select_fusion.refs_0_.x_ref, ...), custom_call_target="tpu_custom_call" | custom-call | tf_op jit(solution)/shard_map/apply_terms/pallas_call | solution.py:124
  49.4 2.2 %collective-permute-done.23 = bf16[4,112,896]{2,1,0:T(8,128)(2,1)S(1)} collective-permute-done((bf16[4,112,896]{2,1,0:T(8,128)(2,1)S(1)}, bf16[4,112,896]{2,1,0:T(8,128)(2,1)S(1)}, u32[]{:S(2)}, u32[]{:S(2)}) %collective-permute-start.23) | collective-permute-done | bytes 802848 | tf_op jit(solution)/shard_map/ppermute | solution.py:19
  51.8 3.8 %collective-permute-start.26 = (bf16[112,896]{1,0:T(8,128)(2,1)S(1)}, bf16[112,896]{1,0:T(8,128)(2,1)S(1)}, u32[]{:S(2)}, u32[]{:S(2)}) collective-permute-start(bf16[112,896]{1,0:T(8,128)(2,1)S(1)} %get-tuple-element.33), channel_id=1, source_target_pairs={{0,6},{1,7},{2,4},{3,5},{4,2},{5,3},{6,0},{7,1},{8,14},{9,15},{10,... | collective-permute-start | bytes 602120 | tf_op jit(solution)/shard_map/ppermute | solution.py:19
  55.6 0.7 collective-permute-start.24
  56.2 5.4 %collective-permute-done.26.refs_2_ = bf16[112,896]{1,0:T(8,128)(2,1)S(1)} collective-permute-done((bf16[112,896]{1,0:T(8,128)(2,1)S(1)}, bf16[112,896]{1,0:T(8,128)(2,1)S(1)}, u32[]{:S(2)}, u32[]{:S(2)}) %collective-permute-start.26) | collective-permute-done | bytes 200736 | tf_op jit(solution)/shard_map/ppermute | solution.py:19
  61.6 11.2 %collective-permute-done.25.refs_1_ = bf16[112,896]{1,0:T(8,128)(2,1)S(1)} collective-permute-done((bf16[112,896]{1,0:T(8,128)(2,1)S(1)}, bf16[112,896]{1,0:T(8,128)(2,1)S(1)}, u32[]{:S(2)}, u32[]{:S(2)}) %collective-permute-start.25) | collective-permute-done | bytes 200736 | tf_op jit(solution)/shard_map/ppermute | solution.py:19
  73.0 0.7 collective-permute-start.42
  73.8 5.6 %collective-permute-start.34 = (bf16[1,112,896]{2,1,0:T(8,128)(2,1)S(1)}, bf16[1,112,896]{2,1,0:T(8,128)(2,1)S(1)}, u32[]{:S(2)}, u32[]{:S(2)}) collective-permute-start(bf16[1,112,896]{2,1,0:T(8,128)(2,1)S(1)} %get-tuple-element.23.refs_0_), channel_id=1, source_target_pairs={{0,8},{8,0},{16,24},{24,16},{1,9},{9,1},{17,25},{25,17},{2,10},{10... | collective-permute-start | bytes 602120 | tf_op jit(solution)/shard_map/ppermute | solution.py:23
  79.4 2.9 %collective-permute-start.28 = (bf16[1,112,896]{2,1,0:T(8,128)(2,1)S(1)}, bf16[1,112,896]{2,1,0:T(8,128)(2,1)S(1)}, u32[]{:S(2)}, u32[]{:S(2)}) collective-permute-start(bf16[1,112,896]{2,1,0:T(8,128)(2,1)S(1)} %get-tuple-element.23.refs_0_), channel_id=1, source_target_pairs={{0,2},{1,3},{2,0},{3,1},{4,6},{5,7},{6,4},{7,5},{8,10},{9,11},{10,... | collective-permute-start | bytes 602120 | tf_op jit(solution)/shard_map/ppermute | solution.py:19
  82.7 2.3 %collective-permute-done.30.refs_4_ = bf16[1,112,896]{2,1,0:T(8,128)(2,1)S(1)} collective-permute-done((bf16[1,112,896]{2,1,0:T(8,128)(2,1)S(1)}, bf16[1,112,896]{2,1,0:T(8,128)(2,1)S(1)}, u32[]{:S(2)}, u32[]{:S(2)}) %collective-permute-start.30) | collective-permute-done | bytes 200736 | tf_op jit(solution)/shard_map/ppermute | solution.py:19
  85.0 5.3 %collective-permute-start.38 = (bf16[1,112,896]{2,1,0:T(8,128)(2,1)S(1)}, bf16[1,112,896]{2,1,0:T(8,128)(2,1)S(1)}, u32[]{:S(2)}, u32[]{:S(2)}) collective-permute-start(bf16[1,112,896]{2,1,0:T(8,128)(2,1)S(1)} %collective-permute-done.30.refs_4_), channel_id=1, source_target_pairs={{0,8},{8,0},{16,24},{24,16},{1,9},{9,1},{17,25},{25,17},{2,10},{10... | collective-permute-start | bytes 602120 | tf_op jit(solution)/shard_map/ppermute | solution.py:23
  91.0 5.1 %collective-permute-done.38.refs_12_ = bf16[1,112,896]{2,1,0:T(8,128)(2,1)S(1)} collective-permute-done((bf16[1,112,896]{2,1,0:T(8,128)(2,1)S(1)}, bf16[1,112,896]{2,1,0:T(8,128)(2,1)S(1)}, u32[]{:S(2)}, u32[]{:S(2)}) %collective-permute-start.38) | collective-permute-done | bytes 200736 | tf_op jit(solution)/shard_map/ppermute | solution.py:23
  96.2 0.8 collective-permute-done.32.refs_6_
  96.9 3.1 %collective-permute-start.46 = (bf16[1,112,896]{2,1,0:T(8,128)(2,1)S(1)}, bf16[1,112,896]{2,1,0:T(8,128)(2,1)S(1)}, u32[]{:S(2)}, u32[]{:S(2)}) collective-permute-start(bf16[1,112,896]{2,1,0:T(8,128)(2,1)S(1)} %collective-permute-done.38.refs_12_), channel_id=1, source_target_pairs={{0,16},{24,8},{1,17},{25,9},{2,18},{26,10},{3,19},{27,11},{4,20},{... | collective-permute-start | bytes 602120 | tf_op jit(solution)/shard_map/ppermute | solution.py:29
  100.7 0.7 collective-permute-start.44
  101.4 3.6 %collective-permute-done.46.refs_20_ = bf16[1,112,896]{2,1,0:T(8,128)(2,1)S(1)} collective-permute-done((bf16[1,112,896]{2,1,0:T(8,128)(2,1)S(1)}, bf16[1,112,896]{2,1,0:T(8,128)(2,1)S(1)}, u32[]{:S(2)}, u32[]{:S(2)}) %collective-permute-start.46) | collective-permute-done | bytes 200736 | tf_op jit(solution)/shard_map/ppermute | solution.py:29
  105.0 2.2 %collective-permute-done.40.refs_14_ = bf16[1,112,896]{2,1,0:T(8,128)(2,1)S(1)} collective-permute-done((bf16[1,112,896]{2,1,0:T(8,128)(2,1)S(1)}, bf16[1,112,896]{2,1,0:T(8,128)(2,1)S(1)}, u32[]{:S(2)}, u32[]{:S(2)}) %collective-permute-start.40) | collective-permute-done | bytes 200736 | tf_op jit(solution)/shard_map/ppermute | solution.py:19
  108.3 3.3 %collective-permute-done.48.refs_22_ = bf16[1,112,896]{2,1,0:T(8,128)(2,1)S(1)} collective-permute-done((bf16[1,112,896]{2,1,0:T(8,128)(2,1)S(1)}, bf16[1,112,896]{2,1,0:T(8,128)(2,1)S(1)}, u32[]{:S(2)}, u32[]{:S(2)}) %collective-permute-start.48) | collective-permute-done | bytes 200736 | tf_op jit(solution)/shard_map/ppermute | solution.py:19
  111.6 1.4 collective-permute-done.49.refs_23_
  113.0 9.7 %apply_terms.3 = (f32[4,112,896]{2,1,0:T(8,128)S(1)}, bf16[4,112,896]{2,1,0:T(8,128)(2,1)S(1)}) custom-call(s32[8]{0:T(128)S(1)} %concatenate.3.scal, bf16[2,1,896,896]{3,2,1,0:T(8,128)(2,1)} %left.3, bf16[2,1,896,896]{3,2,1,0:T(8,128)(2,1)} %right.3, bf16[1,112,896]{2,1,0:T(8,128)(2,1)S(1)} %get-tuple-element.23.refs_0_, ...), custom_call_target="tpu_custom_call" | custom-call | tf_op jit(solution)/shard_map/apply_terms/pallas_call | solution.py:124
  122.9 2.2 %collective-permute-done.50 = bf16[4,112,896]{2,1,0:T(8,128)(2,1)S(1)} collective-permute-done((bf16[4,112,896]{2,1,0:T(8,128)(2,1)S(1)}, bf16[4,112,896]{2,1,0:T(8,128)(2,1)S(1)}, u32[]{:S(2)}, u32[]{:S(2)}) %collective-permute-start.50) | collective-permute-done | bytes 802848 | tf_op jit(solution)/shard_map/ppermute | solution.py:19
  125.2 1.5 collective-permute-start.53
  127.0 2.6 %collective-permute-start.51 = (bf16[112,896]{1,0:T(8,128)(2,1)S(1)}, bf16[112,896]{1,0:T(8,128)(2,1)S(1)}, u32[]{:S(2)}, u32[]{:S(2)}) collective-permute-start(bf16[112,896]{1,0:T(8,128)(2,1)S(1)} %get-tuple-element.31), channel_id=1, source_target_pairs={{0,2},{1,3},{2,0},{3,1},{4,6},{5,7},{6,4},{7,5},{8,10},{9,11},{10,... | collective-permute-start | bytes 602120 | tf_op jit(solution)/shard_map/ppermute | solution.py:19
  129.7 5.4 %collective-permute-done.53.refs_2_ = bf16[112,896]{1,0:T(8,128)(2,1)S(1)} collective-permute-done((bf16[112,896]{1,0:T(8,128)(2,1)S(1)}, bf16[112,896]{1,0:T(8,128)(2,1)S(1)}, u32[]{:S(2)}, u32[]{:S(2)}) %collective-permute-start.53) | collective-permute-done | bytes 200736 | tf_op jit(solution)/shard_map/ppermute | solution.py:19
  135.1 9.9 %collective-permute-done.52.refs_1_ = bf16[112,896]{1,0:T(8,128)(2,1)S(1)} collective-permute-done((bf16[112,896]{1,0:T(8,128)(2,1)S(1)}, bf16[112,896]{1,0:T(8,128)(2,1)S(1)}, u32[]{:S(2)}, u32[]{:S(2)}) %collective-permute-start.52) | collective-permute-done | bytes 200736 | tf_op jit(solution)/shard_map/ppermute | solution.py:19
  145.2 14.8 %all_to_all.5.tiles = f32[32,8,128]{2,1,0:T(8,128)S(1)} all-to-all(f32[32,8,128]{2,1,0:T(8,128)S(1)} %broadcast_in_dim.19), channel_id=1, replica_groups=mesh['sec'=4,'term'=8] {'sec','term'}, dimensions={0} | all-to-all | bytes 262144 | tf_op jit(solution)/shard_map/all_to_all | solution.py:156
  160.0 1.1 finish.1
  (74 shorter events, 6.6 us)
Async XLA Ops:
  3.0 13.5 %collective-permute-start.3 = (bf16[1,112,896]{2,1,0:T(8,128)(2,1)S(1)}, bf16[1,112,896]{2,1,0:T(8,128)(2,1)S(1)}, u32[]{:S(2)}, u32[]{:S(2)}) collective-permute-start(bf16[1,112,896]{2,1,0:T(8,128)(2,1)S(1)} %and_select_fusion.refs_0_.x_ref), channel_id=1, source_target_pairs={{0,4},{1,5},{2,6},{3,7},{4,0},{5,1},{6,2},{7,3},{8,12},{9,13},{10,... | collective-permute-start | bytes 602120 | tf_op jit(solution)/shard_map/ppermute | solution.py:19
  7.1 10.9 %collective-permute-start.15 = (bf16[1,112,896]{2,1,0:T(8,128)(2,1)S(1)}, bf16[1,112,896]{2,1,0:T(8,128)(2,1)S(1)}, u32[]{:S(2)}, u32[]{:S(2)}) collective-permute-start(bf16[1,112,896]{2,1,0:T(8,128)(2,1)S(1)} %and_select_fusion.refs_0_.x_ref), channel_id=1, source_target_pairs={{8,16},{16,8},{9,17},{17,9},{10,18},{18,10},{11,19},{19,11},{12,20... | collective-permute-start | bytes 602120 | tf_op jit(solution)/shard_map/ppermute | solution.py:34
  7.8 10.9 %collective-permute-start = (bf16[1,112,896]{2,1,0:T(8,128)(2,1)S(1)}, bf16[1,112,896]{2,1,0:T(8,128)(2,1)S(1)}, u32[]{:S(2)}, u32[]{:S(2)}) collective-permute-start(bf16[1,112,896]{2,1,0:T(8,128)(2,1)S(1)} %and_select_fusion.refs_0_.x_ref), channel_id=1, source_target_pairs={{0,2},{1,3},{2,0},{3,1},{4,6},{5,7},{6,4},{7,5},{8,10},{9,11},{10,... | collective-permute-start | bytes 602120 | tf_op jit(solution)/shard_map/ppermute | solution.py:19
  9.4 12.7 %collective-permute-start.7 = (bf16[1,112,896]{2,1,0:T(8,128)(2,1)S(1)}, bf16[1,112,896]{2,1,0:T(8,128)(2,1)S(1)}, u32[]{:S(2)}, u32[]{:S(2)}) collective-permute-start(bf16[1,112,896]{2,1,0:T(8,128)(2,1)S(1)} %and_select_fusion.refs_0_.x_ref), channel_id=1, source_target_pairs={{0,8},{8,0},{16,24},{24,16},{1,9},{9,1},{17,25},{25,17},{2,10},{10... | collective-permute-start | bytes 602120 | tf_op jit(solution)/shard_map/ppermute | solution.py:23
  13.7 8.5 %collective-permute-start.1 = (bf16[1,112,896]{2,1,0:T(8,128)(2,1)S(1)}, bf16[1,112,896]{2,1,0:T(8,128)(2,1)S(1)}, u32[]{:S(2)}, u32[]{:S(2)}) collective-permute-start(bf16[1,112,896]{2,1,0:T(8,128)(2,1)S(1)} %and_select_fusion.refs_0_.x_ref), channel_id=1, source_target_pairs={{0,1},{1,0},{2,3},{3,2},{4,5},{5,4},{6,7},{7,6},{8,9},{9,8},{10,11... | collective-permute-start | bytes 602120 | tf_op jit(solution)/shard_map/ppermute | solution.py:19
  16.5 8.5 %collective-permute-start.11 = (bf16[1,112,896]{2,1,0:T(8,128)(2,1)S(1)}, bf16[1,112,896]{2,1,0:T(8,128)(2,1)S(1)}, u32[]{:S(2)}, u32[]{:S(2)}) collective-permute-start(bf16[1,112,896]{2,1,0:T(8,128)(2,1)S(1)} %collective-permute-done.3.refs_4_), channel_id=1, source_target_pairs={{0,8},{8,0},{16,24},{24,16},{1,9},{9,1},{17,25},{25,17},{2,10},{10... | collective-permute-start | bytes 602120 | tf_op jit(solution)/shard_map/ppermute | solution.py:23
  18.1 7.0 %collective-permute-start.5 = (bf16[1,112,896]{2,1,0:T(8,128)(2,1)S(1)}, bf16[1,112,896]{2,1,0:T(8,128)(2,1)S(1)}, u32[]{:S(2)}, u32[]{:S(2)}) collective-permute-start(bf16[1,112,896]{2,1,0:T(8,128)(2,1)S(1)} %collective-permute-done.3.refs_4_), channel_id=1, source_target_pairs={{0,2},{1,3},{2,0},{3,1},{4,6},{5,7},{6,4},{7,5},{8,10},{9,11},{10,... | collective-permute-start | bytes 602120 | tf_op jit(solution)/shard_map/ppermute | solution.py:19
  18.7 4.0 %collective-permute-start.16 = (bf16[1,112,896]{2,1,0:T(8,128)(2,1)S(1)}, bf16[1,112,896]{2,1,0:T(8,128)(2,1)S(1)}, u32[]{:S(2)}, u32[]{:S(2)}) collective-permute-start(bf16[1,112,896]{2,1,0:T(8,128)(2,1)S(1)} %collective-permute-done.15.refs_16_), channel_id=1, source_target_pairs={{0,1},{1,0},{2,3},{3,2},{4,5},{5,4},{6,7},{7,6},{8,9},{9,8},{10,11... | collective-permute-start | bytes 602120 | tf_op jit(solution)/shard_map/ppermute | solution.py:19
  22.2 5.4 %collective-permute-start.8 = (bf16[1,112,896]{2,1,0:T(8,128)(2,1)S(1)}, bf16[1,112,896]{2,1,0:T(8,128)(2,1)S(1)}, u32[]{:S(2)}, u32[]{:S(2)}) collective-permute-start(bf16[1,112,896]{2,1,0:T(8,128)(2,1)S(1)} %collective-permute-done.7.refs_8_), channel_id=1, source_target_pairs={{0,1},{1,0},{2,3},{3,2},{4,5},{5,4},{6,7},{7,6},{8,9},{9,8},{10,11... | collective-permute-start | bytes 602120 | tf_op jit(solution)/shard_map/ppermute | solution.py:19
  22.2 6.6 %collective-permute-start.4 = (bf16[1,112,896]{2,1,0:T(8,128)(2,1)S(1)}, bf16[1,112,896]{2,1,0:T(8,128)(2,1)S(1)}, u32[]{:S(2)}, u32[]{:S(2)}) collective-permute-start(bf16[1,112,896]{2,1,0:T(8,128)(2,1)S(1)} %collective-permute-done.3.refs_4_), channel_id=1, source_target_pairs={{0,1},{1,0},{2,3},{3,2},{4,5},{5,4},{6,7},{7,6},{8,9},{9,8},{10,11... | collective-permute-start | bytes 602120 | tf_op jit(solution)/shard_map/ppermute | solution.py:19
  22.7 7.2 %collective-permute-start.9 = (bf16[1,112,896]{2,1,0:T(8,128)(2,1)S(1)}, bf16[1,112,896]{2,1,0:T(8,128)(2,1)S(1)}, u32[]{:S(2)}, u32[]{:S(2)}) collective-permute-start(bf16[1,112,896]{2,1,0:T(8,128)(2,1)S(1)} %collective-permute-done.refs_2_), channel_id=1, source_target_pairs={{0,8},{8,0},{16,24},{24,16},{1,9},{9,1},{17,25},{25,17},{2,10},{10... | collective-permute-start | bytes 602120 | tf_op jit(solution)/shard_map/ppermute | solution.py:23
  25.0 4.9 %collective-permute-start.2 = (bf16[1,112,896]{2,1,0:T(8,128)(2,1)S(1)}, bf16[1,112,896]{2,1,0:T(8,128)(2,1)S(1)}, u32[]{:S(2)}, u32[]{:S(2)}) collective-permute-start(bf16[1,112,896]{2,1,0:T(8,128)(2,1)S(1)} %collective-permute-done.refs_2_), channel_id=1, source_target_pairs={{0,1},{1,0},{2,3},{3,2},{4,5},{5,4},{6,7},{7,6},{8,9},{9,8},{10,11... | collective-permute-start | bytes 602120 | tf_op jit(solution)/shard_map/ppermute | solution.py:19
  25.0 6.5 %collective-permute-start.19 = (bf16[1,112,896]{2,1,0:T(8,128)(2,1)S(1)}, bf16[1,112,896]{2,1,0:T(8,128)(2,1)S(1)}, u32[]{:S(2)}, u32[]{:S(2)}) collective-permute-start(bf16[1,112,896]{2,1,0:T(8,128)(2,1)S(1)} %collective-permute-done.11.refs_12_), channel_id=1, source_target_pairs={{0,16},{24,8},{1,17},{25,9},{2,18},{26,10},{3,19},{27,11},{4,20},{... | collective-permute-start | bytes 602120 | tf_op jit(solution)/shard_map/ppermute | solution.py:29
  27.6 6.2 %collective-permute-start.13 = (bf16[1,112,896]{2,1,0:T(8,128)(2,1)S(1)}, bf16[1,112,896]{2,1,0:T(8,128)(2,1)S(1)}, u32[]{:S(2)}, u32[]{:S(2)}) collective-permute-start(bf16[1,112,896]{2,1,0:T(8,128)(2,1)S(1)} %collective-permute-done.11.refs_12_), channel_id=1, source_target_pairs={{0,2},{1,3},{2,0},{3,1},{4,6},{5,7},{6,4},{7,5},{8,10},{9,11},{10,... | collective-permute-start | bytes 602120 | tf_op jit(solution)/shard_map/ppermute | solution.py:19
  28.8 5.0 %collective-permute-start.12 = (bf16[1,112,896]{2,1,0:T(8,128)(2,1)S(1)}, bf16[1,112,896]{2,1,0:T(8,128)(2,1)S(1)}, u32[]{:S(2)}, u32[]{:S(2)}) collective-permute-start(bf16[1,112,896]{2,1,0:T(8,128)(2,1)S(1)} %collective-permute-done.11.refs_12_), channel_id=1, source_target_pairs={{0,1},{1,0},{2,3},{3,2},{4,5},{5,4},{6,7},{7,6},{8,9},{9,8},{10,11... | collective-permute-start | bytes 602120 | tf_op jit(solution)/shard_map/ppermute | solution.py:19
  29.9 4.4 %collective-permute-start.6 = (bf16[1,112,896]{2,1,0:T(8,128)(2,1)S(1)}, bf16[1,112,896]{2,1,0:T(8,128)(2,1)S(1)}, u32[]{:S(2)}, u32[]{:S(2)}) collective-permute-start(bf16[1,112,896]{2,1,0:T(8,128)(2,1)S(1)} %collective-permute-done.5.refs_6_), channel_id=1, source_target_pairs={{0,1},{1,0},{2,3},{3,2},{4,5},{5,4},{6,7},{7,6},{8,9},{9,8},{10,11... | collective-permute-start | bytes 602120 | tf_op jit(solution)/shard_map/ppermute | solution.py:19
  29.9 4.5 %collective-permute-start.17 = (bf16[1,112,896]{2,1,0:T(8,128)(2,1)S(1)}, bf16[1,112,896]{2,1,0:T(8,128)(2,1)S(1)}, u32[]{:S(2)}, u32[]{:S(2)}) collective-permute-start(bf16[1,112,896]{2,1,0:T(8,128)(2,1)S(1)} %collective-permute-done.refs_2_), channel_id=1, source_target_pairs={{8,16},{16,8},{9,17},{17,9},{10,18},{18,10},{11,19},{19,11},{12,20... | collective-permute-start | bytes 602120 | tf_op jit(solution)/shard_map/ppermute | solution.py:34
  31.5 6.6 %collective-permute-start.21 = (bf16[1,112,896]{2,1,0:T(8,128)(2,1)S(1)}, bf16[1,112,896]{2,1,0:T(8,128)(2,1)S(1)}, u32[]{:S(2)}, u32[]{:S(2)}) collective-permute-start(bf16[1,112,896]{2,1,0:T(8,128)(2,1)S(1)} %collective-permute-done.19.refs_20_), channel_id=1, source_target_pairs={{0,2},{1,3},{2,0},{3,1},{4,6},{5,7},{6,4},{7,5},{8,10},{9,11},{10,... | collective-permute-start | bytes 602120 | tf_op jit(solution)/shard_map/ppermute | solution.py:19
  33.8 4.3 %collective-permute-start.10 = (bf16[1,112,896]{2,1,0:T(8,128)(2,1)S(1)}, bf16[1,112,896]{2,1,0:T(8,128)(2,1)S(1)}, u32[]{:S(2)}, u32[]{:S(2)}) collective-permute-start(bf16[1,112,896]{2,1,0:T(8,128)(2,1)S(1)} %collective-permute-done.9.refs_10_), channel_id=1, source_target_pairs={{0,1},{1,0},{2,3},{3,2},{4,5},{5,4},{6,7},{7,6},{8,9},{9,8},{10,11... | collective-permute-start | bytes 602120 | tf_op jit(solution)/shard_map/ppermute | solution.py:19
  33.8 4.3 %collective-permute-start.20 = (bf16[1,112,896]{2,1,0:T(8,128)(2,1)S(1)}, bf16[1,112,896]{2,1,0:T(8,128)(2,1)S(1)}, u32[]{:S(2)}, u32[]{:S(2)}) collective-permute-start(bf16[1,112,896]{2,1,0:T(8,128)(2,1)S(1)} %collective-permute-done.19.refs_20_), channel_id=1, source_target_pairs={{0,1},{1,0},{2,3},{3,2},{4,5},{5,4},{6,7},{7,6},{8,9},{9,8},{10,11... | collective-permute-start | bytes 602120 | tf_op jit(solution)/shard_map/ppermute | solution.py:19
  34.3 3.8 %collective-permute-start.14 = (bf16[1,112,896]{2,1,0:T(8,128)(2,1)S(1)}, bf16[1,112,896]{2,1,0:T(8,128)(2,1)S(1)}, u32[]{:S(2)}, u32[]{:S(2)}) collective-permute-start(bf16[1,112,896]{2,1,0:T(8,128)(2,1)S(1)} %collective-permute-done.13.refs_14_), channel_id=1, source_target_pairs={{0,1},{1,0},{2,3},{3,2},{4,5},{5,4},{6,7},{7,6},{8,9},{9,8},{10,11... | collective-permute-start | bytes 602120 | tf_op jit(solution)/shard_map/ppermute | solution.py:19
  51.8 9.8 %collective-permute-start.26 = (bf16[112,896]{1,0:T(8,128)(2,1)S(1)}, bf16[112,896]{1,0:T(8,128)(2,1)S(1)}, u32[]{:S(2)}, u32[]{:S(2)}) collective-permute-start(bf16[112,896]{1,0:T(8,128)(2,1)S(1)} %get-tuple-element.33), channel_id=1, source_target_pairs={{0,6},{1,7},{2,4},{3,5},{4,2},{5,3},{6,0},{7,1},{8,14},{9,15},{10,... | collective-permute-start | bytes 602120 | tf_op jit(solution)/shard_map/ppermute | solution.py:19
  55.6 17.2 %collective-permute-start.25 = (bf16[112,896]{1,0:T(8,128)(2,1)S(1)}, bf16[112,896]{1,0:T(8,128)(2,1)S(1)}, u32[]{:S(2)}, u32[]{:S(2)}) collective-permute-start(bf16[112,896]{1,0:T(8,128)(2,1)S(1)} %get-tuple-element.34), channel_id=1, source_target_pairs={{0,4},{1,5},{2,6},{3,7},{4,0},{5,1},{6,2},{7,3},{8,12},{9,13},{10,... | collective-permute-start | bytes 602120 | tf_op jit(solution)/shard_map/ppermute | solution.py:19
  55.6 17.2 %collective-permute-start.24 = (bf16[112,896]{1,0:T(8,128)(2,1)S(1)}, bf16[112,896]{1,0:T(8,128)(2,1)S(1)}, u32[]{:S(2)}, u32[]{:S(2)}) collective-permute-start(bf16[112,896]{1,0:T(8,128)(2,1)S(1)} %get-tuple-element.35), channel_id=1, source_target_pairs={{0,2},{1,3},{2,0},{3,1},{4,6},{5,7},{6,4},{7,5},{8,10},{9,11},{10,... | collective-permute-start | bytes 602120 | tf_op jit(solution)/shard_map/ppermute | solution.py:19
  73.0 9.2 %collective-permute-start.42 = (bf16[1,112,896]{2,1,0:T(8,128)(2,1)S(1)}, bf16[1,112,896]{2,1,0:T(8,128)(2,1)S(1)}, u32[]{:S(2)}, u32[]{:S(2)}) collective-permute-start(bf16[1,112,896]{2,1,0:T(8,128)(2,1)S(1)} %get-tuple-element.23.refs_0_), channel_id=1, source_target_pairs={{8,16},{16,8},{9,17},{17,9},{10,18},{18,10},{11,19},{19,11},{12,20... | collective-permute-start | bytes 602120 | tf_op jit(solution)/shard_map/ppermute | solution.py:34
  73.7 11.4 %collective-permute-start.30 = (bf16[1,112,896]{2,1,0:T(8,128)(2,1)S(1)}, bf16[1,112,896]{2,1,0:T(8,128)(2,1)S(1)}, u32[]{:S(2)}, u32[]{:S(2)}) collective-permute-start(bf16[1,112,896]{2,1,0:T(8,128)(2,1)S(1)} %get-tuple-element.23.refs_0_), channel_id=1, source_target_pairs={{0,4},{1,5},{2,6},{3,7},{4,0},{5,1},{6,2},{7,3},{8,12},{9,13},{10,... | collective-permute-start | bytes 602120 | tf_op jit(solution)/shard_map/ppermute | solution.py:19
  73.8 16.6 %collective-permute-start.34 = (bf16[1,112,896]{2,1,0:T(8,128)(2,1)S(1)}, bf16[1,112,896]{2,1,0:T(8,128)(2,1)S(1)}, u32[]{:S(2)}, u32[]{:S(2)}) collective-permute-start(bf16[1,112,896]{2,1,0:T(8,128)(2,1)S(1)} %get-tuple-element.23.refs_0_), channel_id=1, source_target_pairs={{0,8},{8,0},{16,24},{24,16},{1,9},{9,1},{17,25},{25,17},{2,10},{10... | collective-permute-start | bytes 602120 | tf_op jit(solution)/shard_map/ppermute | solution.py:23
  79.4 11.0 %collective-permute-start.28 = (bf16[1,112,896]{2,1,0:T(8,128)(2,1)S(1)}, bf16[1,112,896]{2,1,0:T(8,128)(2,1)S(1)}, u32[]{:S(2)}, u32[]{:S(2)}) collective-permute-start(bf16[1,112,896]{2,1,0:T(8,128)(2,1)S(1)} %get-tuple-element.23.refs_0_), channel_id=1, source_target_pairs={{0,2},{1,3},{2,0},{3,1},{4,6},{5,7},{6,4},{7,5},{8,10},{9,11},{10,... | collective-permute-start | bytes 602120 | tf_op jit(solution)/shard_map/ppermute | solution.py:19
  82.2 8.2 %collective-permute-start.27 = (bf16[1,112,896]{2,1,0:T(8,128)(2,1)S(1)}, bf16[1,112,896]{2,1,0:T(8,128)(2,1)S(1)}, u32[]{:S(2)}, u32[]{:S(2)}) collective-permute-start(bf16[1,112,896]{2,1,0:T(8,128)(2,1)S(1)} %get-tuple-element.23.refs_0_), channel_id=1, source_target_pairs={{0,1},{1,0},{2,3},{3,2},{4,5},{5,4},{6,7},{7,6},{8,9},{9,8},{10,11... | collective-permute-start | bytes 602120 | tf_op jit(solution)/shard_map/ppermute | solution.py:19
  82.2 8.7 %collective-permute-start.43 = (bf16[1,112,896]{2,1,0:T(8,128)(2,1)S(1)}, bf16[1,112,896]{2,1,0:T(8,128)(2,1)S(1)}, u32[]{:S(2)}, u32[]{:S(2)}) collective-permute-start(bf16[1,112,896]{2,1,0:T(8,128)(2,1)S(1)} %collective-permute-done.42.refs_16_), channel_id=1, source_target_pairs={{0,1},{1,0},{2,3},{3,2},{4,5},{5,4},{6,7},{7,6},{8,9},{9,8},{10,11... | collective-permute-start | bytes 602120 | tf_op jit(solution)/shard_map/ppermute | solution.py:19
  85.0 11.1 %collective-permute-start.38 = (bf16[1,112,896]{2,1,0:T(8,128)(2,1)S(1)}, bf16[1,112,896]{2,1,0:T(8,128)(2,1)S(1)}, u32[]{:S(2)}, u32[]{:S(2)}) collective-permute-start(bf16[1,112,896]{2,1,0:T(8,128)(2,1)S(1)} %collective-permute-done.30.refs_4_), channel_id=1, source_target_pairs={{0,8},{8,0},{16,24},{24,16},{1,9},{9,1},{17,25},{25,17},{2,10},{10... | collective-permute-start | bytes 602120 | tf_op jit(solution)/shard_map/ppermute | solution.py:23
  90.4 6.6 %collective-permute-start.32 = (bf16[1,112,896]{2,1,0:T(8,128)(2,1)S(1)}, bf16[1,112,896]{2,1,0:T(8,128)(2,1)S(1)}, u32[]{:S(2)}, u32[]{:S(2)}) collective-permute-start(bf16[1,112,896]{2,1,0:T(8,128)(2,1)S(1)} %collective-permute-done.30.refs_4_), channel_id=1, source_target_pairs={{0,2},{1,3},{2,0},{3,1},{4,6},{5,7},{6,4},{7,5},{8,10},{9,11},{10,... | collective-permute-start | bytes 602120 | tf_op jit(solution)/shard_map/ppermute | solution.py:19
  90.4 9.7 %collective-permute-start.35 = (bf16[1,112,896]{2,1,0:T(8,128)(2,1)S(1)}, bf16[1,112,896]{2,1,0:T(8,128)(2,1)S(1)}, u32[]{:S(2)}, u32[]{:S(2)}) collective-permute-start(bf16[1,112,896]{2,1,0:T(8,128)(2,1)S(1)} %collective-permute-done.34.refs_8_), channel_id=1, source_target_pairs={{0,1},{1,0},{2,3},{3,2},{4,5},{5,4},{6,7},{7,6},{8,9},{9,8},{10,11... | collective-permute-start | bytes 602120 | tf_op jit(solution)/shard_map/ppermute | solution.py:19
  90.5 9.7 %collective-permute-start.31 = (bf16[1,112,896]{2,1,0:T(8,128)(2,1)S(1)}, bf16[1,112,896]{2,1,0:T(8,128)(2,1)S(1)}, u32[]{:S(2)}, u32[]{:S(2)}) collective-permute-start(bf16[1,112,896]{2,1,0:T(8,128)(2,1)S(1)} %collective-permute-done.30.refs_4_), channel_id=1, source_target_pairs={{0,1},{1,0},{2,3},{3,2},{4,5},{5,4},{6,7},{7,6},{8,9},{9,8},{10,11... | collective-permute-start | bytes 602120 | tf_op jit(solution)/shard_map/ppermute | solution.py:19
  91.0 9.5 %collective-permute-start.36 = (bf16[1,112,896]{2,1,0:T(8,128)(2,1)S(1)}, bf16[1,112,896]{2,1,0:T(8,128)(2,1)S(1)}, u32[]{:S(2)}, u32[]{:S(2)}) collective-permute-start(bf16[1,112,896]{2,1,0:T(8,128)(2,1)S(1)} %collective-permute-done.28.refs_2_), channel_id=1, source_target_pairs={{0,8},{8,0},{16,24},{24,16},{1,9},{9,1},{17,25},{25,17},{2,10},{10... | collective-permute-start | bytes 602120 | tf_op jit(solution)/shard_map/ppermute | solution.py:23
  96.2 4.6 %collective-permute-start.29 = (bf16[1,112,896]{2,1,0:T(8,128)(2,1)S(1)}, bf16[1,112,896]{2,1,0:T(8,128)(2,1)S(1)}, u32[]{:S(2)}, u32[]{:S(2)}) collective-permute-start(bf16[1,112,896]{2,1,0:T(8,128)(2,1)S(1)} %collective-permute-done.28.refs_2_), channel_id=1, source_target_pairs={{0,1},{1,0},{2,3},{3,2},{4,5},{5,4},{6,7},{7,6},{8,9},{9,8},{10,11... | collective-permute-start | bytes 602120 | tf_op jit(solution)/shard_map/ppermute | solution.py:19
  96.9 8.1 %collective-permute-start.46 = (bf16[1,112,896]{2,1,0:T(8,128)(2,1)S(1)}, bf16[1,112,896]{2,1,0:T(8,128)(2,1)S(1)}, u32[]{:S(2)}, u32[]{:S(2)}) collective-permute-start(bf16[1,112,896]{2,1,0:T(8,128)(2,1)S(1)} %collective-permute-done.38.refs_12_), channel_id=1, source_target_pairs={{0,16},{24,8},{1,17},{25,9},{2,18},{26,10},{3,19},{27,11},{4,20},{... | collective-permute-start | bytes 602120 | tf_op jit(solution)/shard_map/ppermute | solution.py:29
  100.1 7.2 %collective-permute-start.40 = (bf16[1,112,896]{2,1,0:T(8,128)(2,1)S(1)}, bf16[1,112,896]{2,1,0:T(8,128)(2,1)S(1)}, u32[]{:S(2)}, u32[]{:S(2)}) collective-permute-start(bf16[1,112,896]{2,1,0:T(8,128)(2,1)S(1)} %collective-permute-done.38.refs_12_), channel_id=1, source_target_pairs={{0,2},{1,3},{2,0},{3,1},{4,6},{5,7},{6,4},{7,5},{8,10},{9,11},{10,... | collective-permute-start | bytes 602120 | tf_op jit(solution)/shard_map/ppermute | solution.py:19
  100.2 7.1 %collective-permute-start.39 = (bf16[1,112,896]{2,1,0:T(8,128)(2,1)S(1)}, bf16[1,112,896]{2,1,0:T(8,128)(2,1)S(1)}, u32[]{:S(2)}, u32[]{:S(2)}) collective-permute-start(bf16[1,112,896]{2,1,0:T(8,128)(2,1)S(1)} %collective-permute-done.38.refs_12_), channel_id=1, source_target_pairs={{0,1},{1,0},{2,3},{3,2},{4,5},{5,4},{6,7},{7,6},{8,9},{9,8},{10,11... | collective-permute-start | bytes 602120 | tf_op jit(solution)/shard_map/ppermute | solution.py:19
  100.4 7.3 %collective-permute-start.33 = (bf16[1,112,896]{2,1,0:T(8,128)(2,1)S(1)}, bf16[1,112,896]{2,1,0:T(8,128)(2,1)S(1)}, u32[]{:S(2)}, u32[]{:S(2)}) collective-permute-start(bf16[1,112,896]{2,1,0:T(8,128)(2,1)S(1)} %collective-permute-done.32.refs_6_), channel_id=1, source_target_pairs={{0,1},{1,0},{2,3},{3,2},{4,5},{5,4},{6,7},{7,6},{8,9},{9,8},{10,11... | collective-permute-start | bytes 602120 | tf_op jit(solution)/shard_map/ppermute | solution.py:19
  100.7 7.1 %collective-permute-start.44 = (bf16[1,112,896]{2,1,0:T(8,128)(2,1)S(1)}, bf16[1,112,896]{2,1,0:T(8,128)(2,1)S(1)}, u32[]{:S(2)}, u32[]{:S(2)}) collective-permute-start(bf16[1,112,896]{2,1,0:T(8,128)(2,1)S(1)} %collective-permute-done.28.refs_2_), channel_id=1, source_target_pairs={{8,16},{16,8},{9,17},{17,9},{10,18},{18,10},{11,19},{19,11},{12,20... | collective-permute-start | bytes 602120 | tf_op jit(solution)/shard_map/ppermute | solution.py:34
  105.0 6.5 %collective-permute-start.48 = (bf16[1,112,896]{2,1,0:T(8,128)(2,1)S(1)}, bf16[1,112,896]{2,1,0:T(8,128)(2,1)S(1)}, u32[]{:S(2)}, u32[]{:S(2)}) collective-permute-start(bf16[1,112,896]{2,1,0:T(8,128)(2,1)S(1)} %collective-permute-done.46.refs_20_), channel_id=1, source_target_pairs={{0,2},{1,3},{2,0},{3,1},{4,6},{5,7},{6,4},{7,5},{8,10},{9,11},{10,... | collective-permute-start | bytes 602120 | tf_op jit(solution)/shard_map/ppermute | solution.py:19
  107.2 4.3 %collective-permute-start.37 = (bf16[1,112,896]{2,1,0:T(8,128)(2,1)S(1)}, bf16[1,112,896]{2,1,0:T(8,128)(2,1)S(1)}, u32[]{:S(2)}, u32[]{:S(2)}) collective-permute-start(bf16[1,112,896]{2,1,0:T(8,128)(2,1)S(1)} %collective-permute-done.36.refs_10_), channel_id=1, source_target_pairs={{0,1},{1,0},{2,3},{3,2},{4,5},{5,4},{6,7},{7,6},{8,9},{9,8},{10,11... | collective-permute-start | bytes 602120 | tf_op jit(solution)/shard_map/ppermute | solution.py:19
  107.3 4.3 %collective-permute-start.47 = (bf16[1,112,896]{2,1,0:T(8,128)(2,1)S(1)}, bf16[1,112,896]{2,1,0:T(8,128)(2,1)S(1)}, u32[]{:S(2)}, u32[]{:S(2)}) collective-permute-start(bf16[1,112,896]{2,1,0:T(8,128)(2,1)S(1)} %collective-permute-done.46.refs_20_), channel_id=1, source_target_pairs={{0,1},{1,0},{2,3},{3,2},{4,5},{5,4},{6,7},{7,6},{8,9},{9,8},{10,11... | collective-permute-start | bytes 602120 | tf_op jit(solution)/shard_map/ppermute | solution.py:19
  107.8 3.8 %collective-permute-start.41 = (bf16[1,112,896]{2,1,0:T(8,128)(2,1)S(1)}, bf16[1,112,896]{2,1,0:T(8,128)(2,1)S(1)}, u32[]{:S(2)}, u32[]{:S(2)}) collective-permute-start(bf16[1,112,896]{2,1,0:T(8,128)(2,1)S(1)} %collective-permute-done.40.refs_14_), channel_id=1, source_target_pairs={{0,1},{1,0},{2,3},{3,2},{4,5},{5,4},{6,7},{7,6},{8,9},{9,8},{10,11... | collective-permute-start | bytes 602120 | tf_op jit(solution)/shard_map/ppermute | solution.py:19
  125.2 9.8 %collective-permute-start.53 = (bf16[112,896]{1,0:T(8,128)(2,1)S(1)}, bf16[112,896]{1,0:T(8,128)(2,1)S(1)}, u32[]{:S(2)}, u32[]{:S(2)}) collective-permute-start(bf16[112,896]{1,0:T(8,128)(2,1)S(1)} %get-tuple-element.29), channel_id=1, source_target_pairs={{0,6},{1,7},{2,4},{3,5},{4,2},{5,3},{6,0},{7,1},{8,14},{9,15},{10,... | collective-permute-start | bytes 602120 | tf_op jit(solution)/shard_map/ppermute | solution.py:19
  126.7 18.2 %collective-permute-start.52 = (bf16[112,896]{1,0:T(8,128)(2,1)S(1)}, bf16[112,896]{1,0:T(8,128)(2,1)S(1)}, u32[]{:S(2)}, u32[]{:S(2)}) collective-permute-start(bf16[112,896]{1,0:T(8,128)(2,1)S(1)} %get-tuple-element.30), channel_id=1, source_target_pairs={{0,4},{1,5},{2,6},{3,7},{4,0},{5,1},{6,2},{7,3},{8,12},{9,13},{10,... | collective-permute-start | bytes 602120 | tf_op jit(solution)/shard_map/ppermute | solution.py:19
  127.0 17.9 %collective-permute-start.51 = (bf16[112,896]{1,0:T(8,128)(2,1)S(1)}, bf16[112,896]{1,0:T(8,128)(2,1)S(1)}, u32[]{:S(2)}, u32[]{:S(2)}) collective-permute-start(bf16[112,896]{1,0:T(8,128)(2,1)S(1)} %get-tuple-element.31), channel_id=1, source_target_pairs={{0,2},{1,3},{2,0},{3,1},{4,6},{5,7},{6,4},{7,5},{8,10},{9,11},{10,... | collective-permute-start | bytes 602120 | tf_op jit(solution)/shard_map/ppermute | solution.py:19
  (6 other events, 15.1 us)

commit v4 on v3

--- a/solution.py
+++ b/solution.py
@@ -38,36 +38,74 @@
     return lax.optimization_barrier((x,) + others)[0]
 
 
-def gather_pieces(shard, beside, sec_count, term_count):
+FIRST = {
+    "routes": {},
+    "after": {"B1": ("p3",), "cA3": ("A1",), "p1": ("p2",)},
+    "order": (),
+}
+SECOND = {
+    "routes": {"B0": ("A0", "forward")},
+    "after": {"B1": ("p3",), "cA3": ("A1",)},
+    "order": (),
+}
+
+
+def default_routes(chips):
+    last = chips - 1
+    routes = {}
+    for i in sorted(range(1, chips), key=lambda i: (bin(i).count("1"), i)):
+        routes[f"p{i}"] = (f"p{i ^ (i & -i)}", i & -i)
+    for i in range(chips):
+        routes[f"A{i}"] = (f"p{i}", "pair") if i < last else (f"A{i ^ 1}", 1)
+    for i in range(chips):
+        near = (f"p{i}", "across") if i < chips // 2 else (f"A{i}", "forward")
+        routes[f"B{i}"] = near if i < last else (f"B{i ^ 1}", 1)
+    return routes
+
+
+def gather_pieces(shard, beside, plan, sec_count, term_count):
     chips = term_count // 2
-
-    def hop(x, bit):
-        return along_term(x, lambda t: t ^ (2 * bit), term_count)
-
-    own = {0: shard}
-    for i in sorted(range(1, chips), key=lambda i: (bin(i).count("1"), i)):
-        own[i] = hop(own[i ^ (i & -i)], i & -i)
-    own[1], beside = lax.optimization_barrier((own[1], beside))
-    last = chips - 1
-    pair = {i: pair_exchange(own[i], sec_count) for i in range(last)}
-    pair[last] = hop(pair[last ^ 1], 1)
-    beyond = {}
-    for i in range(last):
-        if i >= chips // 2:
-            beyond[i] = pair_forward(pair[i], sec_count)
+    routes, waits = default_routes(chips), {}
+    if chips == 4 and sec_count == 4:
+        routes.update(plan["routes"])
+        waits = plan["after"]
+    across = {"pair": pair_exchange, "forward": pair_forward, "across": across_pairs}
+    got = {"p0": shard}
+
+    def fetch(name):
+        if name in got:
+            return got[name]
+        if name[0] == "c":
+            origin, way = name[1:], 0
         else:
-            beyond[i] = across_pairs(after(own[i], own[last]) if i else own[i], sec_count)
-    beyond[last] = hop(beyond[last ^ 1], 1)
-    pieces = []
-    for table in (own, pair, beyond):
-        for i in range(chips):
-            pieces.append(table[i])
-            pieces.append(along_term(table[i], lambda t: t ^ 1, term_count))
-    return pieces, beside
-
-
-def apply_kernel(chips, terms, rows, scal, left, right, *refs):
-    pieces = refs[: 6 * chips]
+            origin, way = routes[name]
+        x = fetch(origin)
+        held = tuple(fetch(other) for other in waits.get(name, ()))
+        if held:
+            x = after(x, *held)
+        if way in across:
+            x = across[way](x, sec_count)
+        else:
+            x = along_term(x, lambda t: t ^ (2 * way or 1), term_count)
+        if name == "p1":
+            x, got["beside"] = lax.optimization_barrier((x, beside))
+        got[name] = x
+        return x
+
+    for name in routes:
+        fetch(name)
+    names = [f"{source}{i}" for source in "pAB" for i in range(chips)]
+    pieces = [piece for name in names for piece in (fetch(name), fetch("c" + name))]
+    return pieces, got["beside"]
+
+
+def operand_order(pieces, plan):
+    order = plan["order"]
+    return order if len(order) == len(pieces) else tuple(range(len(pieces)))
+
+
+def apply_kernel(chips, terms, rows, order, scal, left, right, *refs):
+    pieces = dict(zip(order, refs))
     mine, theirs, x_s, l_s, r_s, a_s, l_sem, r_sem = refs[6 * chips :]
     width = x_s.shape[2]
     z, c = scal[2 * terms], scal[2 * terms + 1]
@@ -115,14 +153,15 @@
         theirs[i] = jnp.where(first, total[rows:], total[:rows]).astype(theirs.dtype)
 
 
-def apply_terms(scal, left_env, right_env, pieces, rows):
+def apply_terms(scal, left_env, right_env, pieces, plan, rows):
     terms, _, width, _ = left_env.shape
     chips = len(pieces) // 6
+    order = operand_order(pieces, plan)
     smem, hbm, vmem = (
         pl.BlockSpec(memory_space=m) for m in (pltpu.SMEM, pltpu.HBM, pltpu.VMEM)
     )
     return pl.pallas_call(
-        functools.partial(apply_kernel, chips, terms, rows),
+        functools.partial(apply_kernel, chips, terms, rows, order),
         out_shape=(
             jax.ShapeDtypeStruct((chips, rows, width), jnp.float32),
             jax.ShapeDtypeStruct((chips, rows, width), jnp.bfloat16),
@@ -139,7 +178,88 @@
         ],
         compiler_params=pltpu.CompilerParams(vmem_limit_bytes=46 * 2**20),
         name="apply_terms",
-    )(scal, left_env, right_env, *pieces)
+    )(scal, left_env, right_env, *(pieces[k] for k in order))
+
+
+def chip_kernel(chips, terms, rows, order, scal, theirs, *refs):
+    lefts, rights, pieces = refs[:2], refs[2:4], dict(zip(order, refs[4:]))
+    own, *parts = refs[4 + 6 * chips : 4 + 7 * chips]
+    x_s, l_s, r_s, a_s, l_sem, r_sem = refs[4 + 7 * chips :]
+    width = x_s.shape[2]
+    z, c, block_rows, block_cols = (scal[2 * terms + k] for k in range(4))
+
+    def offset(i, core):
+        return pl.multiple_of((jnp.bitwise_xor(z, i) * 2 + core) * rows, rows)
+
+    def l_copy(w, i):
+        band = pl.ds(offset(i, c), rows)
+        return pltpu.make_async_copy(
+            lefts[w // terms].at[w % terms, 0, band],
+            l_s.at[w, pl.ds(i * rows, rows)],
+            l_sem.at[w],
+        )
+
+    def r_copy(w):
+        return pltpu.make_async_copy(
+            rights[w // terms].at[w % terms, 0], r_s.at[pl.ds(w * width, width)], r_sem.at[w]
+        )
+
+    for w in range(2 * terms):
+        for i in range(chips):
+            l_copy(w, i).start()
+    for w in range(2 * terms):
+        r_copy(w).start()
+    for source in range(3):
+        for i in range(chips):
+            for other in range(2):
+                band = pl.ds(offset(i, jnp.bitwise_xor(c, other)), rows)
+                x_s[source, band, :] = pieces[source * 2 * chips + 2 * i + other][0]
+    for w in range(2 * terms):
+        table = theirs if w >= terms else scal
+        source, on = table[w % terms], table[terms + w % terms].astype(jnp.float32)
+        for i in range(chips):
+            l_copy(w, i).wait()
+        product = jnp.dot(l_s[w], x_s[source], preferred_element_type=jnp.float32)
+        a_s[:, w * width : (w + 1) * width] = (product * on).astype(jnp.bfloat16)
+    for w in range(2 * terms):
+        r_copy(w).wait()
+    total = jnp.dot(a_s[...], r_s[...], preferred_element_type=jnp.float32)
+    col = lax.broadcasted_iota(jnp.int32, (rows, width), 1)
+    row = lax.broadcasted_iota(jnp.int32, (rows, width), 0)
+    for i in range(chips):
+        inside = (row + offset(i, c) < block_rows) & (col < block_cols)
+        band = jnp.where(inside, total[i * rows : (i + 1) * rows], 0.0)
+        if i:
+            parts[i - 1][...] = band.astype(jnp.bfloat16)
+        else:
+            own[...] = band
+
+
+def apply_chip_terms(scal, theirs, envs, pieces, plan, rows):
+    terms, _, width, _ = envs[0].shape
+    chips = len(pieces) // 6
+    order = operand_order(pieces, plan)
+    smem, hbm, vmem = (
+        pl.BlockSpec(memory_space=m) for m in (pltpu.SMEM, pltpu.HBM, pltpu.VMEM)
+    )
+    own, *parts = pl.pallas_call(
+        functools.partial(chip_kernel, chips, terms, rows, order),
+        out_shape=[jax.ShapeDtypeStruct((rows, width), jnp.float32)]
+        + [jax.ShapeDtypeStruct((rows, width), jnp.bfloat16)] * (chips - 1),
+        in_specs=[smem] * 2 + [hbm] * 4 + [vmem] * len(pieces),
+        out_specs=[vmem] * chips,
+        scratch_shapes=[
+            pltpu.VMEM((3, width, width), jnp.bfloat16),
+            pltpu.VMEM((2 * terms, chips * rows, width), jnp.bfloat16),
+            pltpu.VMEM((2 * terms * width, width), jnp.bfloat16),
+            pltpu.VMEM((chips * rows, 2 * terms * width), jnp.bfloat16),
+            pltpu.SemaphoreType.DMA((2 * terms,)),
+            pltpu.SemaphoreType.DMA((2 * terms,)),
+        ],
+        compiler_params=pltpu.CompilerParams(vmem_limit_bytes=46 * 2**20),
+        name="apply_chip_terms",
+    )(scal, theirs, *envs, *(pieces[k] for k in order))
+    return own, parts
 
 
 def reduce_parts(mine, theirs, term_count):
@@ -150,6 +270,14 @@
         for i in range(1, term_count // 2)
     ]
     return totals[0], parts
+
+
+def send_parts(parts, term_count):
+    sent = [
+        along_term(parts[i - 1], lambda t, b=i: t ^ (2 * b), term_count)
+        for i in range(len(parts), 0, -1)
+    ]
+    return sent[::-1]
 
 
 def everyones(tile, count):
@@ -220,6 +348,7 @@
 
 def on_device(theta, left_env, right_env, term_shift, term_on, block_rows, block_cols):
     rows, width = theta.shape[1:]
+    terms = left_env.shape[0]
     sec_count, term_count = lax.axis_size("sec"), lax.axis_size("term")
     sec, term = lax.axis_index("sec"), lax.axis_index("term")
     row = term * rows + lax.broadcasted_iota(jnp.int32, (1, rows, width), 1)
@@ -237,9 +366,13 @@
     tile = jax.ShapeDtypeStruct((8, 128), jnp.float32)
     pair = jax.ShapeDtypeStruct((2,), jnp.float32)
 
-    pieces, scal = gather_pieces(start, scal, sec_count, term_count)
-    mine, theirs = apply_terms(scal, left_env, right_env, pieces, rows)
+    pieces, scal = gather_pieces(start, scal, FIRST, sec_count, term_count)
+    mine, theirs = apply_terms(scal, left_env, right_env, pieces, FIRST, rows)
     own, got = reduce_parts(mine, theirs, term_count)
+    local = lax.optimization_barrier((left_env, right_env, scal[: 2 * terms], own))[:3]
+    swapped = [along_term(a, lambda t: t ^ 1, term_count) for a in local]
+    own, swapped = lax.optimization_barrier((own, swapped))
+    envs = (left_env, swapped[0], right_env, swapped[1])
     y, shard, sums = pl.pallas_call(
         image_kernel,
         out_shape=(block, jax.ShapeDtypeStruct((1, rows, width), jnp.bfloat16), tile),
@@ -248,9 +381,9 @@
         compiler_params=small,
         name="image",
     )(start, own, *got)
-    pieces, _ = gather_pieces(shard, (), sec_count, term_count)
-    mine, theirs = apply_terms(scal, left_env, right_env, pieces, rows)
-    own, got = reduce_parts(mine, theirs, term_count)
+    pieces, _ = gather_pieces(shard, (), SECOND, sec_count, term_count)
+    own, parts = apply_chip_terms(scal, swapped[2], envs, pieces, SECOND, rows)
+    got = send_parts(parts, term_count)
     h, sums = pl.pallas_call(
         gram_kernel,
         out_shape=(block, tile),
@@ -258,7 +391,7 @@
         out_specs=(vmem, vmem),
         compiler_params=small,
         name="gram",
-    )(sums, start, y, own, *got)
+    )(sums, start, y, own, *got[::-1])
     sums = everyones(sums, sec_count * term_count)
     vector, alphas, betas = pl.pallas_call(
         finish_kernel,

time: 162 us -> 158 us (0.975)
  starting transfers between devices: 52.4 us -> 47.7 us
  waiting for transfers between devices: 68.1 us -> 71.8 us
  blocking collectives: 14.8 us -> 12.1 us
    ppermute x6, starting transfers between devices: 18.4 us -> 11.8 us  [pair_exchange(): lax.ppermute(x, 'sec', [(i, i ^ 1) for i in range(count) if i ^ 1 < count])]
    ppermute x42 -> x44, waiting for transfers between devices: 54.5 us -> 59.1 us  [along_term(): return lax.ppermute(x, 'term', [(i, partner(i)) for i in range(count)])]
    ppermute x2 -> x3, starting transfers between devices: 5.67 us -> 8.79 us  [pair_forward(): return lax.ppermute(x, 'sec', pairs)]
    all_to_all x1, blocking collectives: 14.8 us -> 12.1 us  [everyones(): lax.all_to_all(jnp.broadcast_to(tile, (count,) + tile.shape), ('sec', 'te...]
    ppermute x2 -> x3, waiting for transfers between devices: 4.55 us -> 3.42 us  [pair_forward(): return lax.ppermute(x, 'sec', pairs)]
    ppermute x42 -> x44, starting transfers between devices: 25.7 us -> 24.9 us  [along_term(): return lax.ppermute(x, 'term', [(i, partner(i)) for i in range(count)])]
  transfers between devices with their start and end apart: 54 -> 56, of which waited for: 21 -> 22; matrix products, arithmetic and copies ran while one was open for 1% -> 1% of each run, Pallas kernels for 0% -> 0%
where the time goes in v4:
time: 158 us
  waiting for transfers between devices  71.8 us (45%)
  starting transfers between devices  47.7 us (30%)
  Pallas kernels  21.3 us (13%)
  blocking collectives  12.1 us (8%)
  between operations  2.4 us (2%)
  other arithmetic  1.87 us (1%)
    ppermute x44, waiting for transfers between devices, along_term(): return lax.ppermute(x, 'term', [(i, partner(i)) for i in range(count)])  59.1 us
    ppermute x44, starting transfers between devices, along_term(): return lax.ppermute(x, 'term', [(i, partner(i)) for i in range(count)])  24.9 us
    all_to_all x1, blocking collectives, everyones(): lax.all_to_all(jnp.broadcast_to(tile, (count,) + tile.shape), ('sec', 'te...  12.1 us
    ppermute x6, starting transfers between devices, pair_exchange(): lax.ppermute(x, 'sec', [(i, i ^ 1) for i in range(count) if i ^ 1 < count])  11.8 us
    pallas_call x1, Pallas kernels, apply_terms(): pl.pallas_call(functools.partial(apply_kernel, chips, terms, rows, order)...  9.94 us
    pallas_call x1, Pallas kernels, apply_chip_terms(): pl.pallas_call(functools.partial(chip_kernel, chips, terms, rows, order),...  9.83 us
    ppermute x6, waiting for transfers between devices, pair_exchange(): lax.ppermute(x, 'sec', [(i, i ^ 1) for i in range(count) if i ^ 1 < count])  9.28 us
    ppermute x3, starting transfers between devices, pair_forward(): return lax.ppermute(x, 'sec', pairs)  8.79 us
  transfers between devices with their start and end apart: 56, of which 22 were waited for; matrix products, arithmetic and copies ran while one was open for 1% of the time, Pallas kernels for 0%

profile of v4, /device:TPU:0, one launch (start us, length us, event | category | flops | bytes accessed | tf_op | source)
XLA Modules:
  0.0 158.0 jit_solution(10277660371393761822)
XLA Ops:
  2.0 1.1 and_select_fusion.refs_0_.x_ref
  3.0 4.1 %collective-permute-start = (bf16[1,112,896]{2,1,0:T(8,128)(2,1)S(1)}, bf16[1,112,896]{2,1,0:T(8,128)(2,1)S(1)}, u32[]{:S(2)}, u32[]{:S(2)}) collective-permute-start(bf16[1,112,896]{2,1,0:T(8,128)(2,1)S(1)} %and_select_fusion.refs_0_.x_ref), channel_id=1, source_target_pairs={{0,4},{1,5},{2,6},{3,7},{4,0},{5,1},{6,2},{7,3},{8,12},{9,13},{10,... | collective-permute-start | bytes 602120 | tf_op jit(solution)/shard_map/ppermute | solution.py:19
  7.1 0.7 collective-permute-start.15
  7.8 4.3 %collective-permute-start.7 = (bf16[1,112,896]{2,1,0:T(8,128)(2,1)S(1)}, bf16[1,112,896]{2,1,0:T(8,128)(2,1)S(1)}, u32[]{:S(2)}, u32[]{:S(2)}) collective-permute-start(bf16[1,112,896]{2,1,0:T(8,128)(2,1)S(1)} %and_select_fusion.refs_0_.x_ref), channel_id=1, source_target_pairs={{0,8},{8,0},{16,24},{24,16},{1,9},{9,1},{17,25},{25,17},{2,10},{10... | collective-permute-start | bytes 602120 | tf_op jit(solution)/shard_map/ppermute | solution.py:23
  12.1 4.3 %collective-permute-done.refs_4_ = bf16[1,112,896]{2,1,0:T(8,128)(2,1)S(1)} collective-permute-done((bf16[1,112,896]{2,1,0:T(8,128)(2,1)S(1)}, bf16[1,112,896]{2,1,0:T(8,128)(2,1)S(1)}, u32[]{:S(2)}, u32[]{:S(2)}) %collective-permute-start) | collective-permute-done | bytes 200736 | tf_op jit(solution)/shard_map/ppermute | solution.py:19
  16.4 0.7 collective-permute-start.1
  17.1 1.5 collective-permute-start.11
  18.6 1.4 collective-permute-start.5
  20.0 1.9 %collective-permute-done.7.refs_8_ = bf16[1,112,896]{2,1,0:T(8,128)(2,1)S(1)} collective-permute-done((bf16[1,112,896]{2,1,0:T(8,128)(2,1)S(1)}, bf16[1,112,896]{2,1,0:T(8,128)(2,1)S(1)}, u32[]{:S(2)}, u32[]{:S(2)}) %collective-permute-start.7) | collective-permute-done | bytes 200736 | tf_op jit(solution)/shard_map/ppermute | solution.py:23
  21.9 0.7 compare_select_fusion.1
  22.5 0.7 concatenate.3.scal
  23.3 1.1 collective-permute-done.1.refs_2_
  24.9 1.5 collective-permute-start.9
  26.4 3.4 %collective-permute-start.19 = (bf16[1,112,896]{2,1,0:T(8,128)(2,1)S(1)}, bf16[1,112,896]{2,1,0:T(8,128)(2,1)S(1)}, u32[]{:S(2)}, u32[]{:S(2)}) collective-permute-start(bf16[1,112,896]{2,1,0:T(8,128)(2,1)S(1)} %collective-permute-done.11.refs_12_), channel_id=1, source_target_pairs={{0,16},{24,8},{1,17},{25,9},{2,18},{26,10},{3,19},{27,11},{4,20},{... | collective-permute-start | bytes 602120 | tf_op jit(solution)/shard_map/ppermute | solution.py:29
  29.8 0.7 collective-permute-start.13
  31.0 0.8 collective-permute-done.9.refs_10_
  31.8 0.7 collective-permute-start.17
  32.5 1.5 collective-permute-done.19.refs_20_
  34.0 2.3 %collective-permute-done.13.refs_14_ = bf16[1,112,896]{2,1,0:T(8,128)(2,1)S(1)} collective-permute-done((bf16[1,112,896]{2,1,0:T(8,128)(2,1)S(1)}, bf16[1,112,896]{2,1,0:T(8,128)(2,1)S(1)}, u32[]{:S(2)}, u32[]{:S(2)}) %collective-permute-start.13) | collective-permute-done | bytes 200736 | tf_op jit(solution)/shard_map/ppermute | solution.py:19
  37.9 4.1 %collective-permute-done.21.refs_22_ = bf16[1,112,896]{2,1,0:T(8,128)(2,1)S(1)} collective-permute-done((bf16[1,112,896]{2,1,0:T(8,128)(2,1)S(1)}, bf16[1,112,896]{2,1,0:T(8,128)(2,1)S(1)}, u32[]{:S(2)}, u32[]{:S(2)}) %collective-permute-start.21) | collective-permute-done | bytes 200736 | tf_op jit(solution)/shard_map/ppermute | solution.py:19
  42.1 1.4 collective-permute-done.22.refs_23_
  43.5 9.9 %apply_terms.1 = (f32[4,112,896]{2,1,0:T(8,128)S(1)}, bf16[4,112,896]{2,1,0:T(8,128)(2,1)S(1)}) custom-call(s32[8]{0:T(128)S(1)} %concatenate.3.scal, bf16[2,1,896,896]{3,2,1,0:T(8,128)(2,1)} %refs_0_.1, bf16[2,1,896,896]{3,2,1,0:T(8,128)(2,1)} %refs_2_.1, bf16[1,112,896]{2,1,0:T(8,128)(2,1)S(1)} %and_select_fusion.refs_0_.x_ref, ...), custom_call_target="tpu_custom_call" | custom-call | tf_op jit(solution)/shard_map/apply_terms/pallas_call | solution.py:163
  53.6 2.2 %collective-permute-done.23 = bf16[4,112,896]{2,1,0:T(8,128)(2,1)S(1)} collective-permute-done((bf16[4,112,896]{2,1,0:T(8,128)(2,1)S(1)}, bf16[4,112,896]{2,1,0:T(8,128)(2,1)S(1)}, u32[]{:S(2)}, u32[]{:S(2)}) %collective-permute-start.23) | collective-permute-done | bytes 802848 | tf_op jit(solution)/shard_map/ppermute | solution.py:19
  56.7 3.4 %collective-permute-start.29 = (bf16[112,896]{1,0:T(8,128)(2,1)S(1)}, bf16[112,896]{1,0:T(8,128)(2,1)S(1)}, u32[]{:S(2)}, u32[]{:S(2)}) collective-permute-start(bf16[112,896]{1,0:T(8,128)(2,1)S(1)} %get-tuple-element.53), channel_id=1, source_target_pairs={{0,6},{1,7},{2,4},{3,5},{4,2},{5,3},{6,0},{7,1},{8,14},{9,15},{10,... | collective-permute-start | bytes 602120 | tf_op jit(solution)/shard_map/ppermute | solution.py:19
  60.1 6.3 %collective-permute-done.26.theirs = s32[4]{0:T(128)S(1)} collective-permute-done((s32[4]{0:T(128)S(1)}, s32[4]{0:T(128)S(1)}, u32[]{:S(2)}, u32[]{:S(2)}) %collective-permute-start.26) | collective-permute-done | bytes 48 | tf_op jit(solution)/shard_map/ppermute | solution.py:19
  67.0 10.5 %collective-permute-done.28.refs_1_ = bf16[112,896]{1,0:T(8,128)(2,1)S(1)} collective-permute-done((bf16[112,896]{1,0:T(8,128)(2,1)S(1)}, bf16[112,896]{1,0:T(8,128)(2,1)S(1)}, u32[]{:S(2)}, u32[]{:S(2)}) %collective-permute-start.28) | collective-permute-done | bytes 200736 | tf_op jit(solution)/shard_map/ppermute | solution.py:19
  77.9 2.0 %collective-permute-start.37 = (bf16[1,112,896]{2,1,0:T(8,128)(2,1)S(1)}, bf16[1,112,896]{2,1,0:T(8,128)(2,1)S(1)}, u32[]{:S(2)}, u32[]{:S(2)}) collective-permute-start(bf16[1,112,896]{2,1,0:T(8,128)(2,1)S(1)} %get-tuple-element.44.refs_4_), channel_id=1, source_target_pairs={{0,8},{8,0},{16,24},{24,16},{1,9},{9,1},{17,25},{25,17},{2,10},{10... | collective-permute-start | bytes 602120 | tf_op jit(solution)/shard_map/ppermute | solution.py:23
  80.0 1.7 %collective-permute-start.33 = (bf16[1,112,896]{2,1,0:T(8,128)(2,1)S(1)}, bf16[1,112,896]{2,1,0:T(8,128)(2,1)S(1)}, u32[]{:S(2)}, u32[]{:S(2)}) collective-permute-start(bf16[1,112,896]{2,1,0:T(8,128)(2,1)S(1)} %get-tuple-element.44.refs_4_), channel_id=1, source_target_pairs={{0,4},{1,5},{2,6},{3,7},{4,0},{5,1},{6,2},{7,3},{8,12},{9,13},{10,... | collective-permute-start | bytes 602120 | tf_op jit(solution)/shard_map/ppermute | solution.py:19
  81.7 2.5 %collective-permute-start.31 = (bf16[1,112,896]{2,1,0:T(8,128)(2,1)S(1)}, bf16[1,112,896]{2,1,0:T(8,128)(2,1)S(1)}, u32[]{:S(2)}, u32[]{:S(2)}) collective-permute-start(bf16[1,112,896]{2,1,0:T(8,128)(2,1)S(1)} %get-tuple-element.44.refs_4_), channel_id=1, source_target_pairs={{0,2},{1,3},{2,0},{3,1},{4,6},{5,7},{6,4},{7,5},{8,10},{9,11},{10,... | collective-permute-start | bytes 602120 | tf_op jit(solution)/shard_map/ppermute | solution.py:19
  84.2 0.6 collective-permute-done.37.refs_12_
  84.8 3.6 %collective-permute-start.45 = (bf16[1,112,896]{2,1,0:T(8,128)(2,1)S(1)}, bf16[1,112,896]{2,1,0:T(8,128)(2,1)S(1)}, u32[]{:S(2)}, u32[]{:S(2)}) collective-permute-start(bf16[1,112,896]{2,1,0:T(8,128)(2,1)S(1)} %collective-permute-done.37.refs_12_), channel_id=1, source_target_pairs={{0,16},{24,8},{1,17},{25,9},{2,18},{26,10},{3,19},{27,11},{4,20},{... | collective-permute-start | bytes 602120 | tf_op jit(solution)/shard_map/ppermute | solution.py:29
  88.5 3.1 %collective-permute-done.33.refs_8_ = bf16[1,112,896]{2,1,0:T(8,128)(2,1)S(1)} collective-permute-done((bf16[1,112,896]{2,1,0:T(8,128)(2,1)S(1)}, bf16[1,112,896]{2,1,0:T(8,128)(2,1)S(1)}, u32[]{:S(2)}, u32[]{:S(2)}) %collective-permute-start.33) | collective-permute-done | bytes 200736 | tf_op jit(solution)/shard_map/ppermute | solution.py:19
  92.1 2.1 %collective-permute-start.39 = (bf16[1,112,896]{2,1,0:T(8,128)(2,1)S(1)}, bf16[1,112,896]{2,1,0:T(8,128)(2,1)S(1)}, u32[]{:S(2)}, u32[]{:S(2)}) collective-permute-start(bf16[1,112,896]{2,1,0:T(8,128)(2,1)S(1)} %collective-permute-done.31.refs_6_), channel_id=1, source_target_pairs={{0,8},{8,0},{16,24},{24,16},{1,9},{9,1},{17,25},{25,17},{2,10},{10... | collective-permute-start | bytes 602120 | tf_op jit(solution)/shard_map/ppermute | solution.py:23
  94.2 5.3 %collective-permute-done.41.refs_16_ = bf16[1,112,896]{2,1,0:T(8,128)(2,1)S(1)} collective-permute-done((bf16[1,112,896]{2,1,0:T(8,128)(2,1)S(1)}, bf16[1,112,896]{2,1,0:T(8,128)(2,1)S(1)}, u32[]{:S(2)}, u32[]{:S(2)}) %collective-permute-start.41) | collective-permute-done | bytes 200736 | tf_op jit(solution)/shard_map/ppermute | solution.py:23
  99.5 1.8 %collective-permute-start.49 = (bf16[1,112,896]{2,1,0:T(8,128)(2,1)S(1)}, bf16[1,112,896]{2,1,0:T(8,128)(2,1)S(1)}, u32[]{:S(2)}, u32[]{:S(2)}) collective-permute-start(bf16[1,112,896]{2,1,0:T(8,128)(2,1)S(1)} %collective-permute-done.41.refs_16_), channel_id=1, source_target_pairs={{0,16},{24,8},{1,17},{25,9},{2,18},{26,10},{3,19},{27,11},{4,20},{... | collective-permute-start | bytes 602120 | tf_op jit(solution)/shard_map/ppermute | solution.py:29
  101.5 0.6 collective-permute-done.39.refs_14_
  102.6 1.9 %collective-permute-done.49.refs_24_ = bf16[1,112,896]{2,1,0:T(8,128)(2,1)S(1)} collective-permute-done((bf16[1,112,896]{2,1,0:T(8,128)(2,1)S(1)}, bf16[1,112,896]{2,1,0:T(8,128)(2,1)S(1)}, u32[]{:S(2)}, u32[]{:S(2)}) %collective-permute-start.49) | collective-permute-done | bytes 200736 | tf_op jit(solution)/shard_map/ppermute | solution.py:29
  104.5 0.8 collective-permute-start.47
  105.3 2.6 %collective-permute-done.43.refs_18_ = bf16[1,112,896]{2,1,0:T(8,128)(2,1)S(1)} collective-permute-done((bf16[1,112,896]{2,1,0:T(8,128)(2,1)S(1)}, bf16[1,112,896]{2,1,0:T(8,128)(2,1)S(1)}, u32[]{:S(2)}, u32[]{:S(2)}) %collective-permute-start.43) | collective-permute-done | bytes 200736 | tf_op jit(solution)/shard_map/ppermute | solution.py:19
  108.9 4.7 %collective-permute-done.51.refs_26_ = bf16[1,112,896]{2,1,0:T(8,128)(2,1)S(1)} collective-permute-done((bf16[1,112,896]{2,1,0:T(8,128)(2,1)S(1)}, bf16[1,112,896]{2,1,0:T(8,128)(2,1)S(1)}, u32[]{:S(2)}, u32[]{:S(2)}) %collective-permute-start.51) | collective-permute-done | bytes 200736 | tf_op jit(solution)/shard_map/ppermute | solution.py:19
  113.7 1.4 collective-permute-done.52.refs_27_
  115.1 9.8 %apply_chip_terms.1 = (f32[112,896]{1,0:T(8,128)S(1)}, bf16[112,896]{1,0:T(8,128)(2,1)S(1)}, bf16[112,896]{1,0:T(8,128)(2,1)S(1)}, bf16[112,896]{1,0:T(8,128)(2,1)S(1)}) custom-call(s32[8]{0:T(128)S(1)} %concatenate.3.scal, s32[4]{0:T(128)S(1)} %collective-permute-done.26.theirs, bf16[2,1,896,896]{3,2,1,0:T(8,128)(2,1)} %refs_0_.1, ...), custom_call_target="tpu_custom_call" | custom-call | tf_op jit(solution)/shard_map/apply_chip_terms/pallas_call | solution.py:245
  124.9 1.7 %collective-permute-start.53 = (bf16[112,896]{1,0:T(8,128)(2,1)S(1)}, bf16[112,896]{1,0:T(8,128)(2,1)S(1)}, u32[]{:S(2)}, u32[]{:S(2)}) collective-permute-start(bf16[112,896]{1,0:T(8,128)(2,1)S(1)} %get-tuple-element.48), channel_id=1, source_target_pairs={{0,6},{1,7},{2,4},{3,5},{4,2},{5,3},{6,0},{7,1},{8,14},{9,15},{10,... | collective-permute-start | bytes 602120 | tf_op jit(solution)/shard_map/ppermute | solution.py:19
  126.6 2.7 %collective-permute-start.55 = (bf16[112,896]{1,0:T(8,128)(2,1)S(1)}, bf16[112,896]{1,0:T(8,128)(2,1)S(1)}, u32[]{:S(2)}, u32[]{:S(2)}) collective-permute-start(bf16[112,896]{1,0:T(8,128)(2,1)S(1)} %get-tuple-element.50), channel_id=1, source_target_pairs={{0,2},{1,3},{2,0},{3,1},{4,6},{5,7},{6,4},{7,5},{8,10},{9,11},{10,... | collective-permute-start | bytes 602120 | tf_op jit(solution)/shard_map/ppermute | solution.py:19
  129.4 5.4 %collective-permute-done.53.refs_0_ = bf16[112,896]{1,0:T(8,128)(2,1)S(1)} collective-permute-done((bf16[112,896]{1,0:T(8,128)(2,1)S(1)}, bf16[112,896]{1,0:T(8,128)(2,1)S(1)}, u32[]{:S(2)}, u32[]{:S(2)}) %collective-permute-start.53) | collective-permute-done | bytes 200736 | tf_op jit(solution)/shard_map/ppermute | solution.py:19
  134.8 9.6 %collective-permute-done.54.refs_1_ = bf16[112,896]{1,0:T(8,128)(2,1)S(1)} collective-permute-done((bf16[112,896]{1,0:T(8,128)(2,1)S(1)}, bf16[112,896]{1,0:T(8,128)(2,1)S(1)}, u32[]{:S(2)}, u32[]{:S(2)}) %collective-permute-start.54) | collective-permute-done | bytes 200736 | tf_op jit(solution)/shard_map/ppermute | solution.py:19
  144.6 12.1 %all_to_all.5.tiles = f32[32,8,128]{2,1,0:T(8,128)S(1)} all-to-all(f32[32,8,128]{2,1,0:T(8,128)S(1)} %broadcast_in_dim.19), channel_id=1, replica_groups=mesh['sec'=4,'term'=8] {'sec','term'}, dimensions={0} | all-to-all | bytes 262144 | tf_op jit(solution)/shard_map/all_to_all | solution.py:284
  156.7 1.1 finish.1
  (85 shorter events, 7.2 us)
Async XLA Ops:
  3.0 13.4 %collective-permute-start = (bf16[1,112,896]{2,1,0:T(8,128)(2,1)S(1)}, bf16[1,112,896]{2,1,0:T(8,128)(2,1)S(1)}, u32[]{:S(2)}, u32[]{:S(2)}) collective-permute-start(bf16[1,112,896]{2,1,0:T(8,128)(2,1)S(1)} %and_select_fusion.refs_0_.x_ref), channel_id=1, source_target_pairs={{0,4},{1,5},{2,6},{3,7},{4,0},{5,1},{6,2},{7,3},{8,12},{9,13},{10,... | collective-permute-start | bytes 602120 | tf_op jit(solution)/shard_map/ppermute | solution.py:19
  7.1 11.5 %collective-permute-start.15 = (bf16[1,112,896]{2,1,0:T(8,128)(2,1)S(1)}, bf16[1,112,896]{2,1,0:T(8,128)(2,1)S(1)}, u32[]{:S(2)}, u32[]{:S(2)}) collective-permute-start(bf16[1,112,896]{2,1,0:T(8,128)(2,1)S(1)} %and_select_fusion.refs_0_.x_ref), channel_id=1, source_target_pairs={{8,16},{16,8},{9,17},{17,9},{10,18},{18,10},{11,19},{19,11},{12,20... | collective-permute-start | bytes 602120 | tf_op jit(solution)/shard_map/ppermute | solution.py:34
  7.8 14.1 %collective-permute-start.7 = (bf16[1,112,896]{2,1,0:T(8,128)(2,1)S(1)}, bf16[1,112,896]{2,1,0:T(8,128)(2,1)S(1)}, u32[]{:S(2)}, u32[]{:S(2)}) collective-permute-start(bf16[1,112,896]{2,1,0:T(8,128)(2,1)S(1)} %and_select_fusion.refs_0_.x_ref), channel_id=1, source_target_pairs={{0,8},{8,0},{16,24},{24,16},{1,9},{9,1},{17,25},{25,17},{2,10},{10... | collective-permute-start | bytes 602120 | tf_op jit(solution)/shard_map/ppermute | solution.py:23
  12.1 12.3 %collective-permute-start.2 = (bf16[1,112,896]{2,1,0:T(8,128)(2,1)S(1)}, bf16[1,112,896]{2,1,0:T(8,128)(2,1)S(1)}, u32[]{:S(2)}, u32[]{:S(2)}) collective-permute-start(bf16[1,112,896]{2,1,0:T(8,128)(2,1)S(1)} %and_select_fusion.refs_0_.x_ref), channel_id=1, source_target_pairs={{0,1},{1,0},{2,3},{3,2},{4,5},{5,4},{6,7},{7,6},{8,9},{9,8},{10,11... | collective-permute-start | bytes 602120 | tf_op jit(solution)/shard_map/ppermute | solution.py:19
  16.4 7.9 %collective-permute-start.1 = (bf16[1,112,896]{2,1,0:T(8,128)(2,1)S(1)}, bf16[1,112,896]{2,1,0:T(8,128)(2,1)S(1)}, u32[]{:S(2)}, u32[]{:S(2)}) collective-permute-start(bf16[1,112,896]{2,1,0:T(8,128)(2,1)S(1)} %and_select_fusion.refs_0_.x_ref), channel_id=1, source_target_pairs={{0,2},{1,3},{2,0},{3,1},{4,6},{5,7},{6,4},{7,5},{8,10},{9,11},{10,... | collective-permute-start | bytes 602120 | tf_op jit(solution)/shard_map/ppermute | solution.py:19
  17.1 9.3 %collective-permute-start.11 = (bf16[1,112,896]{2,1,0:T(8,128)(2,1)S(1)}, bf16[1,112,896]{2,1,0:T(8,128)(2,1)S(1)}, u32[]{:S(2)}, u32[]{:S(2)}) collective-permute-start(bf16[1,112,896]{2,1,0:T(8,128)(2,1)S(1)} %collective-permute-done.refs_4_), channel_id=1, source_target_pairs={{0,8},{8,0},{16,24},{24,16},{1,9},{9,1},{17,25},{25,17},{2,10},{10... | collective-permute-start | bytes 602120 | tf_op jit(solution)/shard_map/ppermute | solution.py:23
  18.6 11.2 %collective-permute-start.5 = (bf16[1,112,896]{2,1,0:T(8,128)(2,1)S(1)}, bf16[1,112,896]{2,1,0:T(8,128)(2,1)S(1)}, u32[]{:S(2)}, u32[]{:S(2)}) collective-permute-start(bf16[1,112,896]{2,1,0:T(8,128)(2,1)S(1)} %collective-permute-done.refs_4_), channel_id=1, source_target_pairs={{0,2},{1,3},{2,0},{3,1},{4,6},{5,7},{6,4},{7,5},{8,10},{9,11},{10,... | collective-permute-start | bytes 602120 | tf_op jit(solution)/shard_map/ppermute | solution.py:19
  24.3 6.2 %collective-permute-start.8 = (bf16[1,112,896]{2,1,0:T(8,128)(2,1)S(1)}, bf16[1,112,896]{2,1,0:T(8,128)(2,1)S(1)}, u32[]{:S(2)}, u32[]{:S(2)}) collective-permute-start(bf16[1,112,896]{2,1,0:T(8,128)(2,1)S(1)} %collective-permute-done.7.refs_8_), channel_id=1, source_target_pairs={{0,1},{1,0},{2,3},{3,2},{4,5},{5,4},{6,7},{7,6},{8,9},{9,8},{10,11... | collective-permute-start | bytes 602120 | tf_op jit(solution)/shard_map/ppermute | solution.py:19
  24.3 6.2 %collective-permute-start.4 = (bf16[1,112,896]{2,1,0:T(8,128)(2,1)S(1)}, bf16[1,112,896]{2,1,0:T(8,128)(2,1)S(1)}, u32[]{:S(2)}, u32[]{:S(2)}) collective-permute-start(bf16[1,112,896]{2,1,0:T(8,128)(2,1)S(1)} %collective-permute-done.refs_4_), channel_id=1, source_target_pairs={{0,1},{1,0},{2,3},{3,2},{4,5},{5,4},{6,7},{7,6},{8,9},{9,8},{10,11... | collective-permute-start | bytes 602120 | tf_op jit(solution)/shard_map/ppermute | solution.py:19
  24.9 7.0 %collective-permute-start.9 = (bf16[1,112,896]{2,1,0:T(8,128)(2,1)S(1)}, bf16[1,112,896]{2,1,0:T(8,128)(2,1)S(1)}, u32[]{:S(2)}, u32[]{:S(2)}) collective-permute-start(bf16[1,112,896]{2,1,0:T(8,128)(2,1)S(1)} %collective-permute-done.1.refs_2_), channel_id=1, source_target_pairs={{0,8},{8,0},{16,24},{24,16},{1,9},{9,1},{17,25},{25,17},{2,10},{10... | collective-permute-start | bytes 602120 | tf_op jit(solution)/shard_map/ppermute | solution.py:23
  26.4 7.6 %collective-permute-start.19 = (bf16[1,112,896]{2,1,0:T(8,128)(2,1)S(1)}, bf16[1,112,896]{2,1,0:T(8,128)(2,1)S(1)}, u32[]{:S(2)}, u32[]{:S(2)}) collective-permute-start(bf16[1,112,896]{2,1,0:T(8,128)(2,1)S(1)} %collective-permute-done.11.refs_12_), channel_id=1, source_target_pairs={{0,16},{24,8},{1,17},{25,9},{2,18},{26,10},{3,19},{27,11},{4,20},{... | collective-permute-start | bytes 602120 | tf_op jit(solution)/shard_map/ppermute | solution.py:29
  29.8 6.5 %collective-permute-start.13 = (bf16[1,112,896]{2,1,0:T(8,128)(2,1)S(1)}, bf16[1,112,896]{2,1,0:T(8,128)(2,1)S(1)}, u32[]{:S(2)}, u32[]{:S(2)}) collective-permute-start(bf16[1,112,896]{2,1,0:T(8,128)(2,1)S(1)} %collective-permute-done.11.refs_12_), channel_id=1, source_target_pairs={{0,2},{1,3},{2,0},{3,1},{4,6},{5,7},{6,4},{7,5},{8,10},{9,11},{10,... | collective-permute-start | bytes 602120 | tf_op jit(solution)/shard_map/ppermute | solution.py:19
  30.5 6.4 %collective-permute-start.3 = (bf16[1,112,896]{2,1,0:T(8,128)(2,1)S(1)}, bf16[1,112,896]{2,1,0:T(8,128)(2,1)S(1)}, u32[]{:S(2)}, u32[]{:S(2)}) collective-permute-start(bf16[1,112,896]{2,1,0:T(8,128)(2,1)S(1)} %collective-permute-done.1.refs_2_), channel_id=1, source_target_pairs={{0,1},{1,0},{2,3},{3,2},{4,5},{5,4},{6,7},{7,6},{8,9},{9,8},{10,11... | collective-permute-start | bytes 602120 | tf_op jit(solution)/shard_map/ppermute | solution.py:19
  30.5 6.4 %collective-permute-start.12 = (bf16[1,112,896]{2,1,0:T(8,128)(2,1)S(1)}, bf16[1,112,896]{2,1,0:T(8,128)(2,1)S(1)}, u32[]{:S(2)}, u32[]{:S(2)}) collective-permute-start(bf16[1,112,896]{2,1,0:T(8,128)(2,1)S(1)} %collective-permute-done.11.refs_12_), channel_id=1, source_target_pairs={{0,1},{1,0},{2,3},{3,2},{4,5},{5,4},{6,7},{7,6},{8,9},{9,8},{10,11... | collective-permute-start | bytes 602120 | tf_op jit(solution)/shard_map/ppermute | solution.py:19
  31.8 5.6 %collective-permute-start.17 = (bf16[1,112,896]{2,1,0:T(8,128)(2,1)S(1)}, bf16[1,112,896]{2,1,0:T(8,128)(2,1)S(1)}, u32[]{:S(2)}, u32[]{:S(2)}) collective-permute-start(bf16[1,112,896]{2,1,0:T(8,128)(2,1)S(1)} %collective-permute-done.1.refs_2_), channel_id=1, source_target_pairs={{8,16},{16,8},{9,17},{17,9},{10,18},{18,10},{11,19},{19,11},{12,20... | collective-permute-start | bytes 602120 | tf_op jit(solution)/shard_map/ppermute | solution.py:34
  36.3 5.7 %collective-permute-start.21 = (bf16[1,112,896]{2,1,0:T(8,128)(2,1)S(1)}, bf16[1,112,896]{2,1,0:T(8,128)(2,1)S(1)}, u32[]{:S(2)}, u32[]{:S(2)}) collective-permute-start(bf16[1,112,896]{2,1,0:T(8,128)(2,1)S(1)} %collective-permute-done.19.refs_20_), channel_id=1, source_target_pairs={{0,2},{1,3},{2,0},{3,1},{4,6},{5,7},{6,4},{7,5},{8,10},{9,11},{10,... | collective-permute-start | bytes 602120 | tf_op jit(solution)/shard_map/ppermute | solution.py:19
  36.9 5.1 %collective-permute-start.14 = (bf16[1,112,896]{2,1,0:T(8,128)(2,1)S(1)}, bf16[1,112,896]{2,1,0:T(8,128)(2,1)S(1)}, u32[]{:S(2)}, u32[]{:S(2)}) collective-permute-start(bf16[1,112,896]{2,1,0:T(8,128)(2,1)S(1)} %collective-permute-done.13.refs_14_), channel_id=1, source_target_pairs={{0,1},{1,0},{2,3},{3,2},{4,5},{5,4},{6,7},{7,6},{8,9},{9,8},{10,11... | collective-permute-start | bytes 602120 | tf_op jit(solution)/shard_map/ppermute | solution.py:19
  36.9 5.1 %collective-permute-start.10 = (bf16[1,112,896]{2,1,0:T(8,128)(2,1)S(1)}, bf16[1,112,896]{2,1,0:T(8,128)(2,1)S(1)}, u32[]{:S(2)}, u32[]{:S(2)}) collective-permute-start(bf16[1,112,896]{2,1,0:T(8,128)(2,1)S(1)} %collective-permute-done.9.refs_10_), channel_id=1, source_target_pairs={{0,1},{1,0},{2,3},{3,2},{4,5},{5,4},{6,7},{7,6},{8,9},{9,8},{10,11... | collective-permute-start | bytes 602120 | tf_op jit(solution)/shard_map/ppermute | solution.py:19
  56.0 11.0 %collective-permute-start.24 = (bf16[2,1,896,896]{3,2,1,0:T(8,128)(2,1)S(1)}, bf16[2,1,896,896]{3,2,1,0:T(8,128)(2,1)S(1)}, u32[]{:S(2)}, u32[]{:S(2)}) collective-permute-start(bf16[2,1,896,896]{3,2,1,0:T(8,128)(2,1)S(1)} %copy-done), channel_id=1, source_target_pairs={{0,1},{1,0},{2,3},{3,2},{4,5},{5,4},{6,7},{7,6},{8,9},{9,8},{10,11... | collective-permute-start | bytes 9633800 | tf_op jit(solution)/shard_map/ppermute | solution.py:19
  56.2 10.8 %collective-permute-start.25 = (bf16[2,1,896,896]{3,2,1,0:T(8,128)(2,1)S(1)}, bf16[2,1,896,896]{3,2,1,0:T(8,128)(2,1)S(1)}, u32[]{:S(2)}, u32[]{:S(2)}) collective-permute-start(bf16[2,1,896,896]{3,2,1,0:T(8,128)(2,1)S(1)} %copy-done.1), channel_id=1, source_target_pairs={{0,1},{1,0},{2,3},{3,2},{4,5},{5,4},{6,7},{7,6},{8,9},{9,8},{10,11... | collective-permute-start | bytes 9633800 | tf_op jit(solution)/shard_map/ppermute | solution.py:19
  56.5 9.8 %collective-permute-start.26 = (s32[4]{0:T(128)S(1)}, s32[4]{0:T(128)S(1)}, u32[]{:S(2)}, u32[]{:S(2)}) collective-permute-start(s32[4]{0:T(128)S(1)} %bitcast.16), channel_id=1, source_target_pairs={{0,1},{1,0},{2,3},{3,2},{4,5},{5,4},{6,7},{7,6},{8,9},{9,8},{10,11... | collective-permute-start | bytes 56 | tf_op jit(solution)/shard_map/ppermute | solution.py:19
  56.7 10.3 %collective-permute-start.29 = (bf16[112,896]{1,0:T(8,128)(2,1)S(1)}, bf16[112,896]{1,0:T(8,128)(2,1)S(1)}, u32[]{:S(2)}, u32[]{:S(2)}) collective-permute-start(bf16[112,896]{1,0:T(8,128)(2,1)S(1)} %get-tuple-element.53), channel_id=1, source_target_pairs={{0,6},{1,7},{2,4},{3,5},{4,2},{5,3},{6,0},{7,1},{8,14},{9,15},{10,... | collective-permute-start | bytes 602120 | tf_op jit(solution)/shard_map/ppermute | solution.py:19
  60.1 17.4 %collective-permute-start.28 = (bf16[112,896]{1,0:T(8,128)(2,1)S(1)}, bf16[112,896]{1,0:T(8,128)(2,1)S(1)}, u32[]{:S(2)}, u32[]{:S(2)}) collective-permute-start(bf16[112,896]{1,0:T(8,128)(2,1)S(1)} %get-tuple-element.54), channel_id=1, source_target_pairs={{0,4},{1,5},{2,6},{3,7},{4,0},{5,1},{6,2},{7,3},{8,12},{9,13},{10,... | collective-permute-start | bytes 602120 | tf_op jit(solution)/shard_map/ppermute | solution.py:19
  66.4 11.3 %collective-permute-start.27 = (bf16[112,896]{1,0:T(8,128)(2,1)S(1)}, bf16[112,896]{1,0:T(8,128)(2,1)S(1)}, u32[]{:S(2)}, u32[]{:S(2)}) collective-permute-start(bf16[112,896]{1,0:T(8,128)(2,1)S(1)} %get-tuple-element.55), channel_id=1, source_target_pairs={{0,2},{1,3},{2,0},{3,1},{4,6},{5,7},{6,4},{7,5},{8,10},{9,11},{10,... | collective-permute-start | bytes 602120 | tf_op jit(solution)/shard_map/ppermute | solution.py:19
  77.9 6.9 %collective-permute-start.37 = (bf16[1,112,896]{2,1,0:T(8,128)(2,1)S(1)}, bf16[1,112,896]{2,1,0:T(8,128)(2,1)S(1)}, u32[]{:S(2)}, u32[]{:S(2)}) collective-permute-start(bf16[1,112,896]{2,1,0:T(8,128)(2,1)S(1)} %get-tuple-element.44.refs_4_), channel_id=1, source_target_pairs={{0,8},{8,0},{16,24},{24,16},{1,9},{9,1},{17,25},{25,17},{2,10},{10... | collective-permute-start | bytes 602120 | tf_op jit(solution)/shard_map/ppermute | solution.py:23
  80.0 11.6 %collective-permute-start.33 = (bf16[1,112,896]{2,1,0:T(8,128)(2,1)S(1)}, bf16[1,112,896]{2,1,0:T(8,128)(2,1)S(1)}, u32[]{:S(2)}, u32[]{:S(2)}) collective-permute-start(bf16[1,112,896]{2,1,0:T(8,128)(2,1)S(1)} %get-tuple-element.44.refs_4_), channel_id=1, source_target_pairs={{0,4},{1,5},{2,6},{3,7},{4,0},{5,1},{6,2},{7,3},{8,12},{9,13},{10,... | collective-permute-start | bytes 602120 | tf_op jit(solution)/shard_map/ppermute | solution.py:19
  81.7 10.2 %collective-permute-start.31 = (bf16[1,112,896]{2,1,0:T(8,128)(2,1)S(1)}, bf16[1,112,896]{2,1,0:T(8,128)(2,1)S(1)}, u32[]{:S(2)}, u32[]{:S(2)}) collective-permute-start(bf16[1,112,896]{2,1,0:T(8,128)(2,1)S(1)} %get-tuple-element.44.refs_4_), channel_id=1, source_target_pairs={{0,2},{1,3},{2,0},{3,1},{4,6},{5,7},{6,4},{7,5},{8,10},{9,11},{10,... | collective-permute-start | bytes 602120 | tf_op jit(solution)/shard_map/ppermute | solution.py:19
  84.2 7.8 %collective-permute-start.30 = (bf16[1,112,896]{2,1,0:T(8,128)(2,1)S(1)}, bf16[1,112,896]{2,1,0:T(8,128)(2,1)S(1)}, u32[]{:S(2)}, u32[]{:S(2)}) collective-permute-start(bf16[1,112,896]{2,1,0:T(8,128)(2,1)S(1)} %get-tuple-element.44.refs_4_), channel_id=1, source_target_pairs={{0,1},{1,0},{2,3},{3,2},{4,5},{5,4},{6,7},{7,6},{8,9},{9,8},{10,11... | collective-permute-start | bytes 602120 | tf_op jit(solution)/shard_map/ppermute | solution.py:19
  84.8 7.2 %collective-permute-start.45 = (bf16[1,112,896]{2,1,0:T(8,128)(2,1)S(1)}, bf16[1,112,896]{2,1,0:T(8,128)(2,1)S(1)}, u32[]{:S(2)}, u32[]{:S(2)}) collective-permute-start(bf16[1,112,896]{2,1,0:T(8,128)(2,1)S(1)} %collective-permute-done.37.refs_12_), channel_id=1, source_target_pairs={{0,16},{24,8},{1,17},{25,9},{2,18},{26,10},{3,19},{27,11},{4,20},{... | collective-permute-start | bytes 602120 | tf_op jit(solution)/shard_map/ppermute | solution.py:29
  88.5 5.7 %collective-permute-start.38 = (bf16[1,112,896]{2,1,0:T(8,128)(2,1)S(1)}, bf16[1,112,896]{2,1,0:T(8,128)(2,1)S(1)}, u32[]{:S(2)}, u32[]{:S(2)}) collective-permute-start(bf16[1,112,896]{2,1,0:T(8,128)(2,1)S(1)} %collective-permute-done.37.refs_12_), channel_id=1, source_target_pairs={{0,1},{1,0},{2,3},{3,2},{4,5},{5,4},{6,7},{7,6},{8,9},{9,8},{10,11... | collective-permute-start | bytes 602120 | tf_op jit(solution)/shard_map/ppermute | solution.py:19
  91.6 7.9 %collective-permute-start.41 = (bf16[1,112,896]{2,1,0:T(8,128)(2,1)S(1)}, bf16[1,112,896]{2,1,0:T(8,128)(2,1)S(1)}, u32[]{:S(2)}, u32[]{:S(2)}) collective-permute-start(bf16[1,112,896]{2,1,0:T(8,128)(2,1)S(1)} %collective-permute-done.33.refs_8_), channel_id=1, source_target_pairs={{0,8},{8,0},{16,24},{24,16},{1,9},{9,1},{17,25},{25,17},{2,10},{10... | collective-permute-start | bytes 602120 | tf_op jit(solution)/shard_map/ppermute | solution.py:23
  92.0 9.3 %collective-permute-start.35 = (bf16[1,112,896]{2,1,0:T(8,128)(2,1)S(1)}, bf16[1,112,896]{2,1,0:T(8,128)(2,1)S(1)}, u32[]{:S(2)}, u32[]{:S(2)}) collective-permute-start(bf16[1,112,896]{2,1,0:T(8,128)(2,1)S(1)} %collective-permute-done.33.refs_8_), channel_id=1, source_target_pairs={{0,2},{1,3},{2,0},{3,1},{4,6},{5,7},{6,4},{7,5},{8,10},{9,11},{10,... | collective-permute-start | bytes 602120 | tf_op jit(solution)/shard_map/ppermute | solution.py:19
  92.0 9.4 %collective-permute-start.34 = (bf16[1,112,896]{2,1,0:T(8,128)(2,1)S(1)}, bf16[1,112,896]{2,1,0:T(8,128)(2,1)S(1)}, u32[]{:S(2)}, u32[]{:S(2)}) collective-permute-start(bf16[1,112,896]{2,1,0:T(8,128)(2,1)S(1)} %collective-permute-done.33.refs_8_), channel_id=1, source_target_pairs={{0,1},{1,0},{2,3},{3,2},{4,5},{5,4},{6,7},{7,6},{8,9},{9,8},{10,11... | collective-permute-start | bytes 602120 | tf_op jit(solution)/shard_map/ppermute | solution.py:19
  92.1 10.0 %collective-permute-start.39 = (bf16[1,112,896]{2,1,0:T(8,128)(2,1)S(1)}, bf16[1,112,896]{2,1,0:T(8,128)(2,1)S(1)}, u32[]{:S(2)}, u32[]{:S(2)}) collective-permute-start(bf16[1,112,896]{2,1,0:T(8,128)(2,1)S(1)} %collective-permute-done.31.refs_6_), channel_id=1, source_target_pairs={{0,8},{8,0},{16,24},{24,16},{1,9},{9,1},{17,25},{25,17},{2,10},{10... | collective-permute-start | bytes 602120 | tf_op jit(solution)/shard_map/ppermute | solution.py:23
  94.2 7.9 %collective-permute-start.32 = (bf16[1,112,896]{2,1,0:T(8,128)(2,1)S(1)}, bf16[1,112,896]{2,1,0:T(8,128)(2,1)S(1)}, u32[]{:S(2)}, u32[]{:S(2)}) collective-permute-start(bf16[1,112,896]{2,1,0:T(8,128)(2,1)S(1)} %collective-permute-done.31.refs_6_), channel_id=1, source_target_pairs={{0,1},{1,0},{2,3},{3,2},{4,5},{5,4},{6,7},{7,6},{8,9},{9,8},{10,11... | collective-permute-start | bytes 602120 | tf_op jit(solution)/shard_map/ppermute | solution.py:19
  99.5 5.0 %collective-permute-start.49 = (bf16[1,112,896]{2,1,0:T(8,128)(2,1)S(1)}, bf16[1,112,896]{2,1,0:T(8,128)(2,1)S(1)}, u32[]{:S(2)}, u32[]{:S(2)}) collective-permute-start(bf16[1,112,896]{2,1,0:T(8,128)(2,1)S(1)} %collective-permute-done.41.refs_16_), channel_id=1, source_target_pairs={{0,16},{24,8},{1,17},{25,9},{2,18},{26,10},{3,19},{27,11},{4,20},{... | collective-permute-start | bytes 602120 | tf_op jit(solution)/shard_map/ppermute | solution.py:29
  101.3 6.6 %collective-permute-start.43 = (bf16[1,112,896]{2,1,0:T(8,128)(2,1)S(1)}, bf16[1,112,896]{2,1,0:T(8,128)(2,1)S(1)}, u32[]{:S(2)}, u32[]{:S(2)}) collective-permute-start(bf16[1,112,896]{2,1,0:T(8,128)(2,1)S(1)} %collective-permute-done.41.refs_16_), channel_id=1, source_target_pairs={{0,2},{1,3},{2,0},{3,1},{4,6},{5,7},{6,4},{7,5},{8,10},{9,11},{10,... | collective-permute-start | bytes 602120 | tf_op jit(solution)/shard_map/ppermute | solution.py:19
  101.4 6.5 %collective-permute-start.46 = (bf16[1,112,896]{2,1,0:T(8,128)(2,1)S(1)}, bf16[1,112,896]{2,1,0:T(8,128)(2,1)S(1)}, u32[]{:S(2)}, u32[]{:S(2)}) collective-permute-start(bf16[1,112,896]{2,1,0:T(8,128)(2,1)S(1)} %collective-permute-done.45.refs_20_), channel_id=1, source_target_pairs={{0,1},{1,0},{2,3},{3,2},{4,5},{5,4},{6,7},{7,6},{8,9},{9,8},{10,11... | collective-permute-start | bytes 602120 | tf_op jit(solution)/shard_map/ppermute | solution.py:19
  102.1 5.9 %collective-permute-start.42 = (bf16[1,112,896]{2,1,0:T(8,128)(2,1)S(1)}, bf16[1,112,896]{2,1,0:T(8,128)(2,1)S(1)}, u32[]{:S(2)}, u32[]{:S(2)}) collective-permute-start(bf16[1,112,896]{2,1,0:T(8,128)(2,1)S(1)} %collective-permute-done.41.refs_16_), channel_id=1, source_target_pairs={{0,1},{1,0},{2,3},{3,2},{4,5},{5,4},{6,7},{7,6},{8,9},{9,8},{10,11... | collective-permute-start | bytes 602120 | tf_op jit(solution)/shard_map/ppermute | solution.py:19
  102.1 6.4 %collective-permute-start.36 = (bf16[1,112,896]{2,1,0:T(8,128)(2,1)S(1)}, bf16[1,112,896]{2,1,0:T(8,128)(2,1)S(1)}, u32[]{:S(2)}, u32[]{:S(2)}) collective-permute-start(bf16[1,112,896]{2,1,0:T(8,128)(2,1)S(1)} %collective-permute-done.35.refs_10_), channel_id=1, source_target_pairs={{0,1},{1,0},{2,3},{3,2},{4,5},{5,4},{6,7},{7,6},{8,9},{9,8},{10,11... | collective-permute-start | bytes 602120 | tf_op jit(solution)/shard_map/ppermute | solution.py:19
  107.9 5.7 %collective-permute-start.51 = (bf16[1,112,896]{2,1,0:T(8,128)(2,1)S(1)}, bf16[1,112,896]{2,1,0:T(8,128)(2,1)S(1)}, u32[]{:S(2)}, u32[]{:S(2)}) collective-permute-start(bf16[1,112,896]{2,1,0:T(8,128)(2,1)S(1)} %collective-permute-done.49.refs_24_), channel_id=1, source_target_pairs={{0,2},{1,3},{2,0},{3,1},{4,6},{5,7},{6,4},{7,5},{8,10},{9,11},{10,... | collective-permute-start | bytes 602120 | tf_op jit(solution)/shard_map/ppermute | solution.py:19
  107.9 5.7 %collective-permute-start.40 = (bf16[1,112,896]{2,1,0:T(8,128)(2,1)S(1)}, bf16[1,112,896]{2,1,0:T(8,128)(2,1)S(1)}, u32[]{:S(2)}, u32[]{:S(2)}) collective-permute-start(bf16[1,112,896]{2,1,0:T(8,128)(2,1)S(1)} %collective-permute-done.39.refs_14_), channel_id=1, source_target_pairs={{0,1},{1,0},{2,3},{3,2},{4,5},{5,4},{6,7},{7,6},{8,9},{9,8},{10,11... | collective-permute-start | bytes 602120 | tf_op jit(solution)/shard_map/ppermute | solution.py:19
  107.9 5.7 %collective-permute-start.44 = (bf16[1,112,896]{2,1,0:T(8,128)(2,1)S(1)}, bf16[1,112,896]{2,1,0:T(8,128)(2,1)S(1)}, u32[]{:S(2)}, u32[]{:S(2)}) collective-permute-start(bf16[1,112,896]{2,1,0:T(8,128)(2,1)S(1)} %collective-permute-done.43.refs_18_), channel_id=1, source_target_pairs={{0,1},{1,0},{2,3},{3,2},{4,5},{5,4},{6,7},{7,6},{8,9},{9,8},{10,11... | collective-permute-start | bytes 602120 | tf_op jit(solution)/shard_map/ppermute | solution.py:19
  108.4 5.2 %collective-permute-start.50 = (bf16[1,112,896]{2,1,0:T(8,128)(2,1)S(1)}, bf16[1,112,896]{2,1,0:T(8,128)(2,1)S(1)}, u32[]{:S(2)}, u32[]{:S(2)}) collective-permute-start(bf16[1,112,896]{2,1,0:T(8,128)(2,1)S(1)} %collective-permute-done.49.refs_24_), channel_id=1, source_target_pairs={{0,1},{1,0},{2,3},{3,2},{4,5},{5,4},{6,7},{7,6},{8,9},{9,8},{10,11... | collective-permute-start | bytes 602120 | tf_op jit(solution)/shard_map/ppermute | solution.py:19
  108.5 5.1 %collective-permute-start.48 = (bf16[1,112,896]{2,1,0:T(8,128)(2,1)S(1)}, bf16[1,112,896]{2,1,0:T(8,128)(2,1)S(1)}, u32[]{:S(2)}, u32[]{:S(2)}) collective-permute-start(bf16[1,112,896]{2,1,0:T(8,128)(2,1)S(1)} %collective-permute-done.47.refs_22_), channel_id=1, source_target_pairs={{0,1},{1,0},{2,3},{3,2},{4,5},{5,4},{6,7},{7,6},{8,9},{9,8},{10,11... | collective-permute-start | bytes 602120 | tf_op jit(solution)/shard_map/ppermute | solution.py:19
  124.9 9.8 %collective-permute-start.53 = (bf16[112,896]{1,0:T(8,128)(2,1)S(1)}, bf16[112,896]{1,0:T(8,128)(2,1)S(1)}, u32[]{:S(2)}, u32[]{:S(2)}) collective-permute-start(bf16[112,896]{1,0:T(8,128)(2,1)S(1)} %get-tuple-element.48), channel_id=1, source_target_pairs={{0,6},{1,7},{2,4},{3,5},{4,2},{5,3},{6,0},{7,1},{8,14},{9,15},{10,... | collective-permute-start | bytes 602120 | tf_op jit(solution)/shard_map/ppermute | solution.py:19
  126.6 17.7 %collective-permute-start.54 = (bf16[112,896]{1,0:T(8,128)(2,1)S(1)}, bf16[112,896]{1,0:T(8,128)(2,1)S(1)}, u32[]{:S(2)}, u32[]{:S(2)}) collective-permute-start(bf16[112,896]{1,0:T(8,128)(2,1)S(1)} %get-tuple-element.49), channel_id=1, source_target_pairs={{0,4},{1,5},{2,6},{3,7},{4,0},{5,1},{6,2},{7,3},{8,12},{9,13},{10,... | collective-permute-start | bytes 602120 | tf_op jit(solution)/shard_map/ppermute | solution.py:19
  126.6 17.7 %collective-permute-start.55 = (bf16[112,896]{1,0:T(8,128)(2,1)S(1)}, bf16[112,896]{1,0:T(8,128)(2,1)S(1)}, u32[]{:S(2)}, u32[]{:S(2)}) collective-permute-start(bf16[112,896]{1,0:T(8,128)(2,1)S(1)} %get-tuple-element.50), channel_id=1, source_target_pairs={{0,2},{1,3},{2,0},{3,1},{4,6},{5,7},{6,4},{7,5},{8,10},{9,11},{10,... | collective-permute-start | bytes 602120 | tf_op jit(solution)/shard_map/ppermute | solution.py:19
  (12 other events, 97.4 us)

commit v5 on v4

--- a/solution.py
+++ b/solution.py
@@ -40,12 +40,12 @@
 
 FIRST = {
     "routes": {},
-    "after": {"B1": ("p3",), "cA3": ("A1",), "p1": ("p2",)},
+    "after": {"B1": ("p3",)},
     "order": (),
 }
 SECOND = {
     "routes": {"B0": ("A0", "forward")},
-    "after": {"B1": ("p3",), "cA3": ("A1",)},
+    "after": {"B1": ("A2",), "cA3": ("A1",)},
     "order": (),
 }
 

time: 158 us -> 156 us (0.987)
  waiting for transfers between devices: 71.8 us -> 66.2 us
  starting transfers between devices: 47.7 us -> 50.3 us
    ppermute x44, waiting for transfers between devices: 59.1 us -> 51.8 us  [along_term(): return lax.ppermute(x, 'term', [(i, partner(i)) for i in range(count)])]
    ppermute x6, starting transfers between devices: 11.8 us -> 14.4 us  [pair_exchange(): lax.ppermute(x, 'sec', [(i, i ^ 1) for i in range(count) if i ^ 1 < count])]
    ppermute x6, waiting for transfers between devices: 9.28 us -> 11 us  [pair_exchange(): lax.ppermute(x, 'sec', [(i, i ^ 1) for i in range(count) if i ^ 1 < count])]
where the time goes in v5:
time: 156 us
  waiting for transfers between devices  66.2 us (42%)
  starting transfers between devices  50.3 us (32%)
  Pallas kernels  21.3 us (14%)
  blocking collectives  13.1 us (8%)
  between operations  2.38 us (2%)
  other arithmetic  1.87 us (1%)
    ppermute x44, waiting for transfers between devices, along_term(): return lax.ppermute(x, 'term', [(i, partner(i)) for i in range(count)])  51.8 us
    ppermute x44, starting transfers between devices, along_term(): return lax.ppermute(x, 'term', [(i, partner(i)) for i in range(count)])  25.6 us
    ppermute x6, starting transfers between devices, pair_exchange(): lax.ppermute(x, 'sec', [(i, i ^ 1) for i in range(count) if i ^ 1 < count])  14.4 us
    all_to_all x1, blocking collectives, everyones(): lax.all_to_all(jnp.broadcast_to(tile, (count,) + tile.shape), ('sec', 'te...  13.1 us
    ppermute x6, waiting for transfers between devices, pair_exchange(): lax.ppermute(x, 'sec', [(i, i ^ 1) for i in range(count) if i ^ 1 < count])  11 us
    pallas_call x1, Pallas kernels, apply_terms(): pl.pallas_call(functools.partial(apply_kernel, chips, terms, rows, order)...  9.94 us
    pallas_call x1, Pallas kernels, apply_chip_terms(): pl.pallas_call(functools.partial(chip_kernel, chips, terms, rows, order),...  9.83 us
    ppermute x3, starting transfers between devices, pair_forward(): return lax.ppermute(x, 'sec', pairs)  8.19 us
  transfers between devices with their start and end apart: 56, of which 22 were waited for; matrix products, arithmetic and copies ran while one was open for 1% of the time, Pallas kernels for 0%

profile of v5, /device:TPU:0, one launch (start us, length us, event | category | flops | bytes accessed | tf_op | source)
XLA Modules:
  0.0 155.9 jit_solution(1222357584678379476)
XLA Ops:
  2.0 1.1 and_select_fusion.refs_0_.x_ref
  3.0 4.1 %collective-permute-start.3 = (bf16[1,112,896]{2,1,0:T(8,128)(2,1)S(1)}, bf16[1,112,896]{2,1,0:T(8,128)(2,1)S(1)}, u32[]{:S(2)}, u32[]{:S(2)}) collective-permute-start(bf16[1,112,896]{2,1,0:T(8,128)(2,1)S(1)} %and_select_fusion.refs_0_.x_ref), channel_id=1, source_target_pairs={{0,4},{1,5},{2,6},{3,7},{4,0},{5,1},{6,2},{7,3},{8,12},{9,13},{10,... | collective-permute-start | bytes 602120 | tf_op jit(solution)/shard_map/ppermute | solution.py:19
  7.1 0.7 collective-permute-start.15
  7.8 1.6 %collective-permute-start = (bf16[1,112,896]{2,1,0:T(8,128)(2,1)S(1)}, bf16[1,112,896]{2,1,0:T(8,128)(2,1)S(1)}, u32[]{:S(2)}, u32[]{:S(2)}) collective-permute-start(bf16[1,112,896]{2,1,0:T(8,128)(2,1)S(1)} %and_select_fusion.refs_0_.x_ref), channel_id=1, source_target_pairs={{0,2},{1,3},{2,0},{3,1},{4,6},{5,7},{6,4},{7,5},{8,10},{9,11},{10,... | collective-permute-start | bytes 602120 | tf_op jit(solution)/shard_map/ppermute | solution.py:19
  9.4 4.2 %collective-permute-start.7 = (bf16[1,112,896]{2,1,0:T(8,128)(2,1)S(1)}, bf16[1,112,896]{2,1,0:T(8,128)(2,1)S(1)}, u32[]{:S(2)}, u32[]{:S(2)}) collective-permute-start(bf16[1,112,896]{2,1,0:T(8,128)(2,1)S(1)} %and_select_fusion.refs_0_.x_ref), channel_id=1, source_target_pairs={{0,8},{8,0},{16,24},{24,16},{1,9},{9,1},{17,25},{25,17},{2,10},{10... | collective-permute-start | bytes 602120 | tf_op jit(solution)/shard_map/ppermute | solution.py:23
  13.7 2.9 %collective-permute-done.3.refs_4_ = bf16[1,112,896]{2,1,0:T(8,128)(2,1)S(1)} collective-permute-done((bf16[1,112,896]{2,1,0:T(8,128)(2,1)S(1)}, bf16[1,112,896]{2,1,0:T(8,128)(2,1)S(1)}, u32[]{:S(2)}, u32[]{:S(2)}) %collective-permute-start.3) | collective-permute-done | bytes 200736 | tf_op jit(solution)/shard_map/ppermute | solution.py:19
  16.5 1.5 collective-permute-start.11
  19.3 0.7 concatenate.3.scal
  20.1 2.1 %collective-permute-done.7.refs_8_ = bf16[1,112,896]{2,1,0:T(8,128)(2,1)S(1)} collective-permute-done((bf16[1,112,896]{2,1,0:T(8,128)(2,1)S(1)}, bf16[1,112,896]{2,1,0:T(8,128)(2,1)S(1)}, u32[]{:S(2)}, u32[]{:S(2)}) %collective-permute-start.7) | collective-permute-done | bytes 200736 | tf_op jit(solution)/shard_map/ppermute | solution.py:23
  22.7 1.6 %collective-permute-start.9 = (bf16[1,112,896]{2,1,0:T(8,128)(2,1)S(1)}, bf16[1,112,896]{2,1,0:T(8,128)(2,1)S(1)}, u32[]{:S(2)}, u32[]{:S(2)}) collective-permute-start(bf16[1,112,896]{2,1,0:T(8,128)(2,1)S(1)} %collective-permute-done.refs_2_), channel_id=1, source_target_pairs={{0,8},{8,0},{16,24},{24,16},{1,9},{9,1},{17,25},{25,17},{2,10},{10... | collective-permute-start | bytes 602120 | tf_op jit(solution)/shard_map/ppermute | solution.py:23
  24.3 0.7 collective-permute-done.11.refs_12_
  25.0 2.6 %collective-permute-start.19 = (bf16[1,112,896]{2,1,0:T(8,128)(2,1)S(1)}, bf16[1,112,896]{2,1,0:T(8,128)(2,1)S(1)}, u32[]{:S(2)}, u32[]{:S(2)}) collective-permute-start(bf16[1,112,896]{2,1,0:T(8,128)(2,1)S(1)} %collective-permute-done.11.refs_12_), channel_id=1, source_target_pairs={{0,16},{24,8},{1,17},{25,9},{2,18},{26,10},{3,19},{27,11},{4,20},{... | collective-permute-start | bytes 602120 | tf_op jit(solution)/shard_map/ppermute | solution.py:29
  27.6 1.2 collective-permute-start.13
  28.8 1.1 collective-permute-done.9.refs_10_
  29.9 0.7 collective-permute-start.17
  30.6 0.9 collective-permute-done.19.refs_20_
  31.5 1.6 %collective-permute-start.21 = (bf16[1,112,896]{2,1,0:T(8,128)(2,1)S(1)}, bf16[1,112,896]{2,1,0:T(8,128)(2,1)S(1)}, u32[]{:S(2)}, u32[]{:S(2)}) collective-permute-start(bf16[1,112,896]{2,1,0:T(8,128)(2,1)S(1)} %collective-permute-done.19.refs_20_), channel_id=1, source_target_pairs={{0,2},{1,3},{2,0},{3,1},{4,6},{5,7},{6,4},{7,5},{8,10},{9,11},{10,... | collective-permute-start | bytes 602120 | tf_op jit(solution)/shard_map/ppermute | solution.py:19
  33.1 0.7 collective-permute-done.13.refs_14_
  34.8 3.3 %collective-permute-done.21.refs_22_ = bf16[1,112,896]{2,1,0:T(8,128)(2,1)S(1)} collective-permute-done((bf16[1,112,896]{2,1,0:T(8,128)(2,1)S(1)}, bf16[1,112,896]{2,1,0:T(8,128)(2,1)S(1)}, u32[]{:S(2)}, u32[]{:S(2)}) %collective-permute-start.21) | collective-permute-done | bytes 200736 | tf_op jit(solution)/shard_map/ppermute | solution.py:19
  38.1 1.4 collective-permute-done.22.refs_23_
  39.6 9.9 %apply_terms.1 = (f32[4,112,896]{2,1,0:T(8,128)S(1)}, bf16[4,112,896]{2,1,0:T(8,128)(2,1)S(1)}) custom-call(s32[8]{0:T(128)S(1)} %concatenate.3.scal, bf16[2,1,896,896]{3,2,1,0:T(8,128)(2,1)} %refs_0_.1, bf16[2,1,896,896]{3,2,1,0:T(8,128)(2,1)} %refs_2_.1, bf16[1,112,896]{2,1,0:T(8,128)(2,1)S(1)} %and_select_fusion.refs_0_.x_ref, ...), custom_call_target="tpu_custom_call" | custom-call | tf_op jit(solution)/shard_map/apply_terms/pallas_call | solution.py:163
  49.7 2.2 %collective-permute-done.23 = bf16[4,112,896]{2,1,0:T(8,128)(2,1)S(1)} collective-permute-done((bf16[4,112,896]{2,1,0:T(8,128)(2,1)S(1)}, bf16[4,112,896]{2,1,0:T(8,128)(2,1)S(1)}, u32[]{:S(2)}, u32[]{:S(2)}) %collective-permute-start.23) | collective-permute-done | bytes 802848 | tf_op jit(solution)/shard_map/ppermute | solution.py:19
  52.8 3.7 %collective-permute-start.29 = (bf16[112,896]{1,0:T(8,128)(2,1)S(1)}, bf16[112,896]{1,0:T(8,128)(2,1)S(1)}, u32[]{:S(2)}, u32[]{:S(2)}) collective-permute-start(bf16[112,896]{1,0:T(8,128)(2,1)S(1)} %get-tuple-element.49), channel_id=1, source_target_pairs={{0,6},{1,7},{2,4},{3,5},{4,2},{5,3},{6,0},{7,1},{8,14},{9,15},{10,... | collective-permute-start | bytes 602120 | tf_op jit(solution)/shard_map/ppermute | solution.py:19
  56.5 5.9 %collective-permute-done.26.theirs = s32[4]{0:T(128)S(1)} collective-permute-done((s32[4]{0:T(128)S(1)}, s32[4]{0:T(128)S(1)}, u32[]{:S(2)}, u32[]{:S(2)}) %collective-permute-start.26) | collective-permute-done | bytes 48 | tf_op jit(solution)/shard_map/ppermute | solution.py:19
  62.5 1.6 %collective-permute-start.27 = (bf16[112,896]{1,0:T(8,128)(2,1)S(1)}, bf16[112,896]{1,0:T(8,128)(2,1)S(1)}, u32[]{:S(2)}, u32[]{:S(2)}) collective-permute-start(bf16[112,896]{1,0:T(8,128)(2,1)S(1)} %get-tuple-element.51), channel_id=1, source_target_pairs={{0,2},{1,3},{2,0},{3,1},{4,6},{5,7},{6,4},{7,5},{8,10},{9,11},{10,... | collective-permute-start | bytes 602120 | tf_op jit(solution)/shard_map/ppermute | solution.py:19
  64.1 9.9 %collective-permute-done.28.refs_1_ = bf16[112,896]{1,0:T(8,128)(2,1)S(1)} collective-permute-done((bf16[112,896]{1,0:T(8,128)(2,1)S(1)}, bf16[112,896]{1,0:T(8,128)(2,1)S(1)}, u32[]{:S(2)}, u32[]{:S(2)}) %collective-permute-start.28) | collective-permute-done | bytes 200736 | tf_op jit(solution)/shard_map/ppermute | solution.py:19
  74.2 4.0 %collective-permute-start.37 = (bf16[1,112,896]{2,1,0:T(8,128)(2,1)S(1)}, bf16[1,112,896]{2,1,0:T(8,128)(2,1)S(1)}, u32[]{:S(2)}, u32[]{:S(2)}) collective-permute-start(bf16[1,112,896]{2,1,0:T(8,128)(2,1)S(1)} %get-tuple-element.40.refs_4_), channel_id=1, source_target_pairs={{0,8},{8,0},{16,24},{24,16},{1,9},{9,1},{17,25},{25,17},{2,10},{10... | collective-permute-start | bytes 602120 | tf_op jit(solution)/shard_map/ppermute | solution.py:23
  78.2 2.4 %collective-permute-start.31 = (bf16[1,112,896]{2,1,0:T(8,128)(2,1)S(1)}, bf16[1,112,896]{2,1,0:T(8,128)(2,1)S(1)}, u32[]{:S(2)}, u32[]{:S(2)}) collective-permute-start(bf16[1,112,896]{2,1,0:T(8,128)(2,1)S(1)} %get-tuple-element.40.refs_4_), channel_id=1, source_target_pairs={{0,2},{1,3},{2,0},{3,1},{4,6},{5,7},{6,4},{7,5},{8,10},{9,11},{10,... | collective-permute-start | bytes 602120 | tf_op jit(solution)/shard_map/ppermute | solution.py:19
  80.6 2.1 %collective-permute-done.37.refs_12_ = bf16[1,112,896]{2,1,0:T(8,128)(2,1)S(1)} collective-permute-done((bf16[1,112,896]{2,1,0:T(8,128)(2,1)S(1)}, bf16[1,112,896]{2,1,0:T(8,128)(2,1)S(1)}, u32[]{:S(2)}, u32[]{:S(2)}) %collective-permute-start.37) | collective-permute-done | bytes 200736 | tf_op jit(solution)/shard_map/ppermute | solution.py:23
  82.8 3.6 %collective-permute-start.45 = (bf16[1,112,896]{2,1,0:T(8,128)(2,1)S(1)}, bf16[1,112,896]{2,1,0:T(8,128)(2,1)S(1)}, u32[]{:S(2)}, u32[]{:S(2)}) collective-permute-start(bf16[1,112,896]{2,1,0:T(8,128)(2,1)S(1)} %collective-permute-done.37.refs_12_), channel_id=1, source_target_pairs={{0,16},{24,8},{1,17},{25,9},{2,18},{26,10},{3,19},{27,11},{4,20},{... | collective-permute-start | bytes 602120 | tf_op jit(solution)/shard_map/ppermute | solution.py:29
  86.4 2.0 %collective-permute-done.33.refs_8_ = bf16[1,112,896]{2,1,0:T(8,128)(2,1)S(1)} collective-permute-done((bf16[1,112,896]{2,1,0:T(8,128)(2,1)S(1)}, bf16[1,112,896]{2,1,0:T(8,128)(2,1)S(1)}, u32[]{:S(2)}, u32[]{:S(2)}) %collective-permute-start.33) | collective-permute-done | bytes 200736 | tf_op jit(solution)/shard_map/ppermute | solution.py:19
  88.9 0.7 collective-permute-done.45.refs_20_
  89.5 2.6 %collective-permute-start.39 = (bf16[1,112,896]{2,1,0:T(8,128)(2,1)S(1)}, bf16[1,112,896]{2,1,0:T(8,128)(2,1)S(1)}, u32[]{:S(2)}, u32[]{:S(2)}) collective-permute-start(bf16[1,112,896]{2,1,0:T(8,128)(2,1)S(1)} %collective-permute-done.31.refs_6_), channel_id=1, source_target_pairs={{0,8},{8,0},{16,24},{24,16},{1,9},{9,1},{17,25},{25,17},{2,10},{10... | collective-permute-start | bytes 602120 | tf_op jit(solution)/shard_map/ppermute | solution.py:23
  92.1 4.2 %collective-permute-done.41.refs_16_ = bf16[1,112,896]{2,1,0:T(8,128)(2,1)S(1)} collective-permute-done((bf16[1,112,896]{2,1,0:T(8,128)(2,1)S(1)}, bf16[1,112,896]{2,1,0:T(8,128)(2,1)S(1)}, u32[]{:S(2)}, u32[]{:S(2)}) %collective-permute-start.41) | collective-permute-done | bytes 200736 | tf_op jit(solution)/shard_map/ppermute | solution.py:23
  96.3 2.1 %collective-permute-start.49 = (bf16[1,112,896]{2,1,0:T(8,128)(2,1)S(1)}, bf16[1,112,896]{2,1,0:T(8,128)(2,1)S(1)}, u32[]{:S(2)}, u32[]{:S(2)}) collective-permute-start(bf16[1,112,896]{2,1,0:T(8,128)(2,1)S(1)} %collective-permute-done.41.refs_16_), channel_id=1, source_target_pairs={{0,16},{24,8},{1,17},{25,9},{2,18},{26,10},{3,19},{27,11},{4,20},{... | collective-permute-start | bytes 602120 | tf_op jit(solution)/shard_map/ppermute | solution.py:29
  98.5 0.8 collective-permute-done.39.refs_14_
  99.8 1.7 %collective-permute-done.49.refs_24_ = bf16[1,112,896]{2,1,0:T(8,128)(2,1)S(1)} collective-permute-done((bf16[1,112,896]{2,1,0:T(8,128)(2,1)S(1)}, bf16[1,112,896]{2,1,0:T(8,128)(2,1)S(1)}, u32[]{:S(2)}, u32[]{:S(2)}) %collective-permute-start.49) | collective-permute-done | bytes 200736 | tf_op jit(solution)/shard_map/ppermute | solution.py:29
  101.5 0.8 collective-permute-start.47
  102.4 2.5 %collective-permute-done.43.refs_18_ = bf16[1,112,896]{2,1,0:T(8,128)(2,1)S(1)} collective-permute-done((bf16[1,112,896]{2,1,0:T(8,128)(2,1)S(1)}, bf16[1,112,896]{2,1,0:T(8,128)(2,1)S(1)}, u32[]{:S(2)}, u32[]{:S(2)}) %collective-permute-start.43) | collective-permute-done | bytes 200736 | tf_op jit(solution)/shard_map/ppermute | solution.py:19
  105.9 4.7 %collective-permute-done.51.refs_26_ = bf16[1,112,896]{2,1,0:T(8,128)(2,1)S(1)} collective-permute-done((bf16[1,112,896]{2,1,0:T(8,128)(2,1)S(1)}, bf16[1,112,896]{2,1,0:T(8,128)(2,1)S(1)}, u32[]{:S(2)}, u32[]{:S(2)}) %collective-permute-start.51) | collective-permute-done | bytes 200736 | tf_op jit(solution)/shard_map/ppermute | solution.py:19
  110.6 1.4 collective-permute-done.52.refs_27_
  112.0 9.8 %apply_chip_terms.1 = (f32[112,896]{1,0:T(8,128)S(1)}, bf16[112,896]{1,0:T(8,128)(2,1)S(1)}, bf16[112,896]{1,0:T(8,128)(2,1)S(1)}, bf16[112,896]{1,0:T(8,128)(2,1)S(1)}) custom-call(s32[8]{0:T(128)S(1)} %concatenate.3.scal, s32[4]{0:T(128)S(1)} %collective-permute-done.26.theirs, bf16[2,1,896,896]{3,2,1,0:T(8,128)(2,1)} %refs_0_.1, ...), custom_call_target="tpu_custom_call" | custom-call | tf_op jit(solution)/shard_map/apply_chip_terms/pallas_call | solution.py:245
  121.9 2.3 %collective-permute-start.53 = (bf16[112,896]{1,0:T(8,128)(2,1)S(1)}, bf16[112,896]{1,0:T(8,128)(2,1)S(1)}, u32[]{:S(2)}, u32[]{:S(2)}) collective-permute-start(bf16[112,896]{1,0:T(8,128)(2,1)S(1)} %get-tuple-element.44), channel_id=1, source_target_pairs={{0,6},{1,7},{2,4},{3,5},{4,2},{5,3},{6,0},{7,1},{8,14},{9,15},{10,... | collective-permute-start | bytes 602120 | tf_op jit(solution)/shard_map/ppermute | solution.py:19
  124.2 2.1 %collective-permute-start.55 = (bf16[112,896]{1,0:T(8,128)(2,1)S(1)}, bf16[112,896]{1,0:T(8,128)(2,1)S(1)}, u32[]{:S(2)}, u32[]{:S(2)}) collective-permute-start(bf16[112,896]{1,0:T(8,128)(2,1)S(1)} %get-tuple-element.46), channel_id=1, source_target_pairs={{0,2},{1,3},{2,0},{3,1},{4,6},{5,7},{6,4},{7,5},{8,10},{9,11},{10,... | collective-permute-start | bytes 602120 | tf_op jit(solution)/shard_map/ppermute | solution.py:19
  126.3 5.4 %collective-permute-done.53.refs_0_ = bf16[112,896]{1,0:T(8,128)(2,1)S(1)} collective-permute-done((bf16[112,896]{1,0:T(8,128)(2,1)S(1)}, bf16[112,896]{1,0:T(8,128)(2,1)S(1)}, u32[]{:S(2)}, u32[]{:S(2)}) %collective-permute-start.53) | collective-permute-done | bytes 200736 | tf_op jit(solution)/shard_map/ppermute | solution.py:19
  131.7 9.6 %collective-permute-done.54.refs_1_ = bf16[112,896]{1,0:T(8,128)(2,1)S(1)} collective-permute-done((bf16[112,896]{1,0:T(8,128)(2,1)S(1)}, bf16[112,896]{1,0:T(8,128)(2,1)S(1)}, u32[]{:S(2)}, u32[]{:S(2)}) %collective-permute-start.54) | collective-permute-done | bytes 200736 | tf_op jit(solution)/shard_map/ppermute | solution.py:19
  141.5 13.1 %all_to_all.5.tiles = f32[32,8,128]{2,1,0:T(8,128)S(1)} all-to-all(f32[32,8,128]{2,1,0:T(8,128)S(1)} %broadcast_in_dim.19), channel_id=1, replica_groups=mesh['sec'=4,'term'=8] {'sec','term'}, dimensions={0} | all-to-all | bytes 262144 | tf_op jit(solution)/shard_map/all_to_all | solution.py:284
  154.6 1.1 finish.1
  (85 shorter events, 6.7 us)
Async XLA Ops:
  3.0 13.5 %collective-permute-start.3 = (bf16[1,112,896]{2,1,0:T(8,128)(2,1)S(1)}, bf16[1,112,896]{2,1,0:T(8,128)(2,1)S(1)}, u32[]{:S(2)}, u32[]{:S(2)}) collective-permute-start(bf16[1,112,896]{2,1,0:T(8,128)(2,1)S(1)} %and_select_fusion.refs_0_.x_ref), channel_id=1, source_target_pairs={{0,4},{1,5},{2,6},{3,7},{4,0},{5,1},{6,2},{7,3},{8,12},{9,13},{10,... | collective-permute-start | bytes 602120 | tf_op jit(solution)/shard_map/ppermute | solution.py:19
  7.1 10.9 %collective-permute-start.15 = (bf16[1,112,896]{2,1,0:T(8,128)(2,1)S(1)}, bf16[1,112,896]{2,1,0:T(8,128)(2,1)S(1)}, u32[]{:S(2)}, u32[]{:S(2)}) collective-permute-start(bf16[1,112,896]{2,1,0:T(8,128)(2,1)S(1)} %and_select_fusion.refs_0_.x_ref), channel_id=1, source_target_pairs={{8,16},{16,8},{9,17},{17,9},{10,18},{18,10},{11,19},{19,11},{12,20... | collective-permute-start | bytes 602120 | tf_op jit(solution)/shard_map/ppermute | solution.py:34
  7.8 10.9 %collective-permute-start = (bf16[1,112,896]{2,1,0:T(8,128)(2,1)S(1)}, bf16[1,112,896]{2,1,0:T(8,128)(2,1)S(1)}, u32[]{:S(2)}, u32[]{:S(2)}) collective-permute-start(bf16[1,112,896]{2,1,0:T(8,128)(2,1)S(1)} %and_select_fusion.refs_0_.x_ref), channel_id=1, source_target_pairs={{0,2},{1,3},{2,0},{3,1},{4,6},{5,7},{6,4},{7,5},{8,10},{9,11},{10,... | collective-permute-start | bytes 602120 | tf_op jit(solution)/shard_map/ppermute | solution.py:19
  9.4 12.7 %collective-permute-start.7 = (bf16[1,112,896]{2,1,0:T(8,128)(2,1)S(1)}, bf16[1,112,896]{2,1,0:T(8,128)(2,1)S(1)}, u32[]{:S(2)}, u32[]{:S(2)}) collective-permute-start(bf16[1,112,896]{2,1,0:T(8,128)(2,1)S(1)} %and_select_fusion.refs_0_.x_ref), channel_id=1, source_target_pairs={{0,8},{8,0},{16,24},{24,16},{1,9},{9,1},{17,25},{25,17},{2,10},{10... | collective-permute-start | bytes 602120 | tf_op jit(solution)/shard_map/ppermute | solution.py:23
  13.7 8.5 %collective-permute-start.1 = (bf16[1,112,896]{2,1,0:T(8,128)(2,1)S(1)}, bf16[1,112,896]{2,1,0:T(8,128)(2,1)S(1)}, u32[]{:S(2)}, u32[]{:S(2)}) collective-permute-start(bf16[1,112,896]{2,1,0:T(8,128)(2,1)S(1)} %and_select_fusion.refs_0_.x_ref), channel_id=1, source_target_pairs={{0,1},{1,0},{2,3},{3,2},{4,5},{5,4},{6,7},{7,6},{8,9},{9,8},{10,11... | collective-permute-start | bytes 602120 | tf_op jit(solution)/shard_map/ppermute | solution.py:19
  16.5 8.5 %collective-permute-start.11 = (bf16[1,112,896]{2,1,0:T(8,128)(2,1)S(1)}, bf16[1,112,896]{2,1,0:T(8,128)(2,1)S(1)}, u32[]{:S(2)}, u32[]{:S(2)}) collective-permute-start(bf16[1,112,896]{2,1,0:T(8,128)(2,1)S(1)} %collective-permute-done.3.refs_4_), channel_id=1, source_target_pairs={{0,8},{8,0},{16,24},{24,16},{1,9},{9,1},{17,25},{25,17},{2,10},{10... | collective-permute-start | bytes 602120 | tf_op jit(solution)/shard_map/ppermute | solution.py:23
  18.1 7.0 %collective-permute-start.5 = (bf16[1,112,896]{2,1,0:T(8,128)(2,1)S(1)}, bf16[1,112,896]{2,1,0:T(8,128)(2,1)S(1)}, u32[]{:S(2)}, u32[]{:S(2)}) collective-permute-start(bf16[1,112,896]{2,1,0:T(8,128)(2,1)S(1)} %collective-permute-done.3.refs_4_), channel_id=1, source_target_pairs={{0,2},{1,3},{2,0},{3,1},{4,6},{5,7},{6,4},{7,5},{8,10},{9,11},{10,... | collective-permute-start | bytes 602120 | tf_op jit(solution)/shard_map/ppermute | solution.py:19
  22.2 5.4 %collective-permute-start.8 = (bf16[1,112,896]{2,1,0:T(8,128)(2,1)S(1)}, bf16[1,112,896]{2,1,0:T(8,128)(2,1)S(1)}, u32[]{:S(2)}, u32[]{:S(2)}) collective-permute-start(bf16[1,112,896]{2,1,0:T(8,128)(2,1)S(1)} %collective-permute-done.7.refs_8_), channel_id=1, source_target_pairs={{0,1},{1,0},{2,3},{3,2},{4,5},{5,4},{6,7},{7,6},{8,9},{9,8},{10,11... | collective-permute-start | bytes 602120 | tf_op jit(solution)/shard_map/ppermute | solution.py:19
  22.2 6.6 %collective-permute-start.4 = (bf16[1,112,896]{2,1,0:T(8,128)(2,1)S(1)}, bf16[1,112,896]{2,1,0:T(8,128)(2,1)S(1)}, u32[]{:S(2)}, u32[]{:S(2)}) collective-permute-start(bf16[1,112,896]{2,1,0:T(8,128)(2,1)S(1)} %collective-permute-done.3.refs_4_), channel_id=1, source_target_pairs={{0,1},{1,0},{2,3},{3,2},{4,5},{5,4},{6,7},{7,6},{8,9},{9,8},{10,11... | collective-permute-start | bytes 602120 | tf_op jit(solution)/shard_map/ppermute | solution.py:19
  22.7 7.2 %collective-permute-start.9 = (bf16[1,112,896]{2,1,0:T(8,128)(2,1)S(1)}, bf16[1,112,896]{2,1,0:T(8,128)(2,1)S(1)}, u32[]{:S(2)}, u32[]{:S(2)}) collective-permute-start(bf16[1,112,896]{2,1,0:T(8,128)(2,1)S(1)} %collective-permute-done.refs_2_), channel_id=1, source_target_pairs={{0,8},{8,0},{16,24},{24,16},{1,9},{9,1},{17,25},{25,17},{2,10},{10... | collective-permute-start | bytes 602120 | tf_op jit(solution)/shard_map/ppermute | solution.py:23
  25.0 4.9 %collective-permute-start.2 = (bf16[1,112,896]{2,1,0:T(8,128)(2,1)S(1)}, bf16[1,112,896]{2,1,0:T(8,128)(2,1)S(1)}, u32[]{:S(2)}, u32[]{:S(2)}) collective-permute-start(bf16[1,112,896]{2,1,0:T(8,128)(2,1)S(1)} %collective-permute-done.refs_2_), channel_id=1, source_target_pairs={{0,1},{1,0},{2,3},{3,2},{4,5},{5,4},{6,7},{7,6},{8,9},{9,8},{10,11... | collective-permute-start | bytes 602120 | tf_op jit(solution)/shard_map/ppermute | solution.py:19
  25.0 6.5 %collective-permute-start.19 = (bf16[1,112,896]{2,1,0:T(8,128)(2,1)S(1)}, bf16[1,112,896]{2,1,0:T(8,128)(2,1)S(1)}, u32[]{:S(2)}, u32[]{:S(2)}) collective-permute-start(bf16[1,112,896]{2,1,0:T(8,128)(2,1)S(1)} %collective-permute-done.11.refs_12_), channel_id=1, source_target_pairs={{0,16},{24,8},{1,17},{25,9},{2,18},{26,10},{3,19},{27,11},{4,20},{... | collective-permute-start | bytes 602120 | tf_op jit(solution)/shard_map/ppermute | solution.py:29
  27.6 6.2 %collective-permute-start.13 = (bf16[1,112,896]{2,1,0:T(8,128)(2,1)S(1)}, bf16[1,112,896]{2,1,0:T(8,128)(2,1)S(1)}, u32[]{:S(2)}, u32[]{:S(2)}) collective-permute-start(bf16[1,112,896]{2,1,0:T(8,128)(2,1)S(1)} %collective-permute-done.11.refs_12_), channel_id=1, source_target_pairs={{0,2},{1,3},{2,0},{3,1},{4,6},{5,7},{6,4},{7,5},{8,10},{9,11},{10,... | collective-permute-start | bytes 602120 | tf_op jit(solution)/shard_map/ppermute | solution.py:19
  28.8 5.0 %collective-permute-start.12 = (bf16[1,112,896]{2,1,0:T(8,128)(2,1)S(1)}, bf16[1,112,896]{2,1,0:T(8,128)(2,1)S(1)}, u32[]{:S(2)}, u32[]{:S(2)}) collective-permute-start(bf16[1,112,896]{2,1,0:T(8,128)(2,1)S(1)} %collective-permute-done.11.refs_12_), channel_id=1, source_target_pairs={{0,1},{1,0},{2,3},{3,2},{4,5},{5,4},{6,7},{7,6},{8,9},{9,8},{10,11... | collective-permute-start | bytes 602120 | tf_op jit(solution)/shard_map/ppermute | solution.py:19
  29.9 4.4 %collective-permute-start.6 = (bf16[1,112,896]{2,1,0:T(8,128)(2,1)S(1)}, bf16[1,112,896]{2,1,0:T(8,128)(2,1)S(1)}, u32[]{:S(2)}, u32[]{:S(2)}) collective-permute-start(bf16[1,112,896]{2,1,0:T(8,128)(2,1)S(1)} %collective-permute-done.5.refs_6_), channel_id=1, source_target_pairs={{0,1},{1,0},{2,3},{3,2},{4,5},{5,4},{6,7},{7,6},{8,9},{9,8},{10,11... | collective-permute-start | bytes 602120 | tf_op jit(solution)/shard_map/ppermute | solution.py:19
  29.9 4.5 %collective-permute-start.17 = (bf16[1,112,896]{2,1,0:T(8,128)(2,1)S(1)}, bf16[1,112,896]{2,1,0:T(8,128)(2,1)S(1)}, u32[]{:S(2)}, u32[]{:S(2)}) collective-permute-start(bf16[1,112,896]{2,1,0:T(8,128)(2,1)S(1)} %collective-permute-done.refs_2_), channel_id=1, source_target_pairs={{8,16},{16,8},{9,17},{17,9},{10,18},{18,10},{11,19},{19,11},{12,20... | collective-permute-start | bytes 602120 | tf_op jit(solution)/shard_map/ppermute | solution.py:34
  31.5 6.6 %collective-permute-start.21 = (bf16[1,112,896]{2,1,0:T(8,128)(2,1)S(1)}, bf16[1,112,896]{2,1,0:T(8,128)(2,1)S(1)}, u32[]{:S(2)}, u32[]{:S(2)}) collective-permute-start(bf16[1,112,896]{2,1,0:T(8,128)(2,1)S(1)} %collective-permute-done.19.refs_20_), channel_id=1, source_target_pairs={{0,2},{1,3},{2,0},{3,1},{4,6},{5,7},{6,4},{7,5},{8,10},{9,11},{10,... | collective-permute-start | bytes 602120 | tf_op jit(solution)/shard_map/ppermute | solution.py:19
  33.8 4.3 %collective-permute-start.10 = (bf16[1,112,896]{2,1,0:T(8,128)(2,1)S(1)}, bf16[1,112,896]{2,1,0:T(8,128)(2,1)S(1)}, u32[]{:S(2)}, u32[]{:S(2)}) collective-permute-start(bf16[1,112,896]{2,1,0:T(8,128)(2,1)S(1)} %collective-permute-done.9.refs_10_), channel_id=1, source_target_pairs={{0,1},{1,0},{2,3},{3,2},{4,5},{5,4},{6,7},{7,6},{8,9},{9,8},{10,11... | collective-permute-start | bytes 602120 | tf_op jit(solution)/shard_map/ppermute | solution.py:19
  52.1 12.0 %collective-permute-start.24 = (bf16[2,1,896,896]{3,2,1,0:T(8,128)(2,1)S(1)}, bf16[2,1,896,896]{3,2,1,0:T(8,128)(2,1)S(1)}, u32[]{:S(2)}, u32[]{:S(2)}) collective-permute-start(bf16[2,1,896,896]{3,2,1,0:T(8,128)(2,1)S(1)} %copy-done), channel_id=1, source_target_pairs={{0,1},{1,0},{2,3},{3,2},{4,5},{5,4},{6,7},{7,6},{8,9},{9,8},{10,11... | collective-permute-start | bytes 9633800 | tf_op jit(solution)/shard_map/ppermute | solution.py:19
  52.3 11.8 %collective-permute-start.25 = (bf16[2,1,896,896]{3,2,1,0:T(8,128)(2,1)S(1)}, bf16[2,1,896,896]{3,2,1,0:T(8,128)(2,1)S(1)}, u32[]{:S(2)}, u32[]{:S(2)}) collective-permute-start(bf16[2,1,896,896]{3,2,1,0:T(8,128)(2,1)S(1)} %copy-done.1), channel_id=1, source_target_pairs={{0,1},{1,0},{2,3},{3,2},{4,5},{5,4},{6,7},{7,6},{8,9},{9,8},{10,11... | collective-permute-start | bytes 9633800 | tf_op jit(solution)/shard_map/ppermute | solution.py:19
  52.6 9.8 %collective-permute-start.26 = (s32[4]{0:T(128)S(1)}, s32[4]{0:T(128)S(1)}, u32[]{:S(2)}, u32[]{:S(2)}) collective-permute-start(s32[4]{0:T(128)S(1)} %bitcast.16), channel_id=1, source_target_pairs={{0,1},{1,0},{2,3},{3,2},{4,5},{5,4},{6,7},{7,6},{8,9},{9,8},{10,11... | collective-permute-start | bytes 56 | tf_op jit(solution)/shard_map/ppermute | solution.py:19
  52.8 11.3 %collective-permute-start.29 = (bf16[112,896]{1,0:T(8,128)(2,1)S(1)}, bf16[112,896]{1,0:T(8,128)(2,1)S(1)}, u32[]{:S(2)}, u32[]{:S(2)}) collective-permute-start(bf16[112,896]{1,0:T(8,128)(2,1)S(1)} %get-tuple-element.49), channel_id=1, source_target_pairs={{0,6},{1,7},{2,4},{3,5},{4,2},{5,3},{6,0},{7,1},{8,14},{9,15},{10,... | collective-permute-start | bytes 602120 | tf_op jit(solution)/shard_map/ppermute | solution.py:19
  56.5 17.4 %collective-permute-start.28 = (bf16[112,896]{1,0:T(8,128)(2,1)S(1)}, bf16[112,896]{1,0:T(8,128)(2,1)S(1)}, u32[]{:S(2)}, u32[]{:S(2)}) collective-permute-start(bf16[112,896]{1,0:T(8,128)(2,1)S(1)} %get-tuple-element.50), channel_id=1, source_target_pairs={{0,4},{1,5},{2,6},{3,7},{4,0},{5,1},{6,2},{7,3},{8,12},{9,13},{10,... | collective-permute-start | bytes 602120 | tf_op jit(solution)/shard_map/ppermute | solution.py:19
  62.5 11.5 %collective-permute-start.27 = (bf16[112,896]{1,0:T(8,128)(2,1)S(1)}, bf16[112,896]{1,0:T(8,128)(2,1)S(1)}, u32[]{:S(2)}, u32[]{:S(2)}) collective-permute-start(bf16[112,896]{1,0:T(8,128)(2,1)S(1)} %get-tuple-element.51), channel_id=1, source_target_pairs={{0,2},{1,3},{2,0},{3,1},{4,6},{5,7},{6,4},{7,5},{8,10},{9,11},{10,... | collective-permute-start | bytes 602120 | tf_op jit(solution)/shard_map/ppermute | solution.py:19
  74.2 8.6 %collective-permute-start.37 = (bf16[1,112,896]{2,1,0:T(8,128)(2,1)S(1)}, bf16[1,112,896]{2,1,0:T(8,128)(2,1)S(1)}, u32[]{:S(2)}, u32[]{:S(2)}) collective-permute-start(bf16[1,112,896]{2,1,0:T(8,128)(2,1)S(1)} %get-tuple-element.40.refs_4_), channel_id=1, source_target_pairs={{0,8},{8,0},{16,24},{24,16},{1,9},{9,1},{17,25},{25,17},{2,10},{10... | collective-permute-start | bytes 602120 | tf_op jit(solution)/shard_map/ppermute | solution.py:23
  78.2 10.2 %collective-permute-start.33 = (bf16[1,112,896]{2,1,0:T(8,128)(2,1)S(1)}, bf16[1,112,896]{2,1,0:T(8,128)(2,1)S(1)}, u32[]{:S(2)}, u32[]{:S(2)}) collective-permute-start(bf16[1,112,896]{2,1,0:T(8,128)(2,1)S(1)} %get-tuple-element.40.refs_4_), channel_id=1, source_target_pairs={{0,4},{1,5},{2,6},{3,7},{4,0},{5,1},{6,2},{7,3},{8,12},{9,13},{10,... | collective-permute-start | bytes 602120 | tf_op jit(solution)/shard_map/ppermute | solution.py:19
  78.2 10.5 %collective-permute-start.31 = (bf16[1,112,896]{2,1,0:T(8,128)(2,1)S(1)}, bf16[1,112,896]{2,1,0:T(8,128)(2,1)S(1)}, u32[]{:S(2)}, u32[]{:S(2)}) collective-permute-start(bf16[1,112,896]{2,1,0:T(8,128)(2,1)S(1)} %get-tuple-element.40.refs_4_), channel_id=1, source_target_pairs={{0,2},{1,3},{2,0},{3,1},{4,6},{5,7},{6,4},{7,5},{8,10},{9,11},{10,... | collective-permute-start | bytes 602120 | tf_op jit(solution)/shard_map/ppermute | solution.py:19
  80.6 8.2 %collective-permute-start.30 = (bf16[1,112,896]{2,1,0:T(8,128)(2,1)S(1)}, bf16[1,112,896]{2,1,0:T(8,128)(2,1)S(1)}, u32[]{:S(2)}, u32[]{:S(2)}) collective-permute-start(bf16[1,112,896]{2,1,0:T(8,128)(2,1)S(1)} %get-tuple-element.40.refs_4_), channel_id=1, source_target_pairs={{0,1},{1,0},{2,3},{3,2},{4,5},{5,4},{6,7},{7,6},{8,9},{9,8},{10,11... | collective-permute-start | bytes 602120 | tf_op jit(solution)/shard_map/ppermute | solution.py:19
  82.8 6.8 %collective-permute-start.45 = (bf16[1,112,896]{2,1,0:T(8,128)(2,1)S(1)}, bf16[1,112,896]{2,1,0:T(8,128)(2,1)S(1)}, u32[]{:S(2)}, u32[]{:S(2)}) collective-permute-start(bf16[1,112,896]{2,1,0:T(8,128)(2,1)S(1)} %collective-permute-done.37.refs_12_), channel_id=1, source_target_pairs={{0,16},{24,8},{1,17},{25,9},{2,18},{26,10},{3,19},{27,11},{4,20},{... | collective-permute-start | bytes 602120 | tf_op jit(solution)/shard_map/ppermute | solution.py:29
  86.3 5.8 %collective-permute-start.38 = (bf16[1,112,896]{2,1,0:T(8,128)(2,1)S(1)}, bf16[1,112,896]{2,1,0:T(8,128)(2,1)S(1)}, u32[]{:S(2)}, u32[]{:S(2)}) collective-permute-start(bf16[1,112,896]{2,1,0:T(8,128)(2,1)S(1)} %collective-permute-done.37.refs_12_), channel_id=1, source_target_pairs={{0,1},{1,0},{2,3},{3,2},{4,5},{5,4},{6,7},{7,6},{8,9},{9,8},{10,11... | collective-permute-start | bytes 602120 | tf_op jit(solution)/shard_map/ppermute | solution.py:19
  88.4 7.9 %collective-permute-start.41 = (bf16[1,112,896]{2,1,0:T(8,128)(2,1)S(1)}, bf16[1,112,896]{2,1,0:T(8,128)(2,1)S(1)}, u32[]{:S(2)}, u32[]{:S(2)}) collective-permute-start(bf16[1,112,896]{2,1,0:T(8,128)(2,1)S(1)} %collective-permute-done.33.refs_8_), channel_id=1, source_target_pairs={{0,8},{8,0},{16,24},{24,16},{1,9},{9,1},{17,25},{25,17},{2,10},{10... | collective-permute-start | bytes 602120 | tf_op jit(solution)/shard_map/ppermute | solution.py:23
  88.7 9.6 %collective-permute-start.35 = (bf16[1,112,896]{2,1,0:T(8,128)(2,1)S(1)}, bf16[1,112,896]{2,1,0:T(8,128)(2,1)S(1)}, u32[]{:S(2)}, u32[]{:S(2)}) collective-permute-start(bf16[1,112,896]{2,1,0:T(8,128)(2,1)S(1)} %collective-permute-done.33.refs_8_), channel_id=1, source_target_pairs={{0,2},{1,3},{2,0},{3,1},{4,6},{5,7},{6,4},{7,5},{8,10},{9,11},{10,... | collective-permute-start | bytes 602120 | tf_op jit(solution)/shard_map/ppermute | solution.py:19
  88.9 9.6 %collective-permute-start.34 = (bf16[1,112,896]{2,1,0:T(8,128)(2,1)S(1)}, bf16[1,112,896]{2,1,0:T(8,128)(2,1)S(1)}, u32[]{:S(2)}, u32[]{:S(2)}) collective-permute-start(bf16[1,112,896]{2,1,0:T(8,128)(2,1)S(1)} %collective-permute-done.33.refs_8_), channel_id=1, source_target_pairs={{0,1},{1,0},{2,3},{3,2},{4,5},{5,4},{6,7},{7,6},{8,9},{9,8},{10,11... | collective-permute-start | bytes 602120 | tf_op jit(solution)/shard_map/ppermute | solution.py:19
  89.5 9.8 %collective-permute-start.39 = (bf16[1,112,896]{2,1,0:T(8,128)(2,1)S(1)}, bf16[1,112,896]{2,1,0:T(8,128)(2,1)S(1)}, u32[]{:S(2)}, u32[]{:S(2)}) collective-permute-start(bf16[1,112,896]{2,1,0:T(8,128)(2,1)S(1)} %collective-permute-done.31.refs_6_), channel_id=1, source_target_pairs={{0,8},{8,0},{16,24},{24,16},{1,9},{9,1},{17,25},{25,17},{2,10},{10... | collective-permute-start | bytes 602120 | tf_op jit(solution)/shard_map/ppermute | solution.py:23
  92.1 7.2 %collective-permute-start.32 = (bf16[1,112,896]{2,1,0:T(8,128)(2,1)S(1)}, bf16[1,112,896]{2,1,0:T(8,128)(2,1)S(1)}, u32[]{:S(2)}, u32[]{:S(2)}) collective-permute-start(bf16[1,112,896]{2,1,0:T(8,128)(2,1)S(1)} %collective-permute-done.31.refs_6_), channel_id=1, source_target_pairs={{0,1},{1,0},{2,3},{3,2},{4,5},{5,4},{6,7},{7,6},{8,9},{9,8},{10,11... | collective-permute-start | bytes 602120 | tf_op jit(solution)/shard_map/ppermute | solution.py:19
  96.3 5.3 %collective-permute-start.49 = (bf16[1,112,896]{2,1,0:T(8,128)(2,1)S(1)}, bf16[1,112,896]{2,1,0:T(8,128)(2,1)S(1)}, u32[]{:S(2)}, u32[]{:S(2)}) collective-permute-start(bf16[1,112,896]{2,1,0:T(8,128)(2,1)S(1)} %collective-permute-done.41.refs_16_), channel_id=1, source_target_pairs={{0,16},{24,8},{1,17},{25,9},{2,18},{26,10},{3,19},{27,11},{4,20},{... | collective-permute-start | bytes 602120 | tf_op jit(solution)/shard_map/ppermute | solution.py:29
  98.3 6.5 %collective-permute-start.43 = (bf16[1,112,896]{2,1,0:T(8,128)(2,1)S(1)}, bf16[1,112,896]{2,1,0:T(8,128)(2,1)S(1)}, u32[]{:S(2)}, u32[]{:S(2)}) collective-permute-start(bf16[1,112,896]{2,1,0:T(8,128)(2,1)S(1)} %collective-permute-done.41.refs_16_), channel_id=1, source_target_pairs={{0,2},{1,3},{2,0},{3,1},{4,6},{5,7},{6,4},{7,5},{8,10},{9,11},{10,... | collective-permute-start | bytes 602120 | tf_op jit(solution)/shard_map/ppermute | solution.py:19
  98.4 6.4 %collective-permute-start.46 = (bf16[1,112,896]{2,1,0:T(8,128)(2,1)S(1)}, bf16[1,112,896]{2,1,0:T(8,128)(2,1)S(1)}, u32[]{:S(2)}, u32[]{:S(2)}) collective-permute-start(bf16[1,112,896]{2,1,0:T(8,128)(2,1)S(1)} %collective-permute-done.45.refs_20_), channel_id=1, source_target_pairs={{0,1},{1,0},{2,3},{3,2},{4,5},{5,4},{6,7},{7,6},{8,9},{9,8},{10,11... | collective-permute-start | bytes 602120 | tf_op jit(solution)/shard_map/ppermute | solution.py:19
  99.3 5.6 %collective-permute-start.42 = (bf16[1,112,896]{2,1,0:T(8,128)(2,1)S(1)}, bf16[1,112,896]{2,1,0:T(8,128)(2,1)S(1)}, u32[]{:S(2)}, u32[]{:S(2)}) collective-permute-start(bf16[1,112,896]{2,1,0:T(8,128)(2,1)S(1)} %collective-permute-done.41.refs_16_), channel_id=1, source_target_pairs={{0,1},{1,0},{2,3},{3,2},{4,5},{5,4},{6,7},{7,6},{8,9},{9,8},{10,11... | collective-permute-start | bytes 602120 | tf_op jit(solution)/shard_map/ppermute | solution.py:19
  99.3 6.1 %collective-permute-start.36 = (bf16[1,112,896]{2,1,0:T(8,128)(2,1)S(1)}, bf16[1,112,896]{2,1,0:T(8,128)(2,1)S(1)}, u32[]{:S(2)}, u32[]{:S(2)}) collective-permute-start(bf16[1,112,896]{2,1,0:T(8,128)(2,1)S(1)} %collective-permute-done.35.refs_10_), channel_id=1, source_target_pairs={{0,1},{1,0},{2,3},{3,2},{4,5},{5,4},{6,7},{7,6},{8,9},{9,8},{10,11... | collective-permute-start | bytes 602120 | tf_op jit(solution)/shard_map/ppermute | solution.py:19
  104.9 5.7 %collective-permute-start.51 = (bf16[1,112,896]{2,1,0:T(8,128)(2,1)S(1)}, bf16[1,112,896]{2,1,0:T(8,128)(2,1)S(1)}, u32[]{:S(2)}, u32[]{:S(2)}) collective-permute-start(bf16[1,112,896]{2,1,0:T(8,128)(2,1)S(1)} %collective-permute-done.49.refs_24_), channel_id=1, source_target_pairs={{0,2},{1,3},{2,0},{3,1},{4,6},{5,7},{6,4},{7,5},{8,10},{9,11},{10,... | collective-permute-start | bytes 602120 | tf_op jit(solution)/shard_map/ppermute | solution.py:19
  104.9 5.7 %collective-permute-start.40 = (bf16[1,112,896]{2,1,0:T(8,128)(2,1)S(1)}, bf16[1,112,896]{2,1,0:T(8,128)(2,1)S(1)}, u32[]{:S(2)}, u32[]{:S(2)}) collective-permute-start(bf16[1,112,896]{2,1,0:T(8,128)(2,1)S(1)} %collective-permute-done.39.refs_14_), channel_id=1, source_target_pairs={{0,1},{1,0},{2,3},{3,2},{4,5},{5,4},{6,7},{7,6},{8,9},{9,8},{10,11... | collective-permute-start | bytes 602120 | tf_op jit(solution)/shard_map/ppermute | solution.py:19
  104.9 5.7 %collective-permute-start.44 = (bf16[1,112,896]{2,1,0:T(8,128)(2,1)S(1)}, bf16[1,112,896]{2,1,0:T(8,128)(2,1)S(1)}, u32[]{:S(2)}, u32[]{:S(2)}) collective-permute-start(bf16[1,112,896]{2,1,0:T(8,128)(2,1)S(1)} %collective-permute-done.43.refs_18_), channel_id=1, source_target_pairs={{0,1},{1,0},{2,3},{3,2},{4,5},{5,4},{6,7},{7,6},{8,9},{9,8},{10,11... | collective-permute-start | bytes 602120 | tf_op jit(solution)/shard_map/ppermute | solution.py:19
  105.4 5.2 %collective-permute-start.50 = (bf16[1,112,896]{2,1,0:T(8,128)(2,1)S(1)}, bf16[1,112,896]{2,1,0:T(8,128)(2,1)S(1)}, u32[]{:S(2)}, u32[]{:S(2)}) collective-permute-start(bf16[1,112,896]{2,1,0:T(8,128)(2,1)S(1)} %collective-permute-done.49.refs_24_), channel_id=1, source_target_pairs={{0,1},{1,0},{2,3},{3,2},{4,5},{5,4},{6,7},{7,6},{8,9},{9,8},{10,11... | collective-permute-start | bytes 602120 | tf_op jit(solution)/shard_map/ppermute | solution.py:19
  105.5 5.1 %collective-permute-start.48 = (bf16[1,112,896]{2,1,0:T(8,128)(2,1)S(1)}, bf16[1,112,896]{2,1,0:T(8,128)(2,1)S(1)}, u32[]{:S(2)}, u32[]{:S(2)}) collective-permute-start(bf16[1,112,896]{2,1,0:T(8,128)(2,1)S(1)} %collective-permute-done.47.refs_22_), channel_id=1, source_target_pairs={{0,1},{1,0},{2,3},{3,2},{4,5},{5,4},{6,7},{7,6},{8,9},{9,8},{10,11... | collective-permute-start | bytes 602120 | tf_op jit(solution)/shard_map/ppermute | solution.py:19
  121.9 9.8 %collective-permute-start.53 = (bf16[112,896]{1,0:T(8,128)(2,1)S(1)}, bf16[112,896]{1,0:T(8,128)(2,1)S(1)}, u32[]{:S(2)}, u32[]{:S(2)}) collective-permute-start(bf16[112,896]{1,0:T(8,128)(2,1)S(1)} %get-tuple-element.44), channel_id=1, source_target_pairs={{0,6},{1,7},{2,4},{3,5},{4,2},{5,3},{6,0},{7,1},{8,14},{9,15},{10,... | collective-permute-start | bytes 602120 | tf_op jit(solution)/shard_map/ppermute | solution.py:19
  124.2 17.1 %collective-permute-start.54 = (bf16[112,896]{1,0:T(8,128)(2,1)S(1)}, bf16[112,896]{1,0:T(8,128)(2,1)S(1)}, u32[]{:S(2)}, u32[]{:S(2)}) collective-permute-start(bf16[112,896]{1,0:T(8,128)(2,1)S(1)} %get-tuple-element.45), channel_id=1, source_target_pairs={{0,4},{1,5},{2,6},{3,7},{4,0},{5,1},{6,2},{7,3},{8,12},{9,13},{10,... | collective-permute-start | bytes 602120 | tf_op jit(solution)/shard_map/ppermute | solution.py:19
  124.2 17.1 %collective-permute-start.55 = (bf16[112,896]{1,0:T(8,128)(2,1)S(1)}, bf16[112,896]{1,0:T(8,128)(2,1)S(1)}, u32[]{:S(2)}, u32[]{:S(2)}) collective-permute-start(bf16[112,896]{1,0:T(8,128)(2,1)S(1)} %get-tuple-element.46), channel_id=1, source_target_pairs={{0,2},{1,3},{2,0},{3,1},{4,6},{5,7},{6,4},{7,5},{8,10},{9,11},{10,... | collective-permute-start | bytes 602120 | tf_op jit(solution)/shard_map/ppermute | solution.py:19
  (12 other events, 96.7 us)

commit v6 on v5

--- a/solution.py
+++ b/solution.py
@@ -369,8 +369,9 @@
     pieces, scal = gather_pieces(start, scal, FIRST, sec_count, term_count)
     mine, theirs = apply_terms(scal, left_env, right_env, pieces, FIRST, rows)
     own, got = reduce_parts(mine, theirs, term_count)
-    local = lax.optimization_barrier((left_env, right_env, scal[: 2 * terms], own))[:3]
+    local = lax.optimization_barrier((left_env, right_env, own))[:2]
     swapped = [along_term(a, lambda t: t ^ 1, term_count) for a in local]
+    table = along_term(lax.optimization_barrier((scal[: 2 * terms], pieces[3]))[0], lambda t: t ^ 1, term_count)
     own, swapped = lax.optimization_barrier((own, swapped))
     envs = (left_env, swapped[0], right_env, swapped[1])
     y, shard, sums = pl.pallas_call(
@@ -382,7 +383,7 @@
         name="image",
     )(start, own, *got)
     pieces, _ = gather_pieces(shard, (), SECOND, sec_count, term_count)
-    own, parts = apply_chip_terms(scal, swapped[2], envs, pieces, SECOND, rows)
+    own, parts = apply_chip_terms(scal, table, envs, pieces, SECOND, rows)
     got = send_parts(parts, term_count)
     h, sums = pl.pallas_call(
         gram_kernel,
@@ -391,7 +392,7 @@
         out_specs=(vmem, vmem),
         compiler_params=small,
         name="gram",
-    )(sums, start, y, own, *got[::-1])
+    )(sums, start, y, own, *got[1:], got[0])
     sums = everyones(sums, sec_count * term_count)
     vector, alphas, betas = pl.pallas_call(
         finish_kernel,

time: 156 us -> 155 us (level)
  starting transfers between devices: 50.3 us -> 48.4 us
    ppermute x6, starting transfers between devices: 14.4 us -> 12.8 us  [pair_exchange(): lax.ppermute(x, 'sec', [(i, i ^ 1) for i in range(count) if i ^ 1 < count])]
where the time goes in v6:
time: 155 us
  waiting for transfers between devices  65.6 us (42%)
  starting transfers between devices  48.4 us (31%)
  Pallas kernels  21.3 us (14%)
  blocking collectives  14.4 us (9%)
  between operations  2.39 us (2%)
  other arithmetic  1.87 us (1%)
    ppermute x44, waiting for transfers between devices, along_term(): return lax.ppermute(x, 'term', [(i, partner(i)) for i in range(count)])  52.2 us
    ppermute x44, starting transfers between devices, along_term(): return lax.ppermute(x, 'term', [(i, partner(i)) for i in range(count)])  24.9 us
    all_to_all x1, blocking collectives, everyones(): lax.all_to_all(jnp.broadcast_to(tile, (count,) + tile.shape), ('sec', 'te...  14.4 us
    ppermute x6, starting transfers between devices, pair_exchange(): lax.ppermute(x, 'sec', [(i, i ^ 1) for i in range(count) if i ^ 1 < count])  12.8 us
    ppermute x6, waiting for transfers between devices, pair_exchange(): lax.ppermute(x, 'sec', [(i, i ^ 1) for i in range(count) if i ^ 1 < count])  10.7 us
    pallas_call x1, Pallas kernels, apply_terms(): pl.pallas_call(functools.partial(apply_kernel, chips, terms, rows, order)...  9.94 us
    pallas_call x1, Pallas kernels, apply_chip_terms(): pl.pallas_call(functools.partial(chip_kernel, chips, terms, rows, order),...  9.83 us
    ppermute x3, starting transfers between devices, pair_forward(): return lax.ppermute(x, 'sec', pairs)  8.55 us
  transfers between devices with their start and end apart: 56, of which 22 were waited for; matrix products, arithmetic and copies ran while one was open for 1% of the time, Pallas kernels for 0%

profile of v6, /device:TPU:0, one launch (start us, length us, event | category | flops | bytes accessed | tf_op | source)
XLA Modules:
  0.0 154.8 jit_solution(16579588715754427059)
XLA Ops:
  2.0 1.1 and_select_fusion.refs_0_.x_ref
  3.0 4.1 %collective-permute-start.3 = (bf16[1,112,896]{2,1,0:T(8,128)(2,1)S(1)}, bf16[1,112,896]{2,1,0:T(8,128)(2,1)S(1)}, u32[]{:S(2)}, u32[]{:S(2)}) collective-permute-start(bf16[1,112,896]{2,1,0:T(8,128)(2,1)S(1)} %and_select_fusion.refs_0_.x_ref), channel_id=1, source_target_pairs={{0,4},{1,5},{2,6},{3,7},{4,0},{5,1},{6,2},{7,3},{8,12},{9,13},{10,... | collective-permute-start | bytes 602120 | tf_op jit(solution)/shard_map/ppermute | solution.py:19
  7.1 0.7 collective-permute-start.15
  7.8 1.6 %collective-permute-start = (bf16[1,112,896]{2,1,0:T(8,128)(2,1)S(1)}, bf16[1,112,896]{2,1,0:T(8,128)(2,1)S(1)}, u32[]{:S(2)}, u32[]{:S(2)}) collective-permute-start(bf16[1,112,896]{2,1,0:T(8,128)(2,1)S(1)} %and_select_fusion.refs_0_.x_ref), channel_id=1, source_target_pairs={{0,2},{1,3},{2,0},{3,1},{4,6},{5,7},{6,4},{7,5},{8,10},{9,11},{10,... | collective-permute-start | bytes 602120 | tf_op jit(solution)/shard_map/ppermute | solution.py:19
  9.4 4.2 %collective-permute-start.7 = (bf16[1,112,896]{2,1,0:T(8,128)(2,1)S(1)}, bf16[1,112,896]{2,1,0:T(8,128)(2,1)S(1)}, u32[]{:S(2)}, u32[]{:S(2)}) collective-permute-start(bf16[1,112,896]{2,1,0:T(8,128)(2,1)S(1)} %and_select_fusion.refs_0_.x_ref), channel_id=1, source_target_pairs={{0,8},{8,0},{16,24},{24,16},{1,9},{9,1},{17,25},{25,17},{2,10},{10... | collective-permute-start | bytes 602120 | tf_op jit(solution)/shard_map/ppermute | solution.py:23
  13.7 2.9 %collective-permute-done.3.refs_4_ = bf16[1,112,896]{2,1,0:T(8,128)(2,1)S(1)} collective-permute-done((bf16[1,112,896]{2,1,0:T(8,128)(2,1)S(1)}, bf16[1,112,896]{2,1,0:T(8,128)(2,1)S(1)}, u32[]{:S(2)}, u32[]{:S(2)}) %collective-permute-start.3) | collective-permute-done | bytes 200736 | tf_op jit(solution)/shard_map/ppermute | solution.py:19
  16.5 1.5 collective-permute-start.11
  18.7 0.7 compare_select_fusion.1
  19.3 0.7 concatenate.3.scal
  20.1 2.1 %collective-permute-done.7.refs_8_ = bf16[1,112,896]{2,1,0:T(8,128)(2,1)S(1)} collective-permute-done((bf16[1,112,896]{2,1,0:T(8,128)(2,1)S(1)}, bf16[1,112,896]{2,1,0:T(8,128)(2,1)S(1)}, u32[]{:S(2)}, u32[]{:S(2)}) %collective-permute-start.7) | collective-permute-done | bytes 200736 | tf_op jit(solution)/shard_map/ppermute | solution.py:23
  22.7 1.6 %collective-permute-start.9 = (bf16[1,112,896]{2,1,0:T(8,128)(2,1)S(1)}, bf16[1,112,896]{2,1,0:T(8,128)(2,1)S(1)}, u32[]{:S(2)}, u32[]{:S(2)}) collective-permute-start(bf16[1,112,896]{2,1,0:T(8,128)(2,1)S(1)} %collective-permute-done.refs_2_), channel_id=1, source_target_pairs={{0,8},{8,0},{16,24},{24,16},{1,9},{9,1},{17,25},{25,17},{2,10},{10... | collective-permute-start | bytes 602120 | tf_op jit(solution)/shard_map/ppermute | solution.py:23
  24.3 0.7 collective-permute-done.11.refs_12_
  25.0 2.6 %collective-permute-start.19 = (bf16[1,112,896]{2,1,0:T(8,128)(2,1)S(1)}, bf16[1,112,896]{2,1,0:T(8,128)(2,1)S(1)}, u32[]{:S(2)}, u32[]{:S(2)}) collective-permute-start(bf16[1,112,896]{2,1,0:T(8,128)(2,1)S(1)} %collective-permute-done.11.refs_12_), channel_id=1, source_target_pairs={{0,16},{24,8},{1,17},{25,9},{2,18},{26,10},{3,19},{27,11},{4,20},{... | collective-permute-start | bytes 602120 | tf_op jit(solution)/shard_map/ppermute | solution.py:29
  27.6 1.2 collective-permute-start.13
  28.8 1.1 collective-permute-done.9.refs_10_
  29.9 0.7 collective-permute-start.17
  30.6 0.9 collective-permute-done.19.refs_20_
  31.5 1.6 %collective-permute-start.21 = (bf16[1,112,896]{2,1,0:T(8,128)(2,1)S(1)}, bf16[1,112,896]{2,1,0:T(8,128)(2,1)S(1)}, u32[]{:S(2)}, u32[]{:S(2)}) collective-permute-start(bf16[1,112,896]{2,1,0:T(8,128)(2,1)S(1)} %collective-permute-done.19.refs_20_), channel_id=1, source_target_pairs={{0,2},{1,3},{2,0},{3,1},{4,6},{5,7},{6,4},{7,5},{8,10},{9,11},{10,... | collective-permute-start | bytes 602120 | tf_op jit(solution)/shard_map/ppermute | solution.py:19
  33.1 0.7 collective-permute-done.13.refs_14_
  34.8 3.3 %collective-permute-done.21.refs_22_ = bf16[1,112,896]{2,1,0:T(8,128)(2,1)S(1)} collective-permute-done((bf16[1,112,896]{2,1,0:T(8,128)(2,1)S(1)}, bf16[1,112,896]{2,1,0:T(8,128)(2,1)S(1)}, u32[]{:S(2)}, u32[]{:S(2)}) %collective-permute-start.21) | collective-permute-done | bytes 200736 | tf_op jit(solution)/shard_map/ppermute | solution.py:19
  38.1 1.4 collective-permute-done.22.refs_23_
  39.6 9.9 %apply_terms.1 = (f32[4,112,896]{2,1,0:T(8,128)S(1)}, bf16[4,112,896]{2,1,0:T(8,128)(2,1)S(1)}) custom-call(s32[8]{0:T(128)S(1)} %concatenate.3.scal, bf16[2,1,896,896]{3,2,1,0:T(8,128)(2,1)} %refs_0_.1, bf16[2,1,896,896]{3,2,1,0:T(8,128)(2,1)} %refs_2_.1, bf16[1,112,896]{2,1,0:T(8,128)(2,1)S(1)} %and_select_fusion.refs_0_.x_ref, ...), custom_call_target="tpu_custom_call" | custom-call | tf_op jit(solution)/shard_map/apply_terms/pallas_call | solution.py:163
  49.7 2.2 %collective-permute-done.23 = bf16[4,112,896]{2,1,0:T(8,128)(2,1)S(1)} collective-permute-done((bf16[4,112,896]{2,1,0:T(8,128)(2,1)S(1)}, bf16[4,112,896]{2,1,0:T(8,128)(2,1)S(1)}, u32[]{:S(2)}, u32[]{:S(2)}) %collective-permute-start.23) | collective-permute-done | bytes 802848 | tf_op jit(solution)/shard_map/ppermute | solution.py:19
  52.6 3.7 %collective-permute-start.28 = (bf16[112,896]{1,0:T(8,128)(2,1)S(1)}, bf16[112,896]{1,0:T(8,128)(2,1)S(1)}, u32[]{:S(2)}, u32[]{:S(2)}) collective-permute-start(bf16[112,896]{1,0:T(8,128)(2,1)S(1)} %get-tuple-element.47), channel_id=1, source_target_pairs={{0,6},{1,7},{2,4},{3,5},{4,2},{5,3},{6,0},{7,1},{8,14},{9,15},{10,... | collective-permute-start | bytes 602120 | tf_op jit(solution)/shard_map/ppermute | solution.py:19
  57.0 0.9 collective-permute-done.24.refs_1_
  57.9 4.6 %collective-permute-done.25.refs_3_ = bf16[2,1,896,896]{3,2,1,0:T(8,128)(2,1)S(1)} collective-permute-done((bf16[2,1,896,896]{3,2,1,0:T(8,128)(2,1)S(1)}, bf16[2,1,896,896]{3,2,1,0:T(8,128)(2,1)S(1)}, u32[]{:S(2)}, u32[]{:S(2)}) %collective-permute-start.25) | collective-permute-done | bytes 3211296 | tf_op jit(solution)/shard_map/ppermute | solution.py:19
  62.5 11.1 %collective-permute-done.27.refs_1_ = bf16[112,896]{1,0:T(8,128)(2,1)S(1)} collective-permute-done((bf16[112,896]{1,0:T(8,128)(2,1)S(1)}, bf16[112,896]{1,0:T(8,128)(2,1)S(1)}, u32[]{:S(2)}, u32[]{:S(2)}) %collective-permute-start.27) | collective-permute-done | bytes 200736 | tf_op jit(solution)/shard_map/ppermute | solution.py:19
  73.8 2.7 %collective-permute-start.37 = (bf16[1,112,896]{2,1,0:T(8,128)(2,1)S(1)}, bf16[1,112,896]{2,1,0:T(8,128)(2,1)S(1)}, u32[]{:S(2)}, u32[]{:S(2)}) collective-permute-start(bf16[1,112,896]{2,1,0:T(8,128)(2,1)S(1)} %get-tuple-element.38.refs_4_), channel_id=1, source_target_pairs={{0,8},{8,0},{16,24},{24,16},{1,9},{9,1},{17,25},{25,17},{2,10},{10... | collective-permute-start | bytes 602120 | tf_op jit(solution)/shard_map/ppermute | solution.py:23
  76.5 3.2 %collective-permute-start.31 = (bf16[1,112,896]{2,1,0:T(8,128)(2,1)S(1)}, bf16[1,112,896]{2,1,0:T(8,128)(2,1)S(1)}, u32[]{:S(2)}, u32[]{:S(2)}) collective-permute-start(bf16[1,112,896]{2,1,0:T(8,128)(2,1)S(1)} %get-tuple-element.38.refs_4_), channel_id=1, source_target_pairs={{0,2},{1,3},{2,0},{3,1},{4,6},{5,7},{6,4},{7,5},{8,10},{9,11},{10,... | collective-permute-start | bytes 602120 | tf_op jit(solution)/shard_map/ppermute | solution.py:19
  80.2 1.0 collective-permute-done.37.refs_12_
  81.2 3.6 %collective-permute-start.45 = (bf16[1,112,896]{2,1,0:T(8,128)(2,1)S(1)}, bf16[1,112,896]{2,1,0:T(8,128)(2,1)S(1)}, u32[]{:S(2)}, u32[]{:S(2)}) collective-permute-start(bf16[1,112,896]{2,1,0:T(8,128)(2,1)S(1)} %collective-permute-done.37.refs_12_), channel_id=1, source_target_pairs={{0,16},{24,8},{1,17},{25,9},{2,18},{26,10},{3,19},{27,11},{4,20},{... | collective-permute-start | bytes 602120 | tf_op jit(solution)/shard_map/ppermute | solution.py:29
  84.9 2.8 %collective-permute-done.33.refs_8_ = bf16[1,112,896]{2,1,0:T(8,128)(2,1)S(1)} collective-permute-done((bf16[1,112,896]{2,1,0:T(8,128)(2,1)S(1)}, bf16[1,112,896]{2,1,0:T(8,128)(2,1)S(1)}, u32[]{:S(2)}, u32[]{:S(2)}) %collective-permute-start.33) | collective-permute-done | bytes 200736 | tf_op jit(solution)/shard_map/ppermute | solution.py:19
  88.2 2.3 %collective-permute-start.39 = (bf16[1,112,896]{2,1,0:T(8,128)(2,1)S(1)}, bf16[1,112,896]{2,1,0:T(8,128)(2,1)S(1)}, u32[]{:S(2)}, u32[]{:S(2)}) collective-permute-start(bf16[1,112,896]{2,1,0:T(8,128)(2,1)S(1)} %collective-permute-done.31.refs_6_), channel_id=1, source_target_pairs={{0,8},{8,0},{16,24},{24,16},{1,9},{9,1},{17,25},{25,17},{2,10},{10... | collective-permute-start | bytes 602120 | tf_op jit(solution)/shard_map/ppermute | solution.py:23
  90.5 5.0 %collective-permute-done.41.refs_16_ = bf16[1,112,896]{2,1,0:T(8,128)(2,1)S(1)} collective-permute-done((bf16[1,112,896]{2,1,0:T(8,128)(2,1)S(1)}, bf16[1,112,896]{2,1,0:T(8,128)(2,1)S(1)}, u32[]{:S(2)}, u32[]{:S(2)}) %collective-permute-start.41) | collective-permute-done | bytes 200736 | tf_op jit(solution)/shard_map/ppermute | solution.py:23
  95.6 2.3 %collective-permute-start.49 = (bf16[1,112,896]{2,1,0:T(8,128)(2,1)S(1)}, bf16[1,112,896]{2,1,0:T(8,128)(2,1)S(1)}, u32[]{:S(2)}, u32[]{:S(2)}) collective-permute-start(bf16[1,112,896]{2,1,0:T(8,128)(2,1)S(1)} %collective-permute-done.41.refs_16_), channel_id=1, source_target_pairs={{0,16},{24,8},{1,17},{25,9},{2,18},{26,10},{3,19},{27,11},{4,20},{... | collective-permute-start | bytes 602120 | tf_op jit(solution)/shard_map/ppermute | solution.py:29
  98.1 0.8 collective-permute-done.39.refs_14_
  99.4 1.8 %collective-permute-done.49.refs_24_ = bf16[1,112,896]{2,1,0:T(8,128)(2,1)S(1)} collective-permute-done((bf16[1,112,896]{2,1,0:T(8,128)(2,1)S(1)}, bf16[1,112,896]{2,1,0:T(8,128)(2,1)S(1)}, u32[]{:S(2)}, u32[]{:S(2)}) %collective-permute-start.49) | collective-permute-done | bytes 200736 | tf_op jit(solution)/shard_map/ppermute | solution.py:29
  101.1 0.8 collective-permute-start.47
  102.0 2.4 %collective-permute-done.43.refs_18_ = bf16[1,112,896]{2,1,0:T(8,128)(2,1)S(1)} collective-permute-done((bf16[1,112,896]{2,1,0:T(8,128)(2,1)S(1)}, bf16[1,112,896]{2,1,0:T(8,128)(2,1)S(1)}, u32[]{:S(2)}, u32[]{:S(2)}) %collective-permute-start.43) | collective-permute-done | bytes 200736 | tf_op jit(solution)/shard_map/ppermute | solution.py:19
  105.4 4.7 %collective-permute-done.51.refs_26_ = bf16[1,112,896]{2,1,0:T(8,128)(2,1)S(1)} collective-permute-done((bf16[1,112,896]{2,1,0:T(8,128)(2,1)S(1)}, bf16[1,112,896]{2,1,0:T(8,128)(2,1)S(1)}, u32[]{:S(2)}, u32[]{:S(2)}) %collective-permute-start.51) | collective-permute-done | bytes 200736 | tf_op jit(solution)/shard_map/ppermute | solution.py:19
  110.2 1.4 collective-permute-done.52.refs_27_
  111.6 9.8 %apply_chip_terms.1 = (f32[112,896]{1,0:T(8,128)S(1)}, bf16[112,896]{1,0:T(8,128)(2,1)S(1)}, bf16[112,896]{1,0:T(8,128)(2,1)S(1)}, bf16[112,896]{1,0:T(8,128)(2,1)S(1)}) custom-call(s32[8]{0:T(128)S(1)} %concatenate.3.scal, s32[4]{0:T(128)S(1)} %collective-permute-done.29.theirs, bf16[2,1,896,896]{3,2,1,0:T(8,128)(2,1)} %refs_0_.1, ...), custom_call_target="tpu_custom_call" | custom-call | tf_op jit(solution)/shard_map/apply_chip_terms/pallas_call | solution.py:245
  121.5 2.4 %collective-permute-start.54 = (bf16[112,896]{1,0:T(8,128)(2,1)S(1)}, bf16[112,896]{1,0:T(8,128)(2,1)S(1)}, u32[]{:S(2)}, u32[]{:S(2)}) collective-permute-start(bf16[112,896]{1,0:T(8,128)(2,1)S(1)} %get-tuple-element.43), channel_id=1, source_target_pairs={{0,6},{1,7},{2,4},{3,5},{4,2},{5,3},{6,0},{7,1},{8,14},{9,15},{10,... | collective-permute-start | bytes 602120 | tf_op jit(solution)/shard_map/ppermute | solution.py:19
  123.8 1.1 collective-permute-start.55
  125.0 12.6 %collective-permute-done.53.refs_0_ = bf16[112,896]{1,0:T(8,128)(2,1)S(1)} collective-permute-done((bf16[112,896]{1,0:T(8,128)(2,1)S(1)}, bf16[112,896]{1,0:T(8,128)(2,1)S(1)}, u32[]{:S(2)}, u32[]{:S(2)}) %collective-permute-start.53) | collective-permute-done | bytes 200736 | tf_op jit(solution)/shard_map/ppermute | solution.py:19
  137.6 1.3 collective-permute-done.55.refs_2_
  139.0 14.4 %all_to_all.5.tiles = f32[32,8,128]{2,1,0:T(8,128)S(1)} all-to-all(f32[32,8,128]{2,1,0:T(8,128)S(1)} %broadcast_in_dim.19), channel_id=1, replica_groups=mesh['sec'=4,'term'=8] {'sec','term'}, dimensions={0} | all-to-all | bytes 262144 | tf_op jit(solution)/shard_map/all_to_all | solution.py:284
  153.5 1.1 finish.1
  (85 shorter events, 7.1 us)
Async XLA Ops:
  3.0 13.5 %collective-permute-start.3 = (bf16[1,112,896]{2,1,0:T(8,128)(2,1)S(1)}, bf16[1,112,896]{2,1,0:T(8,128)(2,1)S(1)}, u32[]{:S(2)}, u32[]{:S(2)}) collective-permute-start(bf16[1,112,896]{2,1,0:T(8,128)(2,1)S(1)} %and_select_fusion.refs_0_.x_ref), channel_id=1, source_target_pairs={{0,4},{1,5},{2,6},{3,7},{4,0},{5,1},{6,2},{7,3},{8,12},{9,13},{10,... | collective-permute-start | bytes 602120 | tf_op jit(solution)/shard_map/ppermute | solution.py:19
  7.1 10.9 %collective-permute-start.15 = (bf16[1,112,896]{2,1,0:T(8,128)(2,1)S(1)}, bf16[1,112,896]{2,1,0:T(8,128)(2,1)S(1)}, u32[]{:S(2)}, u32[]{:S(2)}) collective-permute-start(bf16[1,112,896]{2,1,0:T(8,128)(2,1)S(1)} %and_select_fusion.refs_0_.x_ref), channel_id=1, source_target_pairs={{8,16},{16,8},{9,17},{17,9},{10,18},{18,10},{11,19},{19,11},{12,20... | collective-permute-start | bytes 602120 | tf_op jit(solution)/shard_map/ppermute | solution.py:34
  7.8 10.9 %collective-permute-start = (bf16[1,112,896]{2,1,0:T(8,128)(2,1)S(1)}, bf16[1,112,896]{2,1,0:T(8,128)(2,1)S(1)}, u32[]{:S(2)}, u32[]{:S(2)}) collective-permute-start(bf16[1,112,896]{2,1,0:T(8,128)(2,1)S(1)} %and_select_fusion.refs_0_.x_ref), channel_id=1, source_target_pairs={{0,2},{1,3},{2,0},{3,1},{4,6},{5,7},{6,4},{7,5},{8,10},{9,11},{10,... | collective-permute-start | bytes 602120 | tf_op jit(solution)/shard_map/ppermute | solution.py:19
  9.4 12.7 %collective-permute-start.7 = (bf16[1,112,896]{2,1,0:T(8,128)(2,1)S(1)}, bf16[1,112,896]{2,1,0:T(8,128)(2,1)S(1)}, u32[]{:S(2)}, u32[]{:S(2)}) collective-permute-start(bf16[1,112,896]{2,1,0:T(8,128)(2,1)S(1)} %and_select_fusion.refs_0_.x_ref), channel_id=1, source_target_pairs={{0,8},{8,0},{16,24},{24,16},{1,9},{9,1},{17,25},{25,17},{2,10},{10... | collective-permute-start | bytes 602120 | tf_op jit(solution)/shard_map/ppermute | solution.py:23
  13.7 8.5 %collective-permute-start.1 = (bf16[1,112,896]{2,1,0:T(8,128)(2,1)S(1)}, bf16[1,112,896]{2,1,0:T(8,128)(2,1)S(1)}, u32[]{:S(2)}, u32[]{:S(2)}) collective-permute-start(bf16[1,112,896]{2,1,0:T(8,128)(2,1)S(1)} %and_select_fusion.refs_0_.x_ref), channel_id=1, source_target_pairs={{0,1},{1,0},{2,3},{3,2},{4,5},{5,4},{6,7},{7,6},{8,9},{9,8},{10,11... | collective-permute-start | bytes 602120 | tf_op jit(solution)/shard_map/ppermute | solution.py:19
  16.5 8.5 %collective-permute-start.11 = (bf16[1,112,896]{2,1,0:T(8,128)(2,1)S(1)}, bf16[1,112,896]{2,1,0:T(8,128)(2,1)S(1)}, u32[]{:S(2)}, u32[]{:S(2)}) collective-permute-start(bf16[1,112,896]{2,1,0:T(8,128)(2,1)S(1)} %collective-permute-done.3.refs_4_), channel_id=1, source_target_pairs={{0,8},{8,0},{16,24},{24,16},{1,9},{9,1},{17,25},{25,17},{2,10},{10... | collective-permute-start | bytes 602120 | tf_op jit(solution)/shard_map/ppermute | solution.py:23
  18.1 7.0 %collective-permute-start.5 = (bf16[1,112,896]{2,1,0:T(8,128)(2,1)S(1)}, bf16[1,112,896]{2,1,0:T(8,128)(2,1)S(1)}, u32[]{:S(2)}, u32[]{:S(2)}) collective-permute-start(bf16[1,112,896]{2,1,0:T(8,128)(2,1)S(1)} %collective-permute-done.3.refs_4_), channel_id=1, source_target_pairs={{0,2},{1,3},{2,0},{3,1},{4,6},{5,7},{6,4},{7,5},{8,10},{9,11},{10,... | collective-permute-start | bytes 602120 | tf_op jit(solution)/shard_map/ppermute | solution.py:19
  22.2 5.4 %collective-permute-start.8 = (bf16[1,112,896]{2,1,0:T(8,128)(2,1)S(1)}, bf16[1,112,896]{2,1,0:T(8,128)(2,1)S(1)}, u32[]{:S(2)}, u32[]{:S(2)}) collective-permute-start(bf16[1,112,896]{2,1,0:T(8,128)(2,1)S(1)} %collective-permute-done.7.refs_8_), channel_id=1, source_target_pairs={{0,1},{1,0},{2,3},{3,2},{4,5},{5,4},{6,7},{7,6},{8,9},{9,8},{10,11... | collective-permute-start | bytes 602120 | tf_op jit(solution)/shard_map/ppermute | solution.py:19
  22.2 6.6 %collective-permute-start.4 = (bf16[1,112,896]{2,1,0:T(8,128)(2,1)S(1)}, bf16[1,112,896]{2,1,0:T(8,128)(2,1)S(1)}, u32[]{:S(2)}, u32[]{:S(2)}) collective-permute-start(bf16[1,112,896]{2,1,0:T(8,128)(2,1)S(1)} %collective-permute-done.3.refs_4_), channel_id=1, source_target_pairs={{0,1},{1,0},{2,3},{3,2},{4,5},{5,4},{6,7},{7,6},{8,9},{9,8},{10,11... | collective-permute-start | bytes 602120 | tf_op jit(solution)/shard_map/ppermute | solution.py:19
  22.7 7.2 %collective-permute-start.9 = (bf16[1,112,896]{2,1,0:T(8,128)(2,1)S(1)}, bf16[1,112,896]{2,1,0:T(8,128)(2,1)S(1)}, u32[]{:S(2)}, u32[]{:S(2)}) collective-permute-start(bf16[1,112,896]{2,1,0:T(8,128)(2,1)S(1)} %collective-permute-done.refs_2_), channel_id=1, source_target_pairs={{0,8},{8,0},{16,24},{24,16},{1,9},{9,1},{17,25},{25,17},{2,10},{10... | collective-permute-start | bytes 602120 | tf_op jit(solution)/shard_map/ppermute | solution.py:23
  25.0 4.9 %collective-permute-start.2 = (bf16[1,112,896]{2,1,0:T(8,128)(2,1)S(1)}, bf16[1,112,896]{2,1,0:T(8,128)(2,1)S(1)}, u32[]{:S(2)}, u32[]{:S(2)}) collective-permute-start(bf16[1,112,896]{2,1,0:T(8,128)(2,1)S(1)} %collective-permute-done.refs_2_), channel_id=1, source_target_pairs={{0,1},{1,0},{2,3},{3,2},{4,5},{5,4},{6,7},{7,6},{8,9},{9,8},{10,11... | collective-permute-start | bytes 602120 | tf_op jit(solution)/shard_map/ppermute | solution.py:19
  25.0 6.5 %collective-permute-start.19 = (bf16[1,112,896]{2,1,0:T(8,128)(2,1)S(1)}, bf16[1,112,896]{2,1,0:T(8,128)(2,1)S(1)}, u32[]{:S(2)}, u32[]{:S(2)}) collective-permute-start(bf16[1,112,896]{2,1,0:T(8,128)(2,1)S(1)} %collective-permute-done.11.refs_12_), channel_id=1, source_target_pairs={{0,16},{24,8},{1,17},{25,9},{2,18},{26,10},{3,19},{27,11},{4,20},{... | collective-permute-start | bytes 602120 | tf_op jit(solution)/shard_map/ppermute | solution.py:29
  27.6 6.2 %collective-permute-start.13 = (bf16[1,112,896]{2,1,0:T(8,128)(2,1)S(1)}, bf16[1,112,896]{2,1,0:T(8,128)(2,1)S(1)}, u32[]{:S(2)}, u32[]{:S(2)}) collective-permute-start(bf16[1,112,896]{2,1,0:T(8,128)(2,1)S(1)} %collective-permute-done.11.refs_12_), channel_id=1, source_target_pairs={{0,2},{1,3},{2,0},{3,1},{4,6},{5,7},{6,4},{7,5},{8,10},{9,11},{10,... | collective-permute-start | bytes 602120 | tf_op jit(solution)/shard_map/ppermute | solution.py:19
  28.8 5.0 %collective-permute-start.12 = (bf16[1,112,896]{2,1,0:T(8,128)(2,1)S(1)}, bf16[1,112,896]{2,1,0:T(8,128)(2,1)S(1)}, u32[]{:S(2)}, u32[]{:S(2)}) collective-permute-start(bf16[1,112,896]{2,1,0:T(8,128)(2,1)S(1)} %collective-permute-done.11.refs_12_), channel_id=1, source_target_pairs={{0,1},{1,0},{2,3},{3,2},{4,5},{5,4},{6,7},{7,6},{8,9},{9,8},{10,11... | collective-permute-start | bytes 602120 | tf_op jit(solution)/shard_map/ppermute | solution.py:19
  29.9 4.4 %collective-permute-start.6 = (bf16[1,112,896]{2,1,0:T(8,128)(2,1)S(1)}, bf16[1,112,896]{2,1,0:T(8,128)(2,1)S(1)}, u32[]{:S(2)}, u32[]{:S(2)}) collective-permute-start(bf16[1,112,896]{2,1,0:T(8,128)(2,1)S(1)} %collective-permute-done.5.refs_6_), channel_id=1, source_target_pairs={{0,1},{1,0},{2,3},{3,2},{4,5},{5,4},{6,7},{7,6},{8,9},{9,8},{10,11... | collective-permute-start | bytes 602120 | tf_op jit(solution)/shard_map/ppermute | solution.py:19
  29.9 4.5 %collective-permute-start.17 = (bf16[1,112,896]{2,1,0:T(8,128)(2,1)S(1)}, bf16[1,112,896]{2,1,0:T(8,128)(2,1)S(1)}, u32[]{:S(2)}, u32[]{:S(2)}) collective-permute-start(bf16[1,112,896]{2,1,0:T(8,128)(2,1)S(1)} %collective-permute-done.refs_2_), channel_id=1, source_target_pairs={{8,16},{16,8},{9,17},{17,9},{10,18},{18,10},{11,19},{19,11},{12,20... | collective-permute-start | bytes 602120 | tf_op jit(solution)/shard_map/ppermute | solution.py:34
  31.5 6.6 %collective-permute-start.21 = (bf16[1,112,896]{2,1,0:T(8,128)(2,1)S(1)}, bf16[1,112,896]{2,1,0:T(8,128)(2,1)S(1)}, u32[]{:S(2)}, u32[]{:S(2)}) collective-permute-start(bf16[1,112,896]{2,1,0:T(8,128)(2,1)S(1)} %collective-permute-done.19.refs_20_), channel_id=1, source_target_pairs={{0,2},{1,3},{2,0},{3,1},{4,6},{5,7},{6,4},{7,5},{8,10},{9,11},{10,... | collective-permute-start | bytes 602120 | tf_op jit(solution)/shard_map/ppermute | solution.py:19
  33.8 4.3 %collective-permute-start.10 = (bf16[1,112,896]{2,1,0:T(8,128)(2,1)S(1)}, bf16[1,112,896]{2,1,0:T(8,128)(2,1)S(1)}, u32[]{:S(2)}, u32[]{:S(2)}) collective-permute-start(bf16[1,112,896]{2,1,0:T(8,128)(2,1)S(1)} %collective-permute-done.9.refs_10_), channel_id=1, source_target_pairs={{0,1},{1,0},{2,3},{3,2},{4,5},{5,4},{6,7},{7,6},{8,9},{9,8},{10,11... | collective-permute-start | bytes 602120 | tf_op jit(solution)/shard_map/ppermute | solution.py:19
  52.1 5.8 %collective-permute-start.24 = (bf16[2,1,896,896]{3,2,1,0:T(8,128)(2,1)S(1)}, bf16[2,1,896,896]{3,2,1,0:T(8,128)(2,1)S(1)}, u32[]{:S(2)}, u32[]{:S(2)}) collective-permute-start(bf16[2,1,896,896]{3,2,1,0:T(8,128)(2,1)S(1)} %copy-done), channel_id=1, source_target_pairs={{0,1},{1,0},{2,3},{3,2},{4,5},{5,4},{6,7},{7,6},{8,9},{9,8},{10,11... | collective-permute-start | bytes 9633800 | tf_op jit(solution)/shard_map/ppermute | solution.py:19
  52.3 10.2 %collective-permute-start.25 = (bf16[2,1,896,896]{3,2,1,0:T(8,128)(2,1)S(1)}, bf16[2,1,896,896]{3,2,1,0:T(8,128)(2,1)S(1)}, u32[]{:S(2)}, u32[]{:S(2)}) collective-permute-start(bf16[2,1,896,896]{3,2,1,0:T(8,128)(2,1)S(1)} %copy-done.1), channel_id=1, source_target_pairs={{0,1},{1,0},{2,3},{3,2},{4,5},{5,4},{6,7},{7,6},{8,9},{9,8},{10,11... | collective-permute-start | bytes 9633800 | tf_op jit(solution)/shard_map/ppermute | solution.py:19
  52.6 9.8 %collective-permute-start.28 = (bf16[112,896]{1,0:T(8,128)(2,1)S(1)}, bf16[112,896]{1,0:T(8,128)(2,1)S(1)}, u32[]{:S(2)}, u32[]{:S(2)}) collective-permute-start(bf16[112,896]{1,0:T(8,128)(2,1)S(1)} %get-tuple-element.47), channel_id=1, source_target_pairs={{0,6},{1,7},{2,4},{3,5},{4,2},{5,3},{6,0},{7,1},{8,14},{9,15},{10,... | collective-permute-start | bytes 602120 | tf_op jit(solution)/shard_map/ppermute | solution.py:19
  56.4 17.2 %collective-permute-start.27 = (bf16[112,896]{1,0:T(8,128)(2,1)S(1)}, bf16[112,896]{1,0:T(8,128)(2,1)S(1)}, u32[]{:S(2)}, u32[]{:S(2)}) collective-permute-start(bf16[112,896]{1,0:T(8,128)(2,1)S(1)} %get-tuple-element.48), channel_id=1, source_target_pairs={{0,4},{1,5},{2,6},{3,7},{4,0},{5,1},{6,2},{7,3},{8,12},{9,13},{10,... | collective-permute-start | bytes 602120 | tf_op jit(solution)/shard_map/ppermute | solution.py:19
  56.4 17.2 %collective-permute-start.26 = (bf16[112,896]{1,0:T(8,128)(2,1)S(1)}, bf16[112,896]{1,0:T(8,128)(2,1)S(1)}, u32[]{:S(2)}, u32[]{:S(2)}) collective-permute-start(bf16[112,896]{1,0:T(8,128)(2,1)S(1)} %get-tuple-element.49), channel_id=1, source_target_pairs={{0,2},{1,3},{2,0},{3,1},{4,6},{5,7},{6,4},{7,5},{8,10},{9,11},{10,... | collective-permute-start | bytes 602120 | tf_op jit(solution)/shard_map/ppermute | solution.py:19
  73.8 7.4 %collective-permute-start.37 = (bf16[1,112,896]{2,1,0:T(8,128)(2,1)S(1)}, bf16[1,112,896]{2,1,0:T(8,128)(2,1)S(1)}, u32[]{:S(2)}, u32[]{:S(2)}) collective-permute-start(bf16[1,112,896]{2,1,0:T(8,128)(2,1)S(1)} %get-tuple-element.38.refs_4_), channel_id=1, source_target_pairs={{0,8},{8,0},{16,24},{24,16},{1,9},{9,1},{17,25},{25,17},{2,10},{10... | collective-permute-start | bytes 602120 | tf_op jit(solution)/shard_map/ppermute | solution.py:23
  76.5 11.2 %collective-permute-start.33 = (bf16[1,112,896]{2,1,0:T(8,128)(2,1)S(1)}, bf16[1,112,896]{2,1,0:T(8,128)(2,1)S(1)}, u32[]{:S(2)}, u32[]{:S(2)}) collective-permute-start(bf16[1,112,896]{2,1,0:T(8,128)(2,1)S(1)} %get-tuple-element.38.refs_4_), channel_id=1, source_target_pairs={{0,4},{1,5},{2,6},{3,7},{4,0},{5,1},{6,2},{7,3},{8,12},{9,13},{10,... | collective-permute-start | bytes 602120 | tf_op jit(solution)/shard_map/ppermute | solution.py:19
  76.5 11.6 %collective-permute-start.31 = (bf16[1,112,896]{2,1,0:T(8,128)(2,1)S(1)}, bf16[1,112,896]{2,1,0:T(8,128)(2,1)S(1)}, u32[]{:S(2)}, u32[]{:S(2)}) collective-permute-start(bf16[1,112,896]{2,1,0:T(8,128)(2,1)S(1)} %get-tuple-element.38.refs_4_), channel_id=1, source_target_pairs={{0,2},{1,3},{2,0},{3,1},{4,6},{5,7},{6,4},{7,5},{8,10},{9,11},{10,... | collective-permute-start | bytes 602120 | tf_op jit(solution)/shard_map/ppermute | solution.py:19
  79.7 5.1 %collective-permute-start.29 = (s32[4]{0:T(128)S(1)}, s32[4]{0:T(128)S(1)}, u32[]{:S(2)}, u32[]{:S(2)}) collective-permute-start(s32[4]{0:T(128)S(1)} %bitcast.16), channel_id=1, source_target_pairs={{0,1},{1,0},{2,3},{3,2},{4,5},{5,4},{6,7},{7,6},{8,9},{9,8},{10,11... | collective-permute-start | bytes 56 | tf_op jit(solution)/shard_map/ppermute | solution.py:19
  79.7 8.4 %collective-permute-start.30 = (bf16[1,112,896]{2,1,0:T(8,128)(2,1)S(1)}, bf16[1,112,896]{2,1,0:T(8,128)(2,1)S(1)}, u32[]{:S(2)}, u32[]{:S(2)}) collective-permute-start(bf16[1,112,896]{2,1,0:T(8,128)(2,1)S(1)} %get-tuple-element.38.refs_4_), channel_id=1, source_target_pairs={{0,1},{1,0},{2,3},{3,2},{4,5},{5,4},{6,7},{7,6},{8,9},{9,8},{10,11... | collective-permute-start | bytes 602120 | tf_op jit(solution)/shard_map/ppermute | solution.py:19
  81.2 7.0 %collective-permute-start.45 = (bf16[1,112,896]{2,1,0:T(8,128)(2,1)S(1)}, bf16[1,112,896]{2,1,0:T(8,128)(2,1)S(1)}, u32[]{:S(2)}, u32[]{:S(2)}) collective-permute-start(bf16[1,112,896]{2,1,0:T(8,128)(2,1)S(1)} %collective-permute-done.37.refs_12_), channel_id=1, source_target_pairs={{0,16},{24,8},{1,17},{25,9},{2,18},{26,10},{3,19},{27,11},{4,20},{... | collective-permute-start | bytes 602120 | tf_op jit(solution)/shard_map/ppermute | solution.py:29
  84.8 5.7 %collective-permute-start.38 = (bf16[1,112,896]{2,1,0:T(8,128)(2,1)S(1)}, bf16[1,112,896]{2,1,0:T(8,128)(2,1)S(1)}, u32[]{:S(2)}, u32[]{:S(2)}) collective-permute-start(bf16[1,112,896]{2,1,0:T(8,128)(2,1)S(1)} %collective-permute-done.37.refs_12_), channel_id=1, source_target_pairs={{0,1},{1,0},{2,3},{3,2},{4,5},{5,4},{6,7},{7,6},{8,9},{9,8},{10,11... | collective-permute-start | bytes 602120 | tf_op jit(solution)/shard_map/ppermute | solution.py:19
  87.7 7.9 %collective-permute-start.41 = (bf16[1,112,896]{2,1,0:T(8,128)(2,1)S(1)}, bf16[1,112,896]{2,1,0:T(8,128)(2,1)S(1)}, u32[]{:S(2)}, u32[]{:S(2)}) collective-permute-start(bf16[1,112,896]{2,1,0:T(8,128)(2,1)S(1)} %collective-permute-done.33.refs_8_), channel_id=1, source_target_pairs={{0,8},{8,0},{16,24},{24,16},{1,9},{9,1},{17,25},{25,17},{2,10},{10... | collective-permute-start | bytes 602120 | tf_op jit(solution)/shard_map/ppermute | solution.py:23
  88.1 9.9 %collective-permute-start.35 = (bf16[1,112,896]{2,1,0:T(8,128)(2,1)S(1)}, bf16[1,112,896]{2,1,0:T(8,128)(2,1)S(1)}, u32[]{:S(2)}, u32[]{:S(2)}) collective-permute-start(bf16[1,112,896]{2,1,0:T(8,128)(2,1)S(1)} %collective-permute-done.33.refs_8_), channel_id=1, source_target_pairs={{0,2},{1,3},{2,0},{3,1},{4,6},{5,7},{6,4},{7,5},{8,10},{9,11},{10,... | collective-permute-start | bytes 602120 | tf_op jit(solution)/shard_map/ppermute | solution.py:19
  88.1 9.9 %collective-permute-start.34 = (bf16[1,112,896]{2,1,0:T(8,128)(2,1)S(1)}, bf16[1,112,896]{2,1,0:T(8,128)(2,1)S(1)}, u32[]{:S(2)}, u32[]{:S(2)}) collective-permute-start(bf16[1,112,896]{2,1,0:T(8,128)(2,1)S(1)} %collective-permute-done.33.refs_8_), channel_id=1, source_target_pairs={{0,1},{1,0},{2,3},{3,2},{4,5},{5,4},{6,7},{7,6},{8,9},{9,8},{10,11... | collective-permute-start | bytes 602120 | tf_op jit(solution)/shard_map/ppermute | solution.py:19
  88.2 10.7 %collective-permute-start.39 = (bf16[1,112,896]{2,1,0:T(8,128)(2,1)S(1)}, bf16[1,112,896]{2,1,0:T(8,128)(2,1)S(1)}, u32[]{:S(2)}, u32[]{:S(2)}) collective-permute-start(bf16[1,112,896]{2,1,0:T(8,128)(2,1)S(1)} %collective-permute-done.31.refs_6_), channel_id=1, source_target_pairs={{0,8},{8,0},{16,24},{24,16},{1,9},{9,1},{17,25},{25,17},{2,10},{10... | collective-permute-start | bytes 602120 | tf_op jit(solution)/shard_map/ppermute | solution.py:23
  90.5 8.3 %collective-permute-start.32 = (bf16[1,112,896]{2,1,0:T(8,128)(2,1)S(1)}, bf16[1,112,896]{2,1,0:T(8,128)(2,1)S(1)}, u32[]{:S(2)}, u32[]{:S(2)}) collective-permute-start(bf16[1,112,896]{2,1,0:T(8,128)(2,1)S(1)} %collective-permute-done.31.refs_6_), channel_id=1, source_target_pairs={{0,1},{1,0},{2,3},{3,2},{4,5},{5,4},{6,7},{7,6},{8,9},{9,8},{10,11... | collective-permute-start | bytes 602120 | tf_op jit(solution)/shard_map/ppermute | solution.py:19
  95.6 5.6 %collective-permute-start.49 = (bf16[1,112,896]{2,1,0:T(8,128)(2,1)S(1)}, bf16[1,112,896]{2,1,0:T(8,128)(2,1)S(1)}, u32[]{:S(2)}, u32[]{:S(2)}) collective-permute-start(bf16[1,112,896]{2,1,0:T(8,128)(2,1)S(1)} %collective-permute-done.41.refs_16_), channel_id=1, source_target_pairs={{0,16},{24,8},{1,17},{25,9},{2,18},{26,10},{3,19},{27,11},{4,20},{... | collective-permute-start | bytes 602120 | tf_op jit(solution)/shard_map/ppermute | solution.py:29
  97.9 6.5 %collective-permute-start.43 = (bf16[1,112,896]{2,1,0:T(8,128)(2,1)S(1)}, bf16[1,112,896]{2,1,0:T(8,128)(2,1)S(1)}, u32[]{:S(2)}, u32[]{:S(2)}) collective-permute-start(bf16[1,112,896]{2,1,0:T(8,128)(2,1)S(1)} %collective-permute-done.41.refs_16_), channel_id=1, source_target_pairs={{0,2},{1,3},{2,0},{3,1},{4,6},{5,7},{6,4},{7,5},{8,10},{9,11},{10,... | collective-permute-start | bytes 602120 | tf_op jit(solution)/shard_map/ppermute | solution.py:19
  98.0 6.4 %collective-permute-start.46 = (bf16[1,112,896]{2,1,0:T(8,128)(2,1)S(1)}, bf16[1,112,896]{2,1,0:T(8,128)(2,1)S(1)}, u32[]{:S(2)}, u32[]{:S(2)}) collective-permute-start(bf16[1,112,896]{2,1,0:T(8,128)(2,1)S(1)} %collective-permute-done.45.refs_20_), channel_id=1, source_target_pairs={{0,1},{1,0},{2,3},{3,2},{4,5},{5,4},{6,7},{7,6},{8,9},{9,8},{10,11... | collective-permute-start | bytes 602120 | tf_op jit(solution)/shard_map/ppermute | solution.py:19
  98.9 5.6 %collective-permute-start.42 = (bf16[1,112,896]{2,1,0:T(8,128)(2,1)S(1)}, bf16[1,112,896]{2,1,0:T(8,128)(2,1)S(1)}, u32[]{:S(2)}, u32[]{:S(2)}) collective-permute-start(bf16[1,112,896]{2,1,0:T(8,128)(2,1)S(1)} %collective-permute-done.41.refs_16_), channel_id=1, source_target_pairs={{0,1},{1,0},{2,3},{3,2},{4,5},{5,4},{6,7},{7,6},{8,9},{9,8},{10,11... | collective-permute-start | bytes 602120 | tf_op jit(solution)/shard_map/ppermute | solution.py:19
  98.9 6.1 %collective-permute-start.36 = (bf16[1,112,896]{2,1,0:T(8,128)(2,1)S(1)}, bf16[1,112,896]{2,1,0:T(8,128)(2,1)S(1)}, u32[]{:S(2)}, u32[]{:S(2)}) collective-permute-start(bf16[1,112,896]{2,1,0:T(8,128)(2,1)S(1)} %collective-permute-done.35.refs_10_), channel_id=1, source_target_pairs={{0,1},{1,0},{2,3},{3,2},{4,5},{5,4},{6,7},{7,6},{8,9},{9,8},{10,11... | collective-permute-start | bytes 602120 | tf_op jit(solution)/shard_map/ppermute | solution.py:19
  104.4 5.7 %collective-permute-start.51 = (bf16[1,112,896]{2,1,0:T(8,128)(2,1)S(1)}, bf16[1,112,896]{2,1,0:T(8,128)(2,1)S(1)}, u32[]{:S(2)}, u32[]{:S(2)}) collective-permute-start(bf16[1,112,896]{2,1,0:T(8,128)(2,1)S(1)} %collective-permute-done.49.refs_24_), channel_id=1, source_target_pairs={{0,2},{1,3},{2,0},{3,1},{4,6},{5,7},{6,4},{7,5},{8,10},{9,11},{10,... | collective-permute-start | bytes 602120 | tf_op jit(solution)/shard_map/ppermute | solution.py:19
  104.4 5.7 %collective-permute-start.40 = (bf16[1,112,896]{2,1,0:T(8,128)(2,1)S(1)}, bf16[1,112,896]{2,1,0:T(8,128)(2,1)S(1)}, u32[]{:S(2)}, u32[]{:S(2)}) collective-permute-start(bf16[1,112,896]{2,1,0:T(8,128)(2,1)S(1)} %collective-permute-done.39.refs_14_), channel_id=1, source_target_pairs={{0,1},{1,0},{2,3},{3,2},{4,5},{5,4},{6,7},{7,6},{8,9},{9,8},{10,11... | collective-permute-start | bytes 602120 | tf_op jit(solution)/shard_map/ppermute | solution.py:19
  104.4 5.7 %collective-permute-start.44 = (bf16[1,112,896]{2,1,0:T(8,128)(2,1)S(1)}, bf16[1,112,896]{2,1,0:T(8,128)(2,1)S(1)}, u32[]{:S(2)}, u32[]{:S(2)}) collective-permute-start(bf16[1,112,896]{2,1,0:T(8,128)(2,1)S(1)} %collective-permute-done.43.refs_18_), channel_id=1, source_target_pairs={{0,1},{1,0},{2,3},{3,2},{4,5},{5,4},{6,7},{7,6},{8,9},{9,8},{10,11... | collective-permute-start | bytes 602120 | tf_op jit(solution)/shard_map/ppermute | solution.py:19
  104.9 5.2 %collective-permute-start.50 = (bf16[1,112,896]{2,1,0:T(8,128)(2,1)S(1)}, bf16[1,112,896]{2,1,0:T(8,128)(2,1)S(1)}, u32[]{:S(2)}, u32[]{:S(2)}) collective-permute-start(bf16[1,112,896]{2,1,0:T(8,128)(2,1)S(1)} %collective-permute-done.49.refs_24_), channel_id=1, source_target_pairs={{0,1},{1,0},{2,3},{3,2},{4,5},{5,4},{6,7},{7,6},{8,9},{9,8},{10,11... | collective-permute-start | bytes 602120 | tf_op jit(solution)/shard_map/ppermute | solution.py:19
  105.0 5.1 %collective-permute-start.48 = (bf16[1,112,896]{2,1,0:T(8,128)(2,1)S(1)}, bf16[1,112,896]{2,1,0:T(8,128)(2,1)S(1)}, u32[]{:S(2)}, u32[]{:S(2)}) collective-permute-start(bf16[1,112,896]{2,1,0:T(8,128)(2,1)S(1)} %collective-permute-done.47.refs_22_), channel_id=1, source_target_pairs={{0,1},{1,0},{2,3},{3,2},{4,5},{5,4},{6,7},{7,6},{8,9},{9,8},{10,11... | collective-permute-start | bytes 602120 | tf_op jit(solution)/shard_map/ppermute | solution.py:19
  121.4 16.2 %collective-permute-start.53 = (bf16[112,896]{1,0:T(8,128)(2,1)S(1)}, bf16[112,896]{1,0:T(8,128)(2,1)S(1)}, u32[]{:S(2)}, u32[]{:S(2)}) collective-permute-start(bf16[112,896]{1,0:T(8,128)(2,1)S(1)} %get-tuple-element.42), channel_id=1, source_target_pairs={{0,4},{1,5},{2,6},{3,7},{4,0},{5,1},{6,2},{7,3},{8,12},{9,13},{10,... | collective-permute-start | bytes 602120 | tf_op jit(solution)/shard_map/ppermute | solution.py:19
  121.5 16.1 %collective-permute-start.54 = (bf16[112,896]{1,0:T(8,128)(2,1)S(1)}, bf16[112,896]{1,0:T(8,128)(2,1)S(1)}, u32[]{:S(2)}, u32[]{:S(2)}) collective-permute-start(bf16[112,896]{1,0:T(8,128)(2,1)S(1)} %get-tuple-element.43), channel_id=1, source_target_pairs={{0,6},{1,7},{2,4},{3,5},{4,2},{5,3},{6,0},{7,1},{8,14},{9,15},{10,... | collective-permute-start | bytes 602120 | tf_op jit(solution)/shard_map/ppermute | solution.py:19
  123.8 15.0 %collective-permute-start.55 = (bf16[112,896]{1,0:T(8,128)(2,1)S(1)}, bf16[112,896]{1,0:T(8,128)(2,1)S(1)}, u32[]{:S(2)}, u32[]{:S(2)}) collective-permute-start(bf16[112,896]{1,0:T(8,128)(2,1)S(1)} %get-tuple-element.44), channel_id=1, source_target_pairs={{0,2},{1,3},{2,0},{3,1},{4,6},{5,7},{6,4},{7,5},{8,10},{9,11},{10,... | collective-permute-start | bytes 602120 | tf_op jit(solution)/shard_map/ppermute | solution.py:19
  (12 other events, 103.6 us)
